TPU v7x, 32 devices: a whole 2x2x4 slice. The times are simulated.
32 devices in a mesh: dp: 8 (over z, y), mp: 4 (over x, core).
Axes of the slice: x: 2, y: 2, z: 4, core: 2. Of those that a mesh axis runs over, the one named last changes fastest.
Arguments:
- tokens: bfloat16 [8192, 2048], P('dp'), may hold values from -6 to 6
- documents: int32 [8, 1024], P('dp'), may hold values from 0 to 3, never falling along the last dimension, each value on 1 to 512 neighbouring positions
- cotangent: bfloat16 [8192, 2048], P('dp'), may hold values from -6 to 6
- attn_gain: float32 [2048], P('dp'), may hold values from 0.5 to 1.5
- query_gain: float32 [128], P('dp'), may hold values from 1 to 2
- key_norm_scale: float32 [128], P('dp'), may hold values from 0.25 to 1.75
- query_weight: float32 [2048, 2048], P('dp', 'mp'), may hold values from -0.125 to 0.125
- key_projection: float32 [2048, 1024], P('dp', 'mp'), may hold values from -0.125 to 0.125
- value_projection: float32 [2048, 1024], P('dp', 'mp'), may hold values from -0.125 to 0.125
- output_weight: float32 [2048, 2048], P('mp', 'dp'), may hold values from -1 to 1
- mlp_gain: float32 [2048], P('dp'), may hold values from 0.5 to 1.5
- gate_weight: float32 [2048, 6144], P('dp', 'mp'), may hold values from -0.125 to 0.125
- up_weight: float32 [2048, 6144], P('dp', 'mp'), may hold values from -0.125 to 0.125
- down_weight: float32 [6144, 2048], P('mp', 'dp'), may hold values from -0.078125 to 0.078125
Outputs:
- layer_output: bfloat16 [8192, 2048], P(('dp', 'mp'))
- input_grad: float32 [8192, 2048], P(('dp', 'mp'))
- attn_gain_grad: float32 [2048], P('dp')
- query_gain_grad: float32 [128], P('dp')
- key_gain_grad: float32 [128], P('dp')
- query_weight_grad: float32 [2048, 2048], P('dp', 'mp')
- key_weight_grad: float32 [2048, 1024], P('dp', 'mp')
- value_weight_grad: float32 [2048, 1024], P('dp', 'mp')
- output_weight_grad: float32 [2048, 2048], P('mp', 'dp')
- mlp_gain_grad: float32 [2048], P('dp')
- gate_weight_grad: float32 [2048, 6144], P('dp', 'mp')
- up_weight_grad: float32 [2048, 6144], P('dp', 'mp')
- down_weight_grad: float32 [6144, 2048], P('mp', 'dp')
Inputs may be any that keep to these rules, and one draw needn't show every extreme that they name: `documents`: document numbers never fall along a sequence; each document holds 1 to 512 positions, and some document holds exactly 512.
All inputs are finite; a program needn't handle non-finite values.
Results may differ from a plain program's by a relative error of at most 0.023.
Values may be sent and summed in bfloat16 or wider, within the bound.
A program may use at most 256 MiB of HBM per device.

v0:
```python
import jax
import jax.numpy as jnp
from jax import lax
from jax.sharding import PartitionSpec as P

QUERY_HEADS = 16
KEY_VALUE_HEADS = 8
HEAD_WIDTH = 128


EPSILON = 1e-06
MASKED = -1e30


def doc_positions(documents):
    indices = jnp.arange(documents.shape[-1], dtype=jnp.int32)
    boundary = jnp.concatenate(
        [
            jnp.ones(documents.shape[:-1] + (1,), dtype=jnp.bool_),
            documents[:, 1:] != documents[:, :-1],
        ],
        -1,
    )
    starts = lax.cummax(jnp.where(boundary, indices[None, :], 0), axis=1)
    return indices[None, :] - starts


def rope_tables(positions, head_size):
    middle = head_size // 2
    frequency = jnp.power(1000000.0, -2.0 * jnp.arange(middle, dtype=jnp.float32) / head_size)
    angles = positions.astype(jnp.float32)[:, None] * frequency[None, :]
    cosine_table = jnp.cos(angles)
    sine_table = jnp.sin(angles)
    return (
        jnp.concatenate([cosine_table, cosine_table], -1),
        jnp.concatenate([sine_table, sine_table], -1),
    )


def rotate(values):
    middle = values.shape[-1] // 2
    return jnp.concatenate([-values[..., middle:], values[..., :middle]], -1)


def rotate_back(values):
    middle = values.shape[-1] // 2
    return jnp.concatenate([values[..., middle:], -values[..., :middle]], -1)


def norm_parts(values):
    scaling = lax.rsqrt(jnp.mean(values * values, -1, keepdims=True) + EPSILON)
    return (values * scaling, scaling)


def norm_back(grad_normed, normed_hat, scaling, gains):
    scaled = grad_normed * gains
    return scaling * (scaled - normed_hat * jnp.mean(scaled * normed_hat, -1, keepdims=True))


def contract_rows(left, right):
    return lax.dot_general(
        left, right, (((0,), (0,)), ((), ())), preferred_element_type=jnp.float32
    )


def contract_cols(left, right):
    return lax.dot_general(
        left, right, (((1,), (1,)), ((), ())), preferred_element_type=jnp.float32
    )


def block_scores(query_rows, key_token_rows, doc_row, start, width, factor):
    scores = (
        jnp.einsum("qgrd,kgd->grqk", query_rows, key_token_rows, preferred_element_type=jnp.float32)
        * factor
    )
    query_index = start + jnp.arange(width)
    key_index = jnp.arange(key_token_rows.shape[0])
    allowed = (doc_row[start : start + width, None] == doc_row[None, :]) & (
        key_index[None, :] <= query_index[:, None]
    )
    return jnp.where(allowed, scores, MASKED)


def on_device(
    tokens,
    documents,
    cotangent,
    attn_gain,
    query_gain,
    key_norm_scale,
    query_weight,
    key_projection,
    value_projection,
    output_weight,
    mlp_gain,
    gate_weight,
    up_weight,
    down_weight,
):
    rows = tokens.shape[0]
    seqs, seq_length = documents.shape
    head_size = HEAD_WIDTH
    local_heads = QUERY_HEADS // lax.axis_size("mp")
    device_groups = KEY_VALUE_HEADS // lax.axis_size("mp")
    query_group = QUERY_HEADS // KEY_VALUE_HEADS
    block = min(512, seq_length)
    factor = head_size ** (-0.5)
    share = rows // lax.axis_size("mp")
    offset = lax.axis_index("mp") * share

    def take(values):
        return lax.dynamic_slice_in_dim(values, offset, share, 0)

    attn_parts = (
        lax.all_gather(attn_gain.astype(jnp.bfloat16), "dp", axis=0, tiled=True),
        lax.all_gather(query_gain.astype(jnp.bfloat16), "dp", axis=0, tiled=True),
        lax.all_gather(key_norm_scale.astype(jnp.bfloat16), "dp", axis=0, tiled=True),
        lax.all_gather(query_weight.astype(jnp.bfloat16), "dp", axis=0, tiled=True),
        lax.all_gather(key_projection.astype(jnp.bfloat16), "dp", axis=0, tiled=True),
        lax.all_gather(value_projection.astype(jnp.bfloat16), "dp", axis=0, tiled=True),
        lax.all_gather(output_weight.astype(jnp.bfloat16), "dp", axis=1, tiled=True),
    )
    gain_one = attn_parts[0].astype(jnp.float32)
    gain_query = attn_parts[1].astype(jnp.float32)
    gain_key = attn_parts[2].astype(jnp.float32)
    query_mat, key_mat, value_mat, output_mat = (
        attn_parts[3],
        attn_parts[4],
        attn_parts[5],
        attn_parts[6],
    )
    mlp_parts = (
        lax.all_gather(mlp_gain.astype(jnp.bfloat16), "dp", axis=0, tiled=True),
        lax.all_gather(gate_weight.astype(jnp.bfloat16), "dp", axis=0, tiled=True),
        lax.all_gather(up_weight.astype(jnp.bfloat16), "dp", axis=0, tiled=True),
        lax.all_gather(down_weight.astype(jnp.bfloat16), "dp", axis=1, tiled=True),
    )
    gain_two = mlp_parts[0].astype(jnp.float32)
    gate_mat, up_mat, down_mat = (mlp_parts[1], mlp_parts[2], mlp_parts[3])
    inputs = tokens.astype(jnp.float32)
    hat_one, inv_one = norm_parts(inputs)
    normed_one = (hat_one * gain_one).astype(jnp.bfloat16)
    query_raw = jnp.dot(normed_one, query_mat, preferred_element_type=jnp.float32)
    key_unnormed = jnp.dot(normed_one, key_mat, preferred_element_type=jnp.float32)
    value_token_rows = jnp.dot(normed_one, value_mat, preferred_element_type=jnp.float32).astype(
        jnp.bfloat16
    )
    positions = doc_positions(documents).reshape(rows)
    cosine_table, sine_table = rope_tables(positions, head_size)
    cosine_table = cosine_table[:, None, :]
    sine_table = sine_table[:, None, :]
    query_hat, query_inv = norm_parts(query_raw.reshape(rows, local_heads, head_size))
    key_hat, key_inv = norm_parts(key_unnormed.reshape(rows, device_groups, head_size))
    query_normed = query_hat * gain_query
    key_normed = key_hat * gain_key
    query_rows = (query_normed * cosine_table + rotate(query_normed) * sine_table).astype(
        jnp.bfloat16
    )
    key_token_rows = (key_normed * cosine_table + rotate(key_normed) * sine_table).astype(
        jnp.bfloat16
    )
    query_seq = query_rows.reshape(seqs, seq_length, device_groups, query_group, head_size)
    key_seq = key_token_rows.reshape(seqs, seq_length, device_groups, head_size)
    value_seq = value_token_rows.reshape(seqs, seq_length, device_groups, head_size)

    def attend_forward(items):
        seq_queries, seq_keys, seq_values, doc_row = items
        outputs = []
        log_totals = []
        for start in range(0, seq_length, block):
            scores = block_scores(
                seq_queries[start : start + block], seq_keys, doc_row, start, block, factor
            )
            highest = jnp.max(scores, -1, keepdims=True)
            exponent = jnp.exp(scores - highest)
            totals = jnp.sum(exponent, -1, keepdims=True)
            weights_block = (exponent / totals).astype(jnp.bfloat16)
            outputs.append(
                jnp.einsum(
                    "grqk,kgd->qgrd", weights_block, seq_values, preferred_element_type=jnp.float32
                )
            )
            log_totals.append(highest + jnp.log(totals))
        return (jnp.concatenate(outputs, 0), jnp.concatenate(log_totals, 2))

    attention_output, log_total = lax.map(
        attend_forward, (query_seq, key_seq, value_seq, documents)
    )
    attended_flat = attention_output.reshape(rows, local_heads * head_size).astype(jnp.bfloat16)
    attn_part = jnp.dot(attended_flat, output_mat, preferred_element_type=jnp.float32)
    hidden = inputs + lax.psum(attn_part, "mp")
    hat_two, inv_two = norm_parts(hidden)
    normed_two = (hat_two * gain_two).astype(jnp.bfloat16)
    hidden_share = take(hidden)
    gate_pre = jnp.dot(normed_two, gate_mat, preferred_element_type=jnp.float32)
    up_pre = jnp.dot(normed_two, up_mat, preferred_element_type=jnp.float32)
    sigmoid = jax.nn.sigmoid(gate_pre)
    swish = gate_pre * sigmoid
    active = (swish * up_pre).astype(jnp.bfloat16)
    mlp_part = jnp.dot(active, down_mat, preferred_element_type=jnp.float32)
    layer_output = (
        hidden_share + take(lax.psum(mlp_part.astype(jnp.bfloat16), "mp").astype(jnp.float32))
    ).astype(jnp.bfloat16)
    back_gain_one, back_gain_query, back_gain_key = (gain_one, gain_query, gain_key)
    back_query, back_key, back_value, back_output = (query_mat, key_mat, value_mat, output_mat)
    back_gate, back_up, back_down = (gate_mat, up_mat, down_mat)
    grad_out = cotangent.astype(jnp.float32)
    grad_active = contract_cols(cotangent, back_down)
    down_grad = contract_rows(active, cotangent)
    grad_gate = (grad_active * up_pre * sigmoid * (1.0 + gate_pre * (1.0 - sigmoid))).astype(
        jnp.bfloat16
    )
    grad_up = (grad_active * swish).astype(jnp.bfloat16)
    gate_grad = contract_rows(normed_two, grad_gate)
    up_grad = contract_rows(normed_two, grad_up)
    normed_two_part = contract_cols(grad_gate, back_gate) + contract_cols(grad_up, back_up)
    normed_two_grad = lax.psum(normed_two_part.astype(jnp.bfloat16), "mp").astype(jnp.float32)
    mlp_gain_part = jnp.sum(normed_two_grad * hat_two, 0)
    grad_hidden = grad_out + norm_back(normed_two_grad, hat_two, inv_two, gain_two)
    grad_hidden_low = grad_hidden.astype(jnp.bfloat16)
    grad_hidden_share = take(grad_hidden)
    output_grad = contract_rows(attended_flat, grad_hidden_low)
    grad_attended = contract_cols(grad_hidden_low, back_output).astype(jnp.bfloat16)
    grad_attended_seq = grad_attended.reshape(
        seqs, seq_length, device_groups, query_group, head_size
    )

    def attend_backward(items):
        seq_queries, seq_keys, seq_values, doc_row, seq_log_total, seq_grad = items
        query_grads = []
        key_grad = jnp.zeros((seq_length, device_groups, head_size), jnp.float32)
        value_grad = jnp.zeros((seq_length, device_groups, head_size), jnp.float32)
        for start in range(0, seq_length, block):
            block_queries = seq_queries[start : start + block]
            block_grad = seq_grad[start : start + block]
            scores = block_scores(block_queries, seq_keys, doc_row, start, block, factor)
            weights_block = jnp.exp(scores - seq_log_total[:, :, start : start + block])
            grad_weights = jnp.einsum(
                "qgrd,kgd->grqk", block_grad, seq_values, preferred_element_type=jnp.float32
            )
            inner = jnp.sum(weights_block * grad_weights, -1, keepdims=True)
            grad_scores = (weights_block * (grad_weights - inner)).astype(jnp.bfloat16)
            query_grads.append(
                jnp.einsum(
                    "grqk,kgd->qgrd", grad_scores, seq_keys, preferred_element_type=jnp.float32
                )
                * factor
            )
            key_grad = (
                key_grad
                + jnp.einsum(
                    "grqk,qgrd->kgd", grad_scores, block_queries, preferred_element_type=jnp.float32
                )
                * factor
            )
            value_grad = value_grad + jnp.einsum(
                "grqk,qgrd->kgd",
                weights_block.astype(jnp.bfloat16),
                block_grad,
                preferred_element_type=jnp.float32,
            )
        return (jnp.concatenate(query_grads, 0), key_grad, value_grad)

    query_rot_grad, key_rot_grad, value_seq_grad = lax.map(
        attend_backward, (query_seq, key_seq, value_seq, documents, log_total, grad_attended_seq)
    )
    query_rot_grad = query_rot_grad.reshape(rows, local_heads, head_size)
    key_rot_grad = key_rot_grad.reshape(rows, device_groups, head_size)
    query_norm_grad = query_rot_grad * cosine_table + rotate_back(query_rot_grad * sine_table)
    key_norm_grad = key_rot_grad * cosine_table + rotate_back(key_rot_grad * sine_table)
    query_gain_part = jnp.sum(query_norm_grad * query_hat, (0, 1))
    key_gain_part = jnp.sum(key_norm_grad * key_hat, (0, 1))
    query_raw_grad = (
        norm_back(query_norm_grad, query_hat, query_inv, back_gain_query)
        .reshape(rows, local_heads * head_size)
        .astype(jnp.bfloat16)
    )
    key_raw_grad = (
        norm_back(key_norm_grad, key_hat, key_inv, back_gain_key)
        .reshape(rows, device_groups * head_size)
        .astype(jnp.bfloat16)
    )
    value_raw_grad = value_seq_grad.reshape(rows, device_groups * head_size).astype(jnp.bfloat16)
    query_grad = contract_rows(normed_one, query_raw_grad)
    key_grad = contract_rows(normed_one, key_raw_grad)
    value_grad = contract_rows(normed_one, value_raw_grad)
    normed_one_part = (
        contract_cols(query_raw_grad, back_query)
        + contract_cols(key_raw_grad, back_key)
        + contract_cols(value_raw_grad, back_value)
    )
    hat_one_share = take(hat_one)
    inv_one_share = take(inv_one)
    normed_one_grad, query_gain_sum, key_gain_sum = (
        lax.psum(normed_one_part.astype(jnp.bfloat16), "mp").astype(jnp.float32),
        lax.psum(query_gain_part.astype(jnp.bfloat16), "mp").astype(jnp.float32),
        lax.psum(key_gain_part.astype(jnp.bfloat16), "mp").astype(jnp.float32),
    )
    attn_gain_total = jnp.sum(normed_one_grad * hat_one, 0)
    input_grad = grad_hidden_share + norm_back(
        take(normed_one_grad), hat_one_share, inv_one_share, back_gain_one
    )
    attn_grads = (
        lax.psum_scatter(
            attn_gain_total.astype(jnp.bfloat16), "dp", scatter_dimension=0, tiled=True
        ).astype(jnp.float32),
        lax.psum_scatter(
            query_gain_sum.astype(jnp.bfloat16), "dp", scatter_dimension=0, tiled=True
        ).astype(jnp.float32),
        lax.psum_scatter(
            key_gain_sum.astype(jnp.bfloat16), "dp", scatter_dimension=0, tiled=True
        ).astype(jnp.float32),
        lax.psum_scatter(
            query_grad.astype(jnp.bfloat16), "dp", scatter_dimension=0, tiled=True
        ).astype(jnp.float32),
        lax.psum_scatter(
            key_grad.astype(jnp.bfloat16), "dp", scatter_dimension=0, tiled=True
        ).astype(jnp.float32),
        lax.psum_scatter(
            value_grad.astype(jnp.bfloat16), "dp", scatter_dimension=0, tiled=True
        ).astype(jnp.float32),
        lax.psum_scatter(
            output_grad.astype(jnp.bfloat16), "dp", scatter_dimension=1, tiled=True
        ).astype(jnp.float32),
    )
    mlp_grads = (
        lax.psum_scatter(
            mlp_gain_part.astype(jnp.bfloat16), "dp", scatter_dimension=0, tiled=True
        ).astype(jnp.float32),
        lax.psum_scatter(
            gate_grad.astype(jnp.bfloat16), "dp", scatter_dimension=0, tiled=True
        ).astype(jnp.float32),
        lax.psum_scatter(
            up_grad.astype(jnp.bfloat16), "dp", scatter_dimension=0, tiled=True
        ).astype(jnp.float32),
        lax.psum_scatter(
            down_grad.astype(jnp.bfloat16), "dp", scatter_dimension=1, tiled=True
        ).astype(jnp.float32),
    )
    return (
        layer_output,
        input_grad,
        attn_grads[0],
        attn_grads[1],
        attn_grads[2],
        attn_grads[3],
        attn_grads[4],
        attn_grads[5],
        attn_grads[6],
        mlp_grads[0],
        mlp_grads[1],
        mlp_grads[2],
        mlp_grads[3],
    )


def solution(mesh):
    in_specs = (
        P("dp", None),
        P("dp", None),
        P("dp", None),
        P("dp"),
        P("dp"),
        P("dp"),
        P("dp", "mp"),
        P("dp", "mp"),
        P("dp", "mp"),
        P("mp", "dp"),
        P("dp"),
        P("dp", "mp"),
        P("dp", "mp"),
        P("mp", "dp"),
    )
    out_specs = (
        P(("dp", "mp"), None),
        P(("dp", "mp"), None),
        P("dp"),
        P("dp"),
        P("dp"),
        P("dp", "mp"),
        P("dp", "mp"),
        P("dp", "mp"),
        P("mp", "dp"),
        P("dp"),
        P("dp", "mp"),
        P("dp", "mp"),
        P("mp", "dp"),
    )
    return jax.shard_map(
        on_device, mesh=mesh, in_specs=in_specs, out_specs=out_specs, check_vma=False
    )
```

profile of v0, /device:TPU:0, one launch (start us, length us, event | category | flops | bytes accessed | tf_op | source)
XLA Modules:
  0.0 1635.1 jit_solution(17745862805396485269)
XLA Ops:
  16.6 22.3 %all-gather = bf16[8,1,256]{2,1,0:T(2,128)(2,1)S(1)} all-gather(bf16[1,1,256]{2,1,0:T(2,128)(2,1)S(1)} %reshape.304), channel_id=1, replica_groups=mesh['dp'=8,'mp'=4] {'dp'}, dimensions={0}, use_global_device_ids=true | all-gather | bytes 4608 | tf_op jit(solution)/shard_map/all_gather | solution.py:116
  38.9 3.1 fusion.6
  43.8 17.2 %all-reduce.7 = (bf16[128]{0:T(256)(128)(2,1)S(1)}, bf16[128]{0:T(256)(128)(2,1)S(1)}) all-reduce(bf16[128]{0:T(256)(128)(2,1)S(1)} %dynamic-update-slice, bf16[128]{0:T(256)(128)(2,1)S(1)} %dynamic-update-slice.1), channel_id=1, replica_groups=mesh['dp'=8,'mp'=4] {'dp'}, use_global_device_ids=true, to_apply=%add | all-reduce | flops 256 | bytes 1024
  63.7 4.0 multiply_reduce_fusion.7
  69.1 26.4 %all-gather.10.cloned.1.call-done = bf16[2048,256]{1,0:T(8,128)(2,1)} async-done(((bf16[256,256]{1,0:T(8,128)(2,1)}), bf16[2048,256]{1,0:T(8,128)(2,1)}) %all-gather.10.cloned.1.call-update) | async-done | bytes 1048592 | tf_op jit(solution)/shard_map/all_gather | solution.py:121
  95.5 4.0 convolution_convert_fusion.8
  99.5 46.8 %all-gather.14.cloned.1.call-done = bf16[2048,512]{1,0:T(8,128)(2,1)} async-done(((bf16[256,512]{1,0:T(8,128)(2,1)}), bf16[2048,512]{1,0:T(8,128)(2,1)}) %all-gather.14.cloned.1.call-update) | async-done | bytes 2097168 | tf_op jit(solution)/shard_map/all_gather | solution.py:119
  146.3 5.4 multiply_reduce_fusion.4
  164.0 34.4 %all-gather.16.cloned.1.call-done = bf16[512,2048]{1,0:T(8,128)(2,1)} async-done(((bf16[512,256]{1,0:T(8,128)(2,1)}), bf16[512,2048]{1,0:T(8,128)(2,1)}) %all-gather.16.cloned.1.call-update) | async-done | bytes 2097168 | tf_op jit(solution)/shard_map/all_gather | solution.py:122
  198.4 7.2 fusion.77
  208.1 2.8 convert_element_type.248
  212.0 17.4 %all-gather.1 = bf16[8,1,256]{2,1,0:T(2,128)(2,1)S(1)} all-gather(bf16[1,1,256]{2,1,0:T(2,128)(2,1)S(1)} %reshape.306), channel_id=1, replica_groups=mesh['dp'=8,'mp'=4] {'dp'}, dimensions={0}, use_global_device_ids=true | all-gather | bytes 4608 | tf_op jit(solution)/shard_map/all_gather | solution.py:134
  230.0 126.9 %all-reduce.14.cloned.1.call-done = f32[1024,2048]{1,0:T(8,128)} async-done(((f32[1024,2048]{1,0:T(8,128)}), f32[1024,2048]{1,0:T(8,128)}) %all-reduce.14.cloned.1.call-update) | async-done | bytes 8388624 | tf_op jit(solution)/shard_map/psum | solution.py:192
  356.8 5.7 multiply_reduce_fusion.1
  362.6 3.3 copy-done.2
  365.9 2.7 multiply_convert_fusion
  368.6 90.1 %all-gather.18.cloned.1.call-done = bf16[2048,1536]{1,0:T(8,128)(2,1)} async-done(((bf16[256,1536]{1,0:T(8,128)(2,1)}), bf16[2048,1536]{1,0:T(8,128)(2,1)}) %all-gather.18.cloned.1.call-update) | async-done | bytes 6291472 | tf_op jit(solution)/shard_map/all_gather | solution.py:135
  458.7 11.9 fusion.78
  470.6 88.1 %all-gather.20.cloned.1.call-done = bf16[2048,1536]{1,0:T(8,128)(2,1)} async-done(((bf16[256,1536]{1,0:T(8,128)(2,1)}), bf16[2048,1536]{1,0:T(8,128)(2,1)}) %all-gather.20.cloned.1.call-update) | async-done | bytes 6291472 | tf_op jit(solution)/shard_map/all_gather | solution.py:136
  558.7 11.7 fusion.79
  570.4 89.1 %all-gather.22.cloned.1.call-done = bf16[1536,2048]{1,0:T(8,128)(2,1)} async-done(((bf16[1536,256]{1,0:T(8,128)(2,1)}), bf16[1536,2048]{1,0:T(8,128)(2,1)}) %all-gather.22.cloned.1.call-update) | async-done | bytes 6291472 | tf_op jit(solution)/shard_map/all_gather | solution.py:137
  659.4 16.4 %multiply_convert_fusion.2 = (bf16[1024,1536]{1,0:T(8,128)(2,1)}, bf16[1024,1536]{1,0:T(8,128)(2,1)S(1)}, bf16[1024,1536]{1,0:T(8,128)(2,1)}) fusion(f32[1024,1536]{1,0:T(8,128)} %fusion.78, f32[1024,1536]{1,0:T(8,128)} %fusion.79, bf16[1024,2048]{1,0:T(8,128)(2,1)} %param.16, bf16[1536,2048]{1,0:T(8,128)(2,1)} %all-gather.22.cloned.1.call-done), kind=kOutput, calls=%fused_computation.43 | convolution fusion | flops 6466043904 | bytes 32505856 | tf_op jit(solution)/shard_map/dot_general | solution.py:67
  675.8 10.0 fusion.80
  685.8 10.2 add_convert_fusion.1
  696.2 11.3 convolution_convert_fusion.3
  707.5 72.4 %all-reduce.16.cloned.1.call-done = bf16[1024,2048]{1,0:T(8,128)(2,1)} async-done(((bf16[1024,2048]{1,0:T(8,128)(2,1)}), bf16[1024,2048]{1,0:T(8,128)(2,1)}) %all-reduce.16.cloned.1.call-update) | async-done | bytes 4194320 | tf_op jit(solution)/shard_map/psum | solution.py:218
  779.9 6.0 fusion.5
  787.0 5.0 fusion.4
  792.0 2.4 fusion.40
  795.5 2.5 fusion.43
  798.0 1.8 fusion.10
  800.2 5.0 fusion.7
  805.2 5.1 fusion.9
  810.3 2.5 convolution_bitcast_fusion
  814.0 2.4 fusion.55
  816.4 2.4 fusion.12
  826.5 2.1 pad_maximum_fusion.2
  828.8 4.9 convolution_convert_fusion.6
  833.9 5.1 fusion.33
  841.0 2.4 fusion.81
  843.4 3.3 add_convert_fusion
  846.8 4.9 convolution_convert_fusion.7
  851.8 6.5 convolution_convert_fusion.5
  858.6 7.1 convolution_convert_fusion.4
  865.8 11.5 convolution_convert_fusion.2
  877.3 1.8 copy-done.54
  879.2 11.0 convolution_convert_fusion.1
  892.1 10.9 convolution_convert_fusion
  906.1 146.2 %all-reduce.18.cloned.1.call-done = (bf16[1024,2048]{1,0:T(8,128)(2,1)}, bf16[1024,2048]{1,0:T(8,128)(2,1)}) async-done(((bf16[1024,2048]{1,0:T(8,128)(2,1)}, bf16[1024,2048]{1,0:T(8,128)(2,1)}), (bf16[1024,2048]{1,0:T(8,128)(2,1)}, bf16[1024,2048]{1,0:T(8,128)(2,1)})) %all-reduce.18.cloned.1.call-update) | async-done | bytes 8388624 | tf_op jit(solution)/shard_map/psum | solution.py:203
  1052.2 6.5 multiply_reduce_fusion
  1058.8 22.0 %all-reduce.6 = (bf16[2048]{0:T(1024)(128)(2,1)S(1)}, bf16[128]{0:T(256)(128)(2,1)S(1)}, bf16[128]{0:T(256)(128)(2,1)S(1)}, bf16[2048]{0:T(1024)(128)(2,1)S(1)}) all-reduce(bf16[2048]{0:T(1024)(128)(2,1)S(1)} %get-tuple-element.84, bf16[128]{0:T(256)(128)(2,1)S(1)} %reduce_sum.170, ...), channel_id=2, replica_groups=mesh['dp'=8,'mp'=4] {'dp'}, use_global_device_ids=true, to_apply=%region_21.22.clone | all-reduce | flops 4352 | bytes 17408
  1081.0 38.8 %reduce-scatter.10.cloned.1.call-done = bf16[256,256]{1,0:T(8,128)(2,1)} async-done(((bf16[2048,256]{1,0:T(8,128)(2,1)}), bf16[256,256]{1,0:T(8,128)(2,1)}) %reduce-scatter.10.cloned.1.call-update) | async-done | bytes 131088 | tf_op jit(solution)/shard_map/reduce_scatter | solution.py:317
  1121.4 5.6 all-reduce.8
  1127.0 6.7 convert_element_type.272
  1134.7 56.6 %reduce-scatter.8.cloned.1.call-done = bf16[256,512]{1,0:T(8,128)(2,1)} async-done(((bf16[2048,512]{1,0:T(8,128)(2,1)}), bf16[256,512]{1,0:T(8,128)(2,1)}) %reduce-scatter.8.cloned.1.call-update) | async-done | bytes 262160 | tf_op jit(solution)/shard_map/reduce_scatter | solution.py:314
  1193.1 69.3 %reduce-scatter.14.cloned.1.call-done = bf16[512,256]{1,0:T(8,128)(2,1)} async-done(((bf16[512,2048]{1,0:T(8,128)(2,1)}), bf16[512,256]{1,0:T(8,128)(2,1)}) %reduce-scatter.14.cloned.1.call-update) | async-done | bytes 262160 | tf_op jit(solution)/shard_map/reduce_scatter | solution.py:323
  1264.8 2.5 multiply_reduce_fusion.2
  1267.3 6.0 multiply_add_fusion
  1273.3 110.0 %reduce-scatter.16.cloned.1.call-done = bf16[256,1536]{1,0:T(8,128)(2,1)} async-done(((bf16[2048,1536]{1,0:T(8,128)(2,1)}), bf16[256,1536]{1,0:T(8,128)(2,1)}) %reduce-scatter.16.cloned.1.call-update) | async-done | bytes 786448 | tf_op jit(solution)/shard_map/reduce_scatter | solution.py:331
  1383.3 2.5 convert_element_type.290
  1385.7 118.5 %reduce-scatter.18.cloned.1.call-done = bf16[256,1536]{1,0:T(8,128)(2,1)} async-done(((bf16[2048,1536]{1,0:T(8,128)(2,1)}), bf16[256,1536]{1,0:T(8,128)(2,1)}) %reduce-scatter.18.cloned.1.call-update) | async-done | bytes 786448 | tf_op jit(solution)/shard_map/reduce_scatter | solution.py:334
  1504.3 2.5 convert_element_type.292
  1506.7 119.0 %reduce-scatter.20.cloned.1.call-done = bf16[1536,256]{1,0:T(8,128)(2,1)} async-done(((bf16[1536,2048]{1,0:T(8,128)(2,1)}), bf16[1536,256]{1,0:T(8,128)(2,1)}) %reduce-scatter.20.cloned.1.call-update) | async-done | bytes 786448 | tf_op jit(solution)/shard_map/reduce_scatter | solution.py:337
  1625.7 2.4 convert_element_type.294
  (241 shorter events, 55.3 us)
Async XLA Ops:
  7.2 34.9 %copy-start.45 = (u32[32]{0:T(128)S(1)}, u32[32]{0:T(128)}, u32[]{:S(2)}) copy-start(u32[32]{0:T(128)} %constant.106) | copy-start | bytes 388
  7.2 34.8 %copy-start.50 = (f32[16]{0:T(128)S(1)}, f32[16]{0:T(128)}, u32[]{:S(2)}) copy-start(f32[16]{0:T(128)} %param.19) | copy-start | bytes 196
  7.2 34.8 %copy-start.51 = (f32[16]{0:T(128)S(1)}, f32[16]{0:T(128)}, u32[]{:S(2)}) copy-start(f32[16]{0:T(128)} %param.18) | copy-start | bytes 196
  7.2 56.4 %all-gather.12.cloned.1.call-start = ((), (), s32[]{:S(2)}) async-start(), calls=%async_computation.8 | async-start | bytes 1179648 | tf_op jit(solution)/shard_map/all_gather | solution.py:120
  8.9 86.6 %all-gather.10.cloned.1.call-start = ((), (), s32[]{:S(2)}) async-start(), calls=%async_computation.7 | async-start | bytes 1179648 | tf_op jit(solution)/shard_map/all_gather | solution.py:121
  10.6 52.3 %copy-start.39 = (s32[1,1024]{1,0:T(1,128)S(1)}, s32[1,1024]{1,0:T(1,128)}, u32[]{:S(2)}) copy-start(s32[1,1024]{1,0:T(1,128)} %param.15) | copy-start | bytes 12292
  10.6 135.7 %all-gather.14.cloned.1.call-start = ((), (), s32[]{:S(2)}) async-start(), calls=%async_computation.9 | async-start | bytes 2359296 | tf_op jit(solution)/shard_map/all_gather | solution.py:119
  12.5 185.9 %all-gather.16.cloned.1.call-start = ((), (), s32[]{:S(2)}) async-start(), calls=%async_computation.10 | async-start | bytes 2359296 | tf_op jit(solution)/shard_map/all_gather | solution.py:122
  14.3 342.5 %all-reduce.14.cloned.1.call-start = ((), (), s32[]{:S(2)}) async-start(), calls=%async_computation.11 | async-start | bytes 16777216 | tf_op jit(solution)/shard_map/psum | solution.py:192
  38.9 107.4 %copy-start.37 = (f32[8,1,256]{2,1,0:T(1,128)}, f32[8,1,256]{2,1,0:T(1,128)S(1)}, u32[]{:S(2)}) copy-start(f32[8,1,256]{2,1,0:T(1,128)S(1)} %convert_element_type.295) | copy-start | bytes 24580
  42.0 104.3 %copy-start.40 = (f32[1024]{0:T(1024)}, f32[1024]{0:T(1024)S(1)}, u32[]{:S(2)}) copy-start(f32[1024]{0:T(1024)S(1)} %add_rsqrt_fusion.3) | copy-start | bytes 12292
  61.0 7.0 copy-start.43
  62.9 89.5 %copy-start.7 = (f32[1024,128]{0,1:T(8,128)}, f32[1024,128]{0,1:T(8,128)S(1)}, u32[]{:S(2)}) copy-start(f32[1024,128]{0,1:T(8,128)S(1)} %pad_maximum_fusion.4) | copy-start | bytes 1572868
  62.9 89.4 %copy-start.9 = (f32[1024,128]{0,1:T(8,128)}, f32[1024,128]{0,1:T(8,128)S(1)}, u32[]{:S(2)}) copy-start(f32[1024,128]{0,1:T(8,128)S(1)} %pad_maximum_fusion.5) | copy-start | bytes 1572868
  69.1 88.1 %copy-start.16 = (bf16[1024,2,128,1]{0,2,3,1:T(8,128)(2,1)}, bf16[1024,2,128,1]{0,2,3,1:T(8,128)(2,1)S(1)}, u32[]{:S(2)}) copy-start(bf16[1024,2,128,1]{0,2,3,1:T(8,128)(2,1)S(1)} %fusion.64) | copy-start | bytes 1572868
  153.9 1.8 copy-start.18
  153.9 3.3 copy-start.20
  155.6 4.5 copy-start
  158.9 3.2 copy-start.1
  163.9 41.7 %copy-start.33 = (bf16[1024,2,2,128]{0,3,2,1:T(8,128)(2,1)}, bf16[1024,2,2,128]{0,3,2,1:T(8,128)(2,1)S(1)}, u32[]{:S(2)}) copy-start(bf16[1024,2,2,128]{0,3,2,1:T(8,128)(2,1)S(1)} %pad_maximum_fusion.3) | copy-start | bytes 3145732
  205.6 6.3 copy-start.49
  205.6 253.0 %all-gather.18.cloned.1.call-start = ((), (), s32[]{:S(2)}) async-start(), calls=%async_computation.12 | async-start | bytes 7077888 | tf_op jit(solution)/shard_map/all_gather | solution.py:135
  208.0 2.9 copy-start.28
  208.0 350.7 %all-gather.20.cloned.1.call-start = ((), (), s32[]{:S(2)}) async-start(), calls=%async_computation.13 | async-start | bytes 7077888 | tf_op jit(solution)/shard_map/all_gather | solution.py:136
  210.8 448.6 %all-gather.22.cloned.1.call-start = ((), (), s32[]{:S(2)}) async-start(), calls=%async_computation.14 | async-start | bytes 7077888 | tf_op jit(solution)/shard_map/all_gather | solution.py:137
  211.9 568.0 %all-reduce.16.cloned.1.call-start = ((), (), s32[]{:S(2)}) async-start(), calls=%async_computation.15 | async-start | bytes 8388608 | tf_op jit(solution)/shard_map/psum | solution.py:218
  362.6 3.3 copy-start.2
  675.8 10.0 copy-start.52
  675.8 10.0 copy-start.46
  696.1 208.3 %reduce-scatter.12.cloned.1.call-start = ((), (), s32[]{:S(2)}) async-start(), calls=%async_computation.18 | async-start | bytes 1179648 | tf_op jit(solution)/shard_map/reduce_scatter | solution.py:320
  779.9 6.0 copy-start.12
  779.9 7.1 copy-start.24
  779.9 15.5 slice-start
  787.0 5.0 copy-start.48
  787.0 8.5 slice-start.1
  792.0 3.3 copy-start.15
  795.5 4.4 slice-start.2
  798.0 2.2 slice-start.3
  805.2 5.1 copy-start.21
  810.3 2.5 copy-start.17
  814.0 12.5 copy-start.13
  820.4 6.2 copy-start.14
  820.4 1.7 copy-start.8
  820.4 1.7 copy-start.36
  820.4 1.7 copy-start.44
  823.9 2.7 copy-start.4
  826.5 2.2 copy-start.38
  826.5 2.2 copy-start.41
  828.7 5.2 copy-start.42
  833.7 218.6 %all-reduce.18.cloned.1.call-start = ((), (), s32[]{:S(2)}) async-start(), calls=%async_computation.23 | async-start | bytes 16777216 | tf_op jit(solution)/shard_map/psum | solution.py:203
  833.9 5.1 copy-start.22
  833.9 5.4 copy-start.29
  840.9 2.4 copy-start.26
  841.0 2.4 copy-start.30
  846.7 5.0 copy-start.32
  846.7 273.0 %reduce-scatter.10.cloned.1.call-start = ((), (), s32[]{:S(2)}) async-start(), calls=%async_computation.17 | async-start | bytes 1179648 | tf_op jit(solution)/shard_map/reduce_scatter | solution.py:317
  851.7 6.9 copy-start.34
  851.7 339.5 %reduce-scatter.8.cloned.1.call-start = ((), (), s32[]{:S(2)}) async-start(), calls=%async_computation.16 | async-start | bytes 2359296 | tf_op jit(solution)/shard_map/reduce_scatter | solution.py:314
  858.3 404.0 %reduce-scatter.14.cloned.1.call-start = ((), (), s32[]{:S(2)}) async-start(), calls=%async_computation.19 | async-start | bytes 2359296 | tf_op jit(solution)/shard_map/reduce_scatter | solution.py:323
  865.7 517.5 %reduce-scatter.16.cloned.1.call-start = ((), (), s32[]{:S(2)}) async-start(), calls=%async_computation.20 | async-start | bytes 7077888 | tf_op jit(solution)/shard_map/reduce_scatter | solution.py:331
  877.3 1.9 copy-start.54
  877.3 627.0 %reduce-scatter.18.cloned.1.call-start = ((), (), s32[]{:S(2)}) async-start(), calls=%async_computation.21 | async-start | bytes 7077888 | tf_op jit(solution)/shard_map/reduce_scatter | solution.py:334
  890.2 1.9 copy-start.53
  890.2 735.5 %reduce-scatter.20.cloned.1.call-start = ((), (), s32[]{:S(2)}) async-start(), calls=%async_computation.22 | async-start | bytes 7077888 | tf_op jit(solution)/shard_map/reduce_scatter | solution.py:337
  (12 other events, 15.9 us)
Sparse Core Ops, SparseCore 0:
  10.7 42.9 all-gather.11
  56.4 39.0 all-gather.9
  98.2 48.0 all-gather.13
  148.8 49.5 all-gather.15
  205.8 151.0 all-reduce.13
  359.5 99.1 all-gather.17
  461.4 97.1 all-gather.19
  561.3 98.1 all-gather.21
  696.2 83.6 all-reduce.15
  833.8 63.5 reduce-scatter.11
  900.0 152.2 all-reduce.17
  1056.1 63.6 reduce-scatter.9
  1124.3 66.9 reduce-scatter.7
  1195.0 67.2 reduce-scatter.13
  1266.2 117.0 reduce-scatter.15
  1387.1 117.0 reduce-scatter.17
  1508.2 117.5 reduce-scatter.19
where the time goes:
time: 1650 us; the launch traced here: 1640 us
  waiting for transfers between devices  1230 us (75%)
  matrix products  182 us (11%)
  other arithmetic  98.9 us (6%)
  blocking collectives  84.5 us (5%)
  local copies, waits for them, and re-layouts  17.7 us (1%)
  between operations  17.4 us (1%)
    psum x1, waiting for transfers between devices, on_device(): lax.psum(mlp_part.astype(jnp.bfloat16), 'mp').astype(jnp.float32)  146 us
    psum x1, waiting for transfers between devices, on_device(): hidden = inputs + lax.psum(attn_part, 'mp')  127 us
    reduce_scatter x1, waiting for transfers between devices, on_device(): lax.psum_scatter(down_grad.astype(jnp.bfloat16), 'dp', scatter_dimension=...  119 us
    reduce_scatter x1, waiting for transfers between devices, on_device(): lax.psum_scatter(up_grad.astype(jnp.bfloat16), 'dp', scatter_dimension=0,...  119 us
    reduce_scatter x1, waiting for transfers between devices, on_device(): lax.psum_scatter(gate_grad.astype(jnp.bfloat16), 'dp', scatter_dimension=...  110 us
    all_gather x1, waiting for transfers between devices, on_device(): lax.all_gather(gate_weight.astype(jnp.bfloat16), 'dp', axis=0, tiled=True)  90.1 us
    all_gather x1, waiting for transfers between devices, on_device(): lax.all_gather(down_weight.astype(jnp.bfloat16), 'dp', axis=1, tiled=True)  89.1 us
    all_gather x1, waiting for transfers between devices, on_device(): lax.all_gather(up_weight.astype(jnp.bfloat16), 'dp', axis=0, tiled=True)  88.1 us
  transfers between devices with their start and end apart: 17, of which 15 were waited for; matrix products, arithmetic and copies ran while one was open for 11% of the time, Pallas kernels for 0%

commit v1 on v0

v1 whole, which is shorter than its diff:
```python
import functools

import jax
import jax.numpy as jnp
from jax import lax
from jax.experimental import pallas as pl
from jax.experimental.pallas import tpu as pltpu
from jax.sharding import PartitionSpec as P

QUERY_HEADS = 16
KEY_VALUE_HEADS = 8
HEAD_WIDTH = 128
GROUP = QUERY_HEADS // KEY_VALUE_HEADS

EPSILON = 1e-06
MASKED = -1e30
MESH = pl.DeviceIdType.MESH
F32 = jnp.float32
BF16 = jnp.bfloat16
MIB = 2**20


def rope_tables(positions, head_size):
    middle = head_size // 2
    frequency = jnp.power(1000000.0, -2.0 * jnp.arange(middle, dtype=F32) / head_size)
    angles = positions.astype(F32)[:, None] * frequency[None, :]
    cosine_table = jnp.cos(angles)
    sine_table = jnp.sin(angles)
    return (
        jnp.concatenate([cosine_table, cosine_table], -1),
        jnp.concatenate([sine_table, sine_table], -1),
    )


def rotate(values):
    middle = values.shape[-1] // 2
    return jnp.concatenate([-values[..., middle:], values[..., :middle]], -1)


def rotate_back(values):
    middle = values.shape[-1] // 2
    return jnp.concatenate([values[..., middle:], -values[..., :middle]], -1)


def norm_parts(values):
    scaling = lax.rsqrt(jnp.mean(values * values, -1, keepdims=True) + EPSILON)
    return (values * scaling, scaling)


def norm_back(grad_normed, normed_hat, scaling, gains):
    scaled = grad_normed * gains
    return scaling * (scaled - normed_hat * jnp.mean(scaled * normed_hat, -1, keepdims=True))


def dot(left, right, left_dim=1, right_dim=0):
    return lax.dot_general(
        left, right, (((left_dim,), (right_dim,)), ((), ())), preferred_element_type=F32
    )


CHUNKS = 2
TILE = 32


def neighbours():
    dp, mp = lax.axis_index("dp"), lax.axis_index("mp")
    x, c = mp // 2, mp % 2
    return (
        x,
        c,
        (dp, x * 2 + 1 - c),
        (dp, (1 - x) * 2 + c),
        (dp + 1 - 2 * (dp % 2), mp),
    )


def enter(peers):
    barrier = pltpu.get_barrier_semaphore()
    for peer in peers:
        pl.semaphore_signal(barrier, inc=1, device_id=peer, device_id_type=MESH)
    pl.semaphore_wait(barrier, len(peers))


def remote(src, dst, send, recv, peer):
    return pltpu.make_async_remote_copy(
        src_ref=src, dst_ref=dst, send_sem=send, recv_sem=recv, device_id=peer, device_id_type=MESH
    )


def tiles(start, rows, step):
    def body(i, carry):
        step(pl.ds(pl.multiple_of(start + i * TILE, TILE), TILE))
        return carry

    lax.fori_loop(0, rows // TILE, body, 0)


class Reduce:
    STAGES = 5

    def __init__(self, part, mine, got, gx, gy, fx, fy, local, send, recv):
        self.refs = (part, mine, got, gx, gy, fx, fy, local, send, recv)
        self.rows = part.shape[3] // CHUNKS
        self.half = part.shape[4] // 2

    @staticmethod
    def scratch(rows, width):
        half = width // 2
        return [
            pltpu.VMEM((2, 2, rows, width), BF16),
            pltpu.VMEM((2, 2, rows, width), BF16),
            pltpu.VMEM((2, rows, half), BF16),
            pltpu.VMEM((2, rows, half), BF16),
            pltpu.VMEM((rows, half), BF16),
            pltpu.VMEM((rows, half), BF16),
            pltpu.SemaphoreType.DMA((CHUNKS,)),
            pltpu.SemaphoreType.DMA((Reduce.STAGES, CHUNKS)),
            pltpu.SemaphoreType.DMA((Reduce.STAGES, CHUNKS)),
        ]

    def copy(self, k, i):
        part, mine, got, gx, gy, fx, fy, local, send, recv = self.refs
        x, c, core_peer, x_peer, y_peer = neighbours()
        rows = pl.ds(k * self.rows, self.rows)
        low, high = pl.ds(0, self.half), pl.ds(self.half, self.half)
        s = [send.at[j, k] for j in range(self.STAGES)]
        r = [recv.at[j, k] for j in range(self.STAGES)]
        all_copies = (
            lambda: pltpu.make_async_copy(part.at[:, :, c, rows], mine.at[:, :, rows], local.at[k]),
            lambda: remote(part.at[:, :, 1 - c, rows], got.at[:, :, rows], s[0], r[0], core_peer),
            lambda: remote(mine.at[:, 1 - x, rows, low], gx.at[:, rows], s[1], r[1], x_peer),
            lambda: remote(mine.at[1, :, rows, high], gy.at[:, rows], s[2], r[2], y_peer),
            lambda: remote(mine.at[1, x, rows, low], fy.at[rows], s[3], r[3], y_peer),
            lambda: remote(mine.at[0, 1 - x, rows, high], fx.at[rows], s[4], r[4], x_peer),
        )
        return all_copies[i]()

    def begin(self, k):
        self.copy(k, 1).start()
        self.copy(k, 0).start()

    def first(self, k):
        _, mine, got = self.refs[:3]
        self.copy(k, 0).wait()
        self.copy(k, 1).wait_recv()

        def add(i, carry):
            def step(rows):
                at = (i // 2, i % 2, rows)
                mine[at] = (mine[at].astype(F32) + got[at].astype(F32)).astype(BF16)

            tiles(k * self.rows, self.rows, step)
            return carry

        lax.fori_loop(0, 4, add, 0)
        self.copy(k, 2).start()
        self.copy(k, 3).start()

    def second(self, k):
        _, mine, _, gx, gy = self.refs[:5]
        x = neighbours()[0]
        low, high = pl.ds(0, self.half), pl.ds(self.half, self.half)
        self.copy(k, 2).wait_recv()
        self.copy(k, 3).wait_recv()

        def step(rows):
            for i in range(2):
                at = (i, x, rows, low)
                mine[at] = (mine[at].astype(F32) + gx[i, rows].astype(F32)).astype(BF16)
                at = (0, i, rows, high)
                mine[at] = (mine[at].astype(F32) + gy[i, rows].astype(F32)).astype(BF16)

        tiles(k * self.rows, self.rows, step)
        self.copy(k, 4).start()
        self.copy(k, 5).start()

    def arrive(self, k):
        self.copy(k, 4).wait_recv()
        self.copy(k, 5).wait_recv()

    def take(self, rows):
        _, mine, _, _, _, fx, fy = self.refs[:7]
        x = neighbours()[0]
        low, high = pl.ds(0, self.half), pl.ds(self.half, self.half)
        return jnp.concatenate(
            [
                mine[0, x, rows, low].astype(F32) + fy[rows].astype(F32),
                mine[0, x, rows, high].astype(F32) + fx[rows].astype(F32),
            ],
            -1,
        )

    def finish(self):
        for k in range(CHUNKS):
            for i in range(1, 6):
                self.copy(k, i).wait_send()


class Gather:
    STAGES = 9

    def __init__(self, mine, full, local, send, recv):
        self.refs = (mine, full, local, send, recv)
        self.rows = mine.shape[0] // CHUNKS
        self.half = mine.shape[1] // 2

    @staticmethod
    def scratch(rows, width):
        return [
            pltpu.VMEM((rows, width), BF16),
            pltpu.SemaphoreType.DMA((CHUNKS,)),
            pltpu.SemaphoreType.DMA((Gather.STAGES, CHUNKS)),
            pltpu.SemaphoreType.DMA((Gather.STAGES, CHUNKS)),
        ]

    def copy(self, k, i):
        mine, full, local, send, recv = self.refs
        x, c, core_peer, x_peer, y_peer = neighbours()
        rows = pl.ds(k * self.rows, self.rows)
        low, high = pl.ds(0, self.half), pl.ds(self.half, self.half)
        s = [send.at[j, k] for j in range(self.STAGES)]
        r = [recv.at[j, k] for j in range(self.STAGES)]

        def pass_on(j, at, peer):
            return lambda: remote(full.at[at], full.at[at], s[j], r[j], peer)

        all_copies = (
            lambda: pltpu.make_async_copy(mine.at[rows], full.at[0, x, c, rows], local.at[k]),
            lambda: remote(mine.at[rows, low], full.at[1, x, c, rows, low], s[0], r[0], y_peer),
            lambda: remote(mine.at[rows, high], full.at[0, x, c, rows, high], s[1], r[1], x_peer),
            lambda: remote(mine.at[rows], full.at[0, x, c, rows], s[2], r[2], core_peer),
            pass_on(3, (slice(None), x, c, rows, low), x_peer),
            lambda: remote(
                full.at[0, :, c, rows, high], full.at[1, :, c, rows, high], s[4], r[4], y_peer
            ),
            pass_on(5, (1, x, c, rows, low), core_peer),
            pass_on(6, (0, 1 - x, c, rows, high), core_peer),
            pass_on(7, (slice(None), 1 - x, c, rows, low), core_peer),
            pass_on(8, (1, slice(None), c, rows, high), core_peer),
        )
        return all_copies[i]()

    def begin(self, k):
        for i in (1, 2, 0, 3):
            self.copy(k, i).start()

    def second(self, k):
        self.copy(k, 0).wait()
        self.copy(k, 1).wait_recv()
        self.copy(k, 4).start()
        self.copy(k, 2).wait_recv()
        for i in (5, 6, 7):
            self.copy(k, i).start()

    def third(self, k):
        for i in (4, 5):
            self.copy(k, i).wait_recv()
            self.copy(k, i + 4).start()

    def finish(self):
        for k in range(CHUNKS):
            for i in (3, 6, 7, 8, 9):
                self.copy(k, i).wait_recv()
            for i in range(1, 10):
                self.copy(k, i).wait_send()


def attention_leg(part, tokens, gain, hidden, normed, *scratch):
    n = len(Reduce.scratch(32, 256))
    reduce, gather = Reduce(part, *scratch[:n]), Gather(scratch[n], normed, *scratch[n + 1 :])
    mine = scratch[n]
    enter(neighbours()[2:])
    for k in range(CHUNKS):
        reduce.begin(k)
    for k in range(CHUNKS):
        reduce.first(k)
    for k in range(CHUNKS):
        reduce.second(k)

    def step(rows):
        h = tokens[rows].astype(F32) + reduce.take(rows)
        hidden[rows] = h
        mine[rows] = (norm_parts(h)[0] * gain[...]).astype(BF16)

    for k in range(CHUNKS):
        reduce.arrive(k)
        tiles(k * reduce.rows, reduce.rows, step)
        gather.begin(k)
    for k in range(CHUNKS):
        gather.second(k)
    for k in range(CHUNKS):
        gather.third(k)
    gather.finish()
    reduce.finish()


def hidden_leg(part, hidden, cotangent, gain, grad_hidden, gain_grad, full, *scratch):
    n = len(Reduce.scratch(32, 256))
    reduce, gather = Reduce(part, *scratch[:n]), Gather(scratch[n], full, *scratch[n + 1 :])
    mine = scratch[n]
    enter(neighbours()[2:])
    for k in range(CHUNKS):
        reduce.begin(k)
    gain_grad[...] = jnp.zeros_like(gain_grad)
    for k in range(CHUNKS):
        reduce.first(k)
    for k in range(CHUNKS):
        reduce.second(k)

    def step(rows):
        grad = reduce.take(rows)
        hat, inv = norm_parts(hidden[rows])
        gain_grad[...] += jnp.sum(grad * hat, 0, keepdims=True)
        grad = cotangent[rows].astype(F32) + norm_back(grad, hat, inv, gain[...])
        grad_hidden[rows] = grad
        mine[rows] = grad.astype(BF16)

    for k in range(CHUNKS):
        reduce.arrive(k)
        tiles(k * reduce.rows, reduce.rows, step)
        gather.begin(k)
    for k in range(CHUNKS):
        gather.second(k)
    for k in range(CHUNKS):
        gather.third(k)
    gather.finish()
    reduce.finish()


def output_leg(
    part, mlp_part, tokens, hidden, grad_hidden, gain, input_grad, output, gain_grad, *scratch
):
    n = len(Reduce.scratch(32, 256))
    legs = Reduce(part, *scratch[:n]), Reduce(mlp_part, *scratch[n:])
    enter(neighbours()[2:])
    for reduce in legs:
        for k in range(CHUNKS):
            reduce.begin(k)
    gain_grad[...] = jnp.zeros_like(gain_grad)
    for reduce in legs:
        for k in range(CHUNKS):
            reduce.first(k)
    for reduce in legs:
        for k in range(CHUNKS):
            reduce.second(k)

    def step_grad(rows):
        grad = legs[0].take(rows)
        hat, inv = norm_parts(tokens[rows].astype(F32))
        gain_grad[...] += jnp.sum(grad * hat, 0, keepdims=True)
        input_grad[rows] = grad_hidden[rows] + norm_back(grad, hat, inv, gain[...])

    def step_output(rows):
        output[rows] = (hidden[rows] + legs[1].take(rows)).astype(BF16)

    for reduce, step in zip(legs, (step_grad, step_output)):
        for k in range(CHUNKS):
            reduce.arrive(k)
            tiles(k * reduce.rows, reduce.rows, step)
    for reduce in legs:
        reduce.finish()


ANY = pl.BlockSpec(memory_space=pl.ANY)
VM = pl.BlockSpec(memory_space=pltpu.VMEM)


def call_leg(kernel, ident, name, in_specs, out_shape, out_specs, scratch, bytes_moved):
    return pl.pallas_call(
        kernel,
        out_shape=out_shape,
        in_specs=in_specs,
        out_specs=out_specs,
        scratch_shapes=scratch,
        name=name,
        cost_estimate=pl.CostEstimate(flops=0, bytes_accessed=bytes_moved, transcendentals=0),
        compiler_params=pltpu.CompilerParams(
            collective_id=ident, has_side_effects=True, vmem_limit_bytes=56 * MIB
        ),
    )


def scores_of(queries, keys, doc_rows, start, factor):
    scores = jnp.einsum("sqrd,skd->srqk", queries, keys, preferred_element_type=F32) * factor
    query_index = start + jnp.arange(queries.shape[1])
    key_index = jnp.arange(keys.shape[1])
    allowed = (doc_rows[:, start : start + queries.shape[1], None] == doc_rows[:, None, : keys.shape[1]]) & (
        key_index[None, None, :] <= query_index[None, :, None]
    )
    return jnp.where(allowed[:, None], scores, MASKED)


def on_device(
    tokens,
    documents,
    cotangent,
    attn_gain,
    query_gain,
    key_norm_scale,
    query_weight,
    key_projection,
    value_projection,
    output_weight,
    mlp_gain,
    gate_weight,
    up_weight,
    down_weight,
):
    n_dp = lax.axis_size("dp")
    dp, mp = lax.axis_index("dp"), lax.axis_index("mp")
    y, core = dp % 2, mp % 2
    slabs = [[i + 2 * k for k in range(n_dp // 2)] for i in range(2)]
    rows, width = tokens.shape
    seq_length = documents.shape[1]
    seqs = 2 * documents.shape[0]
    share = rows // 4
    head = HEAD_WIDTH
    factor = head ** (-0.5)
    query_cols, key_cols, hidden_cols = (
        query_weight.shape[1] // 2,
        key_projection.shape[1] // 2,
        gate_weight.shape[1] // 2,
    )
    attn_cols = query_cols + 2 * key_cols

    def y_swap(values):
        return lax.ppermute(values, "dp", [(i, i ^ 1) for i in range(n_dp)])

    def core_swap(values):
        return lax.ppermute(values, "mp", [(i, i ^ 1) for i in range(4)])

    def in_order(where, mine, other, axis):
        return jnp.where(
            where == 0,
            jnp.concatenate([mine, other], axis),
            jnp.concatenate([other, mine], axis),
        )

    def half(values, which, axis):
        size = values.shape[axis] // 2
        return lax.dynamic_slice_in_dim(values, which * size, size, axis)

    def slab_gather(values):
        return lax.all_gather(values, "dp", axis=0, tiled=True, axis_index_groups=slabs)

    def slab_scatter(values):
        return lax.psum_scatter(
            values, "dp", scatter_dimension=0, tiled=True, axis_index_groups=slabs
        )

    attn_low = [w.astype(BF16) for w in (query_weight, key_projection, value_projection)]
    output_low = output_weight.astype(BF16)

    def attn_pack(which):
        return jnp.concatenate(
            [half(w, which, 1) for w in attn_low] + [half(output_low, which, 0).T], 1
        )

    attn_mine = in_order(y, attn_pack(y), y_swap(attn_pack(1 - y)), 0)
    attn_full = slab_gather(attn_mine)

    mlp_low = [w.astype(BF16) for w in (gate_weight, up_weight)]
    down_low = down_weight.astype(BF16)

    def mlp_pack(which):
        return jnp.concatenate([half(w, which, 1) for w in mlp_low], 1)

    mlp_mine = in_order(y, mlp_pack(y), y_swap(mlp_pack(1 - y)), 0)
    down_mine = in_order(y, half(down_low, y, 0).T, y_swap(half(down_low, 1 - y, 0).T), 0)
    gate_up_full = slab_gather(mlp_mine)
    down_full = slab_gather(down_mine)

    gains = lax.all_gather(
        jnp.concatenate(
            [
                g.astype(BF16).reshape(1, -1)
                for g in (attn_gain, mlp_gain, query_gain, key_norm_scale)
            ],
            1,
        ),
        "dp",
        axis=0,
        tiled=True,
    ).astype(F32)
    n_gain, n_head = attn_gain.shape[0], query_gain.shape[0]
    gain_one = gains[:, :n_gain].reshape(1, width)
    gain_two = gains[:, n_gain : 2 * n_gain].reshape(1, width)
    gain_query = gains[:, 2 * n_gain : 2 * n_gain + n_head].reshape(head)
    gain_key = gains[:, 2 * n_gain + n_head :].reshape(head)

    def partner_rows(values):
        got = y_swap(half(values, core, 0))
        return in_order(core, got, core_swap(got), 0)

    tokens_pair = jnp.concatenate([tokens, partner_rows(tokens)], 0)
    cot_pair = jnp.concatenate([cotangent, partner_rows(cotangent)], 0)
    docs = jnp.concatenate([documents, y_swap(documents)], 0)
    pair_rows = 2 * rows
    tokens_share = lax.dynamic_slice_in_dim(tokens, mp * share, share, 0)
    cot_share = lax.dynamic_slice_in_dim(cotangent, mp * share, share, 0)

    inputs = tokens_pair.astype(F32)
    normed_one = (norm_parts(inputs)[0] * gain_one).astype(BF16)
    raw = dot(normed_one, attn_full[:, :attn_cols])
    query_raw, key_raw = raw[:, :query_cols], raw[:, query_cols : query_cols + key_cols]
    values = raw[:, query_cols + key_cols :].astype(BF16)
    starts = sum((docs < i).sum(1, keepdims=True) * (docs == i) for i in range(1, 4))
    positions = (jnp.arange(seq_length, dtype=jnp.int32)[None] - starts).reshape(pair_rows)
    cosine, sine = rope_tables(positions, head)
    cosine, sine = cosine[:, None, :], sine[:, None, :]
    query_hat, query_inv = norm_parts(query_raw.reshape(pair_rows, GROUP, head))
    key_hat, key_inv = norm_parts(key_raw.reshape(pair_rows, 1, head))
    query_normed, key_normed = query_hat * gain_query, key_hat * gain_key
    queries = (query_normed * cosine + rotate(query_normed) * sine).astype(BF16)
    keys = (key_normed * cosine + rotate(key_normed) * sine).astype(BF16)
    queries = queries.reshape(seqs, seq_length, GROUP, head)
    keys = keys.reshape(seqs, seq_length, head)
    values = values.reshape(seqs, seq_length, head)
    block = min(512, seq_length)
    outputs, log_totals = [], []
    for start in range(0, seq_length, block):
        end = start + block
        scores = scores_of(queries[:, start:end], keys[:, :end], docs, start, factor)
        highest = jnp.max(scores, -1, keepdims=True)
        exponent = jnp.exp(scores - highest)
        totals = jnp.sum(exponent, -1, keepdims=True)
        weights = (exponent / totals).astype(BF16)
        outputs.append(
            jnp.einsum("srqk,skd->sqrd", weights, values[:, :end], preferred_element_type=F32)
        )
        log_totals.append(highest + jnp.log(totals))
    attended = jnp.concatenate(outputs, 1).reshape(pair_rows, GROUP * head).astype(BF16)
    out_mat = attn_full[:, attn_cols:]
    attn_part = dot(attended, out_mat, 1, 1).astype(BF16)

    grouped = (2, 2, 2, share, width)
    reduce_scratch, gather_scratch = Reduce.scratch(share, width), Gather.scratch(share, width)
    hidden, normed_two = call_leg(
        attention_leg,
        0,
        "attention_leg",
        [ANY, VM, VM],
        (jax.ShapeDtypeStruct((share, width), F32), jax.ShapeDtypeStruct(grouped, BF16)),
        (VM, ANY),
        reduce_scratch + gather_scratch,
        200 * MIB,
    )(attn_part.reshape(grouped), tokens_share, gain_two)
    normed_two = normed_two.reshape(pair_rows, width)

    gate_up = dot(normed_two, gate_up_full)
    gate_pre, up_pre = gate_up[:, :hidden_cols], gate_up[:, hidden_cols:]
    sigmoid = jax.nn.sigmoid(gate_pre)
    swish = gate_pre * sigmoid
    active = (swish * up_pre).astype(BF16)
    down_grad = slab_scatter(dot(cot_pair, active, 0, 0).astype(BF16))
    mlp_part = dot(active, down_full, 1, 1).astype(BF16)
    grad_active = dot(cot_pair, down_full)
    grad_gate = (grad_active * up_pre * sigmoid * (1.0 + gate_pre * (1.0 - sigmoid))).astype(BF16)
    grad_up = (grad_active * swish).astype(BF16)
    grad_gate_up = jnp.concatenate([grad_gate, grad_up], 1)
    gate_up_grad = slab_scatter(dot(normed_two, grad_gate_up, 0, 0).astype(BF16))
    normed_two_part = dot(grad_gate_up, gate_up_full, 1, 1).astype(BF16)

    grad_hidden, mlp_gain_part, grad_hidden_low = call_leg(
        hidden_leg,
        1,
        "hidden_leg",
        [ANY, VM, VM, VM],
        (
            jax.ShapeDtypeStruct((share, width), F32),
            jax.ShapeDtypeStruct((1, width), F32),
            jax.ShapeDtypeStruct(grouped, BF16),
        ),
        (VM, VM, ANY),
        reduce_scratch + gather_scratch,
        200 * MIB,
    )(normed_two_part.reshape(grouped), hidden, cot_share, gain_two)
    grad_hidden_low = grad_hidden_low.reshape(pair_rows, width)

    output_grad = dot(grad_hidden_low, attended, 0, 0).astype(BF16)
    grad_attended = dot(grad_hidden_low, out_mat).astype(BF16)
    grad_attended = grad_attended.reshape(seqs, seq_length, GROUP, head)
    query_grads = []
    key_rot_grad = jnp.zeros((seqs, seq_length, head), F32)
    value_grad = jnp.zeros((seqs, seq_length, head), F32)
    for i, start in enumerate(range(0, seq_length, block)):
        end = start + block
        block_queries, block_grad = queries[:, start:end], grad_attended[:, start:end]
        scores = scores_of(block_queries, keys[:, :end], docs, start, factor)
        weights = jnp.exp(scores - log_totals[i])
        grad_weights = jnp.einsum(
            "sqrd,skd->srqk", block_grad, values[:, :end], preferred_element_type=F32
        )
        inner = jnp.sum(weights * grad_weights, -1, keepdims=True)
        grad_scores = (weights * (grad_weights - inner)).astype(BF16)
        query_grads.append(
            jnp.einsum("srqk,skd->sqrd", grad_scores, keys[:, :end], preferred_element_type=F32)
            * factor
        )
        key_rot_grad = key_rot_grad.at[:, :end].add(
            jnp.einsum("srqk,sqrd->skd", grad_scores, block_queries, preferred_element_type=F32)
            * factor
        )
        value_grad = value_grad.at[:, :end].add(
            jnp.einsum(
                "srqk,sqrd->skd", weights.astype(BF16), block_grad, preferred_element_type=F32
            )
        )
    query_rot_grad = jnp.concatenate(query_grads, 1).reshape(pair_rows, GROUP, head)
    key_rot_grad = key_rot_grad.reshape(pair_rows, 1, head)
    query_norm_grad = query_rot_grad * cosine + rotate_back(query_rot_grad * sine)
    key_norm_grad = key_rot_grad * cosine + rotate_back(key_rot_grad * sine)
    query_gain_part = jnp.sum(query_norm_grad * query_hat, (0, 1))
    key_gain_part = jnp.sum(key_norm_grad * key_hat, (0, 1))
    raw_grad = jnp.concatenate(
        [
            norm_back(query_norm_grad, query_hat, query_inv, gain_query)
            .reshape(pair_rows, query_cols)
            .astype(BF16),
            norm_back(key_norm_grad, key_hat, key_inv, gain_key)
            .reshape(pair_rows, key_cols)
            .astype(BF16),
            value_grad.reshape(pair_rows, key_cols).astype(BF16),
        ],
        1,
    )
    attn_grad = slab_scatter(
        jnp.concatenate([dot(normed_one, raw_grad, 0, 0).astype(BF16), output_grad], 1)
    )
    normed_one_part = dot(raw_grad, attn_full[:, :attn_cols], 1, 1).astype(BF16)

    input_grad, layer_output, attn_gain_part = call_leg(
        output_leg,
        2,
        "output_leg",
        [ANY, ANY, VM, VM, VM, VM],
        (
            jax.ShapeDtypeStruct((share, width), F32),
            jax.ShapeDtypeStruct((share, width), BF16),
            jax.ShapeDtypeStruct((1, width), F32),
        ),
        (VM, VM, VM),
        reduce_scratch + reduce_scratch,
        200 * MIB,
    )(
        normed_one_part.reshape(grouped),
        mlp_part.reshape(grouped),
        tokens_share,
        hidden,
        grad_hidden,
        gain_one,
    )

    def back(values):
        other = y_swap(half(values, 1 - y, 0)).astype(F32)
        return half(values, y, 0).astype(F32), other

    attn_own, attn_other = back(attn_grad)
    gate_up_own, gate_up_other = back(gate_up_grad)
    down_own, down_other = back(down_grad)

    def columns(own, other, start, size, axis=1):
        own, other = own[:, start : start + size], other[:, start : start + size]
        if axis == 0:
            own, other = own.T, other.T
        return in_order(y, own, other, axis)

    gain_parts = jnp.concatenate(
        [
            attn_gain_part.reshape(-1, n_gain),
            mlp_gain_part.reshape(-1, n_gain),
            query_gain_part.reshape(-1, n_head),
            key_gain_part.reshape(-1, n_head),
        ],
        1,
    )
    gain_sums = lax.psum(gain_parts, ("dp", "mp"))
    gain_sums = lax.dynamic_slice_in_dim(gain_sums, dp, 1, 0)[0]
    return (
        layer_output,
        input_grad,
        gain_sums[:n_gain],
        gain_sums[2 * n_gain : 2 * n_gain + n_head],
        gain_sums[2 * n_gain + n_head :],
        columns(attn_own, attn_other, 0, query_cols),
        columns(attn_own, attn_other, query_cols, key_cols),
        columns(attn_own, attn_other, query_cols + key_cols, key_cols),
        columns(attn_own, attn_other, attn_cols, query_cols, 0),
        gain_sums[n_gain : 2 * n_gain],
        columns(gate_up_own, gate_up_other, 0, hidden_cols),
        columns(gate_up_own, gate_up_other, hidden_cols, hidden_cols),
        columns(down_own, down_other, 0, hidden_cols, 0),
    )


def solution(mesh):
    in_specs = (
        P("dp", None),
        P("dp", None),
        P("dp", None),
        P("dp"),
        P("dp"),
        P("dp"),
        P("dp", "mp"),
        P("dp", "mp"),
        P("dp", "mp"),
        P("mp", "dp"),
        P("dp"),
        P("dp", "mp"),
        P("dp", "mp"),
        P("mp", "dp"),
    )
    out_specs = (
        P(("dp", "mp"), None),
        P(("dp", "mp"), None),
        P("dp"),
        P("dp"),
        P("dp"),
        P("dp", "mp"),
        P("dp", "mp"),
        P("dp", "mp"),
        P("mp", "dp"),
        P("dp"),
        P("dp", "mp"),
        P("dp", "mp"),
        P("mp", "dp"),
    )
    return jax.shard_map(
        on_device, mesh=mesh, in_specs=in_specs, out_specs=out_specs, check_vma=False
    )
```

time: 1650 us -> 829 us (0.50)
  waiting for transfers between devices: 1230 us -> 48.4 us
  Pallas kernels: 0 us -> 244 us
  blocking collectives: 84.5 us -> 168 us
  local copies, waits for them, and re-layouts: 17.7 us -> 98.1 us
  matrix products: 182 us -> 157 us
  other arithmetic: 98.9 us -> 80.1 us
    reduce_scatter x7 -> x3, waiting for transfers between devices: 512 us -> 0.02 us  [slab_scatter(): lax.psum_scatter(values, 'dp', scatter_dimension=0, tiled=True, axis_inde...]
    all_gather x7 -> x3, waiting for transfers between devices: 375 us -> 0.02 us  [slab_gather(): lax.all_gather(values, 'dp', axis=0, tiled=True, axis_index_groups=slabs)]
    psum x3 -> x0, waiting for transfers between devices: 345 us -> none  [the longest x1 146 us: on_device(): lax.psum(mlp_part.astype(jnp.bfloat16), 'mp').astype(jnp.float32)]
    pallas_call x0 -> x3, Pallas kernels: none -> 244 us  [the longest x1 81.9 us: on_device(): call_leg(hidden_leg, 1, 'hidden_leg', [ANY, VM, VM, VM], (jax.ShapeDtypeS...]
    all_gather x2 -> x1, blocking collectives: 39.7 us -> 119 us  [on_device(): lax.all_gather(jnp.concatenate([g.astype(BF16).reshape(1, -1) for g in (a...]
    ppermute x0 -> x11, waiting for transfers between devices: none -> 48.3 us  [the longest x9 48.3 us: y_swap(): return lax.ppermute(values, 'dp', [(i, i ^ 1) for i in range(n_dp)])]
    psum x1, blocking collectives: 5.64 us -> 49.5 us  [on_device(): gain_sums = lax.psum(gain_parts, ('dp', 'mp'))]
    unnamed x2 -> x0, blocking collectives: 39.2 us -> none
  transfers between devices with their start and end apart: 17 -> 17, of which waited for: 15 -> 4; matrix products, arithmetic and copies ran while one was open for 11% -> 29% of each run, Pallas kernels for 0% -> 20%
where the time goes in v1:
time: 829 us; the launch traced here: 825 us
  Pallas kernels  244 us (29%)
  blocking collectives  168 us (20%)
  matrix products  157 us (19%)
  local copies, waits for them, and re-layouts  98.1 us (12%)
  other arithmetic  80.1 us (10%)
  waiting for transfers between devices  48.4 us (6%)
  between operations  16.1 us (2%)
  starting transfers between devices  12.9 us (2%)
    dot_general x12, matrix products, dot(): lax.dot_general(left, right, (((left_dim,), (right_dim,)), ((), ())), pre...  133 us
    all_gather x1, blocking collectives, on_device(): lax.all_gather(jnp.concatenate([g.astype(BF16).reshape(1, -1) for g in (a...  119 us
    pallas_call x1, Pallas kernels, on_device(): call_leg(hidden_leg, 1, 'hidden_leg', [ANY, VM, VM, VM], (jax.ShapeDtypeS...  81.9 us
    pallas_call x1, Pallas kernels, on_device(): call_leg(attention_leg, 0, 'attention_leg', [ANY, VM, VM], (jax.ShapeDtyp...  81.2 us
    pallas_call x1, Pallas kernels, on_device(): call_leg(output_leg, 2, 'output_leg', [ANY, ANY, VM, VM, VM, VM], (jax.Sh...  80.6 us
    psum x1, blocking collectives, on_device(): gain_sums = lax.psum(gain_parts, ('dp', 'mp'))  49.5 us
    ppermute x9, waiting for transfers between devices, y_swap(): return lax.ppermute(values, 'dp', [(i, i ^ 1) for i in range(n_dp)])  48.3 us
    unnamed x186, local copies, waits for them, and re-layouts  40.9 us
  transfers between devices with their start and end apart: 17, of which 4 were waited for; matrix products, arithmetic and copies ran while one was open for 29% of the time, Pallas kernels for 20%

profile of v1, /device:TPU:0, one launch (start us, length us, event | category | flops | bytes accessed | tf_op | source)
XLA Modules:
  0.0 825.1 jit_solution(11169496902301858702)
XLA Ops:
  11.9 3.0 collective-permute-start.2
  14.9 9.1 %collective-permute-done.2 = bf16[256,768]{0,1:T(8,128)(2,1)S(1)} collective-permute-done((bf16[256,768]{0,1:T(8,128)(2,1)S(1)}, bf16[256,768]{0,1:T(8,128)(2,1)S(1)}, u32[]{:S(2)}, u32[]{:S(2)}) %collective-permute-start.2) | collective-permute-done | bytes 393248 | tf_op jit(solution)/shard_map/ppermute | solution.py:427
  28.8 17.0 %collective-permute-done.7 = bf16[256,1536]{1,0:T(8,128)(2,1)S(1)} collective-permute-done((bf16[256,1536]{1,0:T(8,128)(2,1)S(1)}, bf16[256,1536]{1,0:T(8,128)(2,1)S(1)}, u32[]{:S(2)}, u32[]{:S(2)}) %collective-permute-start.7) | collective-permute-done | bytes 786464 | tf_op jit(solution)/shard_map/ppermute | solution.py:427
  47.7 1.9 constant_dynamic-slice_fusion.17
  56.2 119.0 %all-gather = bf16[8,1,544]{2,1,0:T(2,128)(2,1)S(1)} all-gather(bf16[1,1,544]{2,1,0:T(2,128)(2,1)S(1)} %maximum_bitcast_fusion), channel_id=1, replica_groups=mesh['dp'=8,'mp'=4] {'dp'}, dimensions={0}, use_global_device_ids=true | all-gather | bytes 9792 | tf_op jit(solution)/shard_map/all_gather | solution.py:473
  178.2 2.3 constant_dynamic-slice_fusion.9.tokens
  180.5 2.3 constant_dynamic-slice_fusion.4.cotangent
  185.8 2.7 fusion.80
  189.0 3.7 multiply_cosine_fusion
  195.5 2.2 copy.233
  199.5 2.2 maximum_select_fusion.7
  202.0 4.8 maximum_select_fusion
  206.8 2.0 fusion
  208.9 6.1 maximum_select_fusion.1
  215.0 8.9 %fusion.35 = f32[2048,512]{0,1:T(8,128)S(1)} fusion(bf16[2048,768]{0,1:T(8,128)(2,1)} %all-gather.5.cloned.1.call-done, f32[2048]{0:T(1024)S(1)} %bitcast.272, f32[2048]{0:T(1024)S(1)} %add_rsqrt_fusion.2, bf16[1024,2048]{1,0:T(8,128)(2,1)} %copy-done.11, bf16[1024,2048]{1,0:T(8,128)(2,1)} %param.26), kind=kOutput, calls=%fused_computation.84 | convolution fusion | flops 4324327424 | bytes 14696448 | tf_op jit(solution)/shard_map/dot_general | solution.py:56
  228.6 2.0 multiply_multiply_fusion
  232.7 1.8 copy.145
  234.5 3.2 concatenate.200
  237.8 2.7 copy.146
  240.5 2.8 reshape.610
  243.2 3.2 copy.144
  246.4 2.6 reshape.611
  249.0 2.0 copy.191
  251.0 3.2 fusion.27
  256.0 2.1 fusion.106
  259.3 2.2 copy-done
  266.3 1.9 copy.165
  268.8 2.2 copy.235
  271.0 6.9 convolution_convert_fusion.3
  277.9 81.2 %attention_leg.1 = (f32[256,2048]{1,0:T(8,128)}, bf16[2,2,2,256,2048]{4,3,2,1,0:T(8,128)(2,1)}) custom-call(bf16[2,2,2,256,2048]{4,3,2,1,0:T(8,128)(2,1)} %bitcast.238, bf16[256,2048]{1,0:T(8,128)(2,1)} %constant_dynamic-slice_fusion.9.tokens, f32[1,2048]{1,0:T(1,128)} %bitcast.267), custom_call_target="tpu_custom_call" | custom-call | bytes 209715200 | tf_op jit(solution)/shard_map/attention_leg/pallas_call | solution.py:538
  359.3 19.0 %fusion.108 = f32[2048,1536]{0,1:T(8,128)} fusion(bf16[2048,2048]{1,0:T(8,128)(2,1)} %bitcast.276, bf16[2048,1536]{1,0:T(8,128)(2,1)} %all-gather.9.cloned.1.call-done), kind=kOutput, calls=%fused_computation.249 | convolution fusion | flops 12884901888 | bytes 27262976 | tf_op jit(solution)/shard_map/dot_general | solution.py:56
  378.3 16.4 %multiply_convert_fusion.2 = (bf16[2048,768]{0,1:T(8,128)(2,1)S(1)}, bf16[2048,768]{0,1:T(8,128)(2,1)}, bf16[2048,768]{0,1:T(8,128)(2,1)}) fusion(f32[2048,1536]{0,1:T(8,128)} %fusion.108, bf16[2048,768]{0,1:T(8,128)(2,1)} %all-gather.7.cloned.1.call-done, bf16[1024,2048]{1,0:T(8,128)(2,1)} %maximum_select_fusion.1, bf16[1024,2048]{1,0:T(8,128)(2,1)} %param.28), kind=kOutput, calls=%fused_computation.26 | convolution fusion | flops 6482821120 | bytes 33554432 | tf_op jit(solution)/shard_map/dot_general | solution.py:56
  394.7 19.7 %convolution_convert_fusion.2 = bf16[2048,2048]{1,0:T(8,128)(2,1)} fusion(bf16[2048,1536]{1,0:T(8,128)(2,1)} %all-gather.9.cloned.1.call-done, bf16[2048,768]{0,1:T(8,128)(2,1)} %get-tuple-element.153, bf16[2048,768]{0,1:T(8,128)(2,1)S(1)} %get-tuple-element.152), kind=kOutput, calls=%fused_computation.18 | convolution fusion | flops 12901679104 | bytes 20971520 | tf_op jit(solution)/shard_map/dot_general | solution.py:56
  414.4 81.9 %hidden_leg.1 = (f32[256,2048]{1,0:T(8,128)}, f32[1,2048]{1,0:T(1,128)}, bf16[2,2,2,256,2048]{4,3,2,1,0:T(8,128)(2,1)}) custom-call(bf16[2,2,2,256,2048]{4,3,2,1,0:T(8,128)(2,1)} %bitcast.247, f32[256,2048]{1,0:T(8,128)} %get-tuple-element.86.hidden, bf16[256,2048]{1,0:T(8,128)(2,1)} %constant_dynamic-slice_fusion.4.cotangent, f32[1,2048]{1,0:T(1,128)} %bitcast.268), custom_call_target="tpu_custom_call" | custom-call | bytes 209715200 | tf_op jit(solution)/shard_map/hidden_leg/pallas_call | solution.py:564
  496.3 6.1 convolution_convert_fusion.7
  503.8 3.7 fusion.13
  512.8 2.4 fusion.5
  519.6 2.4 copy.163
  522.0 11.3 %fusion.19 = bf16[2048,768]{1,0:T(8,128)(2,1)} fusion(bf16[2048,768]{0,1:T(8,128)(2,1)} %get-tuple-element.154, bf16[1024,2048]{1,0:T(8,128)(2,1)} %maximum_select_fusion.1, bf16[1024,2048]{1,0:T(8,128)(2,1)} %param.28), kind=kOutput, calls=%fused_computation.47 | convolution fusion | flops 6460801024 | bytes 14680064 | tf_op jit(solution)/shard_map/dot_general | solution.py:56
  537.1 2.0 pad_maximum_fusion.11
  539.1 2.9 copy.166
  542.0 3.5 pad_maximum_fusion.12
  545.5 4.2 copy.175
  549.7 4.0 copy.234
  553.7 2.2 copy.231
  561.5 3.1 fusion.53
  564.6 5.7 fusion.49
  570.3 2.0 copy.218
  572.4 4.2 fusion.30
  578.0 4.5 multiply_reduce_fusion
  585.2 2.4 convolution_convert_fusion.6
  588.7 4.6 convolution_convert_fusion.5
  593.4 2.1 pad_maximum_fusion.9
  595.5 19.5 %convolution_convert_fusion.4 = bf16[2048,1536]{1,0:T(8,128)(2,1)} fusion(bf16[2048,2048]{1,0:T(8,128)(2,1)} %bitcast.277, bf16[2048,768]{0,1:T(8,128)(2,1)} %get-tuple-element.153, bf16[2048,768]{0,1:T(8,128)(2,1)} %copy-done.77), kind=kOutput, calls=%fused_computation.20 | convolution fusion | flops 12900630528 | bytes 20971520 | tf_op jit(solution)/shard_map/dot_general | solution.py:56
  616.3 8.6 %convolution_convert_fusion.1 = bf16[2048,2048]{1,0:T(8,128)(2,1)} fusion(bf16[2048,768]{0,1:T(8,128)(2,1)} %all-gather.5.cloned.1.call-done, bf16[2048,128]{0,1:T(8,128)(2,1)S(1)} %copy-done.55, bf16[2048,128]{0,1:T(8,128)(2,1)S(1)} %multiply_convert_fusion.3, bf16[2048,256]{0,1:T(8,128)(2,1)S(1)} %get-tuple-element.156), kind=kOutput, calls=%fused_computation.17 | convolution fusion | flops 4305453056 | bytes 12582912 | tf_op jit(solution)/shard_map/dot_general | solution.py:56
  624.9 9.4 %convolution_convert_fusion = bf16[2048,2048]{1,0:T(8,128)(2,1)} fusion(bf16[2048,768]{0,1:T(8,128)(2,1)S(1)} %copy-done.76, bf16[2048,768]{0,1:T(8,128)(2,1)S(1)} %copy-done.73), kind=kOutput, calls=%fused_computation.16 | convolution fusion | flops 6446645248 | bytes 14680064 | tf_op jit(solution)/shard_map/dot_general | solution.py:56
  634.2 80.6 %output_leg.1 = (f32[256,2048]{1,0:T(8,128)}, bf16[256,2048]{1,0:T(8,128)(2,1)}, f32[1,2048]{1,0:T(1,128)}) custom-call(bf16[2,2,2,256,2048]{4,3,2,1,0:T(8,128)(2,1)} %bitcast.245, bf16[2,2,2,256,2048]{4,3,2,1,0:T(8,128)(2,1)} %bitcast.246, bf16[256,2048]{1,0:T(8,128)(2,1)} %constant_dynamic-slice_fusion.9.tokens, f32[256,2048]{1,0:T(8,128)} %get-tuple-element.86.hidden, ...), custom_call_target="tpu_custom_call" | custom-call | bytes 209715200 | tf_op jit(solution)/shard_map/output_leg/pallas_call | solution.py:632
  717.6 49.5 %psum.7 = f32[8,544]{1,0:T(8,128)S(1)} all-reduce(f32[8,544]{1,0:T(8,128)S(1)} %pad_maximum_fusion.22), channel_id=1, replica_groups=mesh['dp'=8,'mp'=4] {'dp','mp'}, use_global_device_ids=true, to_apply=%region_17.18 | all-reduce | flops 4352 | bytes 34816 | tf_op jit(solution)/shard_map/psum | solution.py:677
  769.5 2.4 collective-permute-start.10
  774.7 14.2 %collective-permute-done.8 = bf16[256,768]{0,1:T(8,128)(2,1)S(1)} collective-permute-done((bf16[256,768]{0,1:T(8,128)(2,1)S(1)}, bf16[256,768]{0,1:T(8,128)(2,1)S(1)}, u32[]{:S(2)}, u32[]{:S(2)}) %collective-permute-start.8) | collective-permute-done | bytes 393248 | tf_op jit(solution)/shard_map/ppermute | solution.py:427
  790.6 2.4 dynamic-slice_convert_fusion
  793.4 1.8 maximum_select_fusion.10
  796.8 1.8 copy.179
  803.6 7.9 collective-permute-done.9
  (326 shorter events, 93.3 us)
Async XLA Ops:
  7.2 207.8 %all-gather.5.cloned.1.call-start = ((), (), s32[]{:S(2)}) async-start(), calls=%async_computation.3 | async-start | bytes 3932160 | tf_op jit(solution)/shard_map/all_gather | solution.py:444
  8.4 16.8 %copy-start.45 = (f32[256,1536]{1,0:T(8,128)S(1)}, f32[256,1536]{1,0:T(8,128)}, u32[]{:S(2)}) copy-start(f32[256,1536]{1,0:T(8,128)} %param.37) | copy-start | bytes 4718596
  11.9 12.1 %collective-permute-start.2 = (bf16[256,768]{0,1:T(8,128)(2,1)S(1)}, bf16[256,768]{0,1:T(8,128)(2,1)S(1)}, u32[]{:S(2)}, u32[]{:S(2)}) collective-permute-start(bf16[256,768]{0,1:T(8,128)(2,1)S(1)} %pad_maximum_fusion.21), channel_id=1, source_target_pairs={{0,4},{4,0},{8,12},{12,8},{16,20},{20,16},{24,28},{28,24},{1,5},{5... | collective-permute-start | bytes 1179656 | tf_op jit(solution)/shard_map/ppermute | solution.py:427
  25.1 334.1 %all-gather.9.cloned.1.call-start = ((), (), s32[]{:S(2)}) async-start(), calls=%async_computation.5 | async-start | bytes 7864320 | tf_op jit(solution)/shard_map/all_gather | solution.py:444
  27.0 18.8 %collective-permute-start.7 = (bf16[256,1536]{1,0:T(8,128)(2,1)S(1)}, bf16[256,1536]{1,0:T(8,128)(2,1)S(1)}, u32[]{:S(2)}, u32[]{:S(2)}) collective-permute-start(bf16[256,1536]{1,0:T(8,128)(2,1)S(1)} %pad_maximum_fusion.20), channel_id=1, source_target_pairs={{0,4},{4,0},{8,12},{12,8},{16,20},{20,16},{24,28},{28,24},{1,5},{5... | collective-permute-start | bytes 2359304 | tf_op jit(solution)/shard_map/ppermute | solution.py:427
  47.6 330.7 %all-gather.7.cloned.1.call-start = ((), (), s32[]{:S(2)}) async-start(), calls=%async_computation.4 | async-start | bytes 3932160 | tf_op jit(solution)/shard_map/all_gather | solution.py:444
  47.6 4.1 copy-start.39
  49.6 5.0 copy-start.46
  49.6 6.5 copy-start.74
  49.6 6.5 copy-start.75
  49.6 6.5 copy-start.71
  49.6 6.5 copy-start.72
  49.6 134.7 %collective-permute-start = (bf16[512,2048]{1,0:T(8,128)(2,1)S(1)}, bf16[512,2048]{1,0:T(8,128)(2,1)}, u32[]{:S(2)}, u32[]{:S(2)}) collective-permute-start(bf16[512,2048]{1,0:T(8,128)(2,1)S(1)} %constant_dynamic-slice_fusion.17), channel_id=1, source_target_pairs={{0,4},{4,0},{8,12},{12,8},{16,20},{20,16},{24,28},{28,24},{1,5},{5... | collective-permute-start | bytes 6291464 | tf_op jit(solution)/shard_map/ppermute | solution.py:427
  51.1 133.1 %collective-permute-start.3 = (s32[1,1024]{1,0:T(1,128)S(1)}, s32[1,1024]{1,0:T(1,128)S(1)}, u32[]{:S(2)}, u32[]{:S(2)}) collective-permute-start(s32[1,1024]{1,0:T(1,128)S(1)} %copy-done.59), channel_id=1, source_target_pairs={{0,4},{4,0},{8,12},{12,8},{16,20},{20,16},{24,28},{28,24},{1,5},{5... | collective-permute-start | bytes 12296 | tf_op jit(solution)/shard_map/ppermute | solution.py:427
  53.2 135.3 %collective-permute-start.4 = (bf16[512,2048]{1,0:T(8,128)(2,1)}, bf16[512,2048]{1,0:T(8,128)(2,1)}, u32[]{:S(2)}, u32[]{:S(2)}) collective-permute-start(bf16[512,2048]{1,0:T(8,128)(2,1)} %constant_dynamic-slice_fusion.10), channel_id=1, source_target_pairs={{0,4},{4,0},{8,12},{12,8},{16,20},{20,16},{24,28},{28,24},{1,5},{5... | collective-permute-start | bytes 6291464 | tf_op jit(solution)/shard_map/ppermute | solution.py:427
  55.5 144.0 %collective-permute-start.6 = (bf16[256,768]{0,1:T(8,128)(2,1)}, bf16[256,768]{0,1:T(8,128)(2,1)}, u32[]{:S(2)}, u32[]{:S(2)}) collective-permute-start(bf16[256,768]{0,1:T(8,128)(2,1)} %get-tuple-element.182), channel_id=1, source_target_pairs={{0,4},{4,0},{8,12},{12,8},{16,20},{20,16},{24,28},{28,24},{1,5},{5... | collective-permute-start | bytes 1179656 | tf_op jit(solution)/shard_map/ppermute | solution.py:427
  183.5 42.2 %copy-start.60 = (f32[128]{0:T(128)}, f32[128]{0:T(128)S(1)}, u32[]{:S(2)}) copy-start(f32[128]{0:T(128)S(1)} %mul.420) | copy-start | bytes 1540
  184.3 17.6 %collective-permute-start.1 = (bf16[512,2048]{1,0:T(8,128)(2,1)}, bf16[512,2048]{1,0:T(8,128)(2,1)}, u32[]{:S(2)}, u32[]{:S(2)}) collective-permute-start(bf16[512,2048]{1,0:T(8,128)(2,1)} %collective-permute-done), channel_id=1, source_target_pairs={{0,1},{1,0},{2,3},{3,2},{4,5},{5,4},{6,7},{7,6},{8,9},{9,8},{10,11... | collective-permute-start | bytes 6291464 | tf_op jit(solution)/shard_map/ppermute | solution.py:430
  188.4 37.3 %copy-start.28 = (f32[2048,64]{0,1:T(8,128)}, f32[2048,64]{0,1:T(8,128)S(1)}, u32[]{:S(2)}) copy-start(f32[2048,64]{0,1:T(8,128)S(1)} %get-tuple-element.211) | copy-start | bytes 1572868
  188.5 20.4 %collective-permute-start.5 = (bf16[512,2048]{1,0:T(8,128)(2,1)}, bf16[512,2048]{1,0:T(8,128)(2,1)}, u32[]{:S(2)}, u32[]{:S(2)}) collective-permute-start(bf16[512,2048]{1,0:T(8,128)(2,1)} %collective-permute-done.4), channel_id=1, source_target_pairs={{0,1},{1,0},{2,3},{3,2},{4,5},{5,4},{6,7},{7,6},{8,9},{9,8},{10,11... | collective-permute-start | bytes 6291464 | tf_op jit(solution)/shard_map/ppermute | solution.py:430
  194.4 56.7 %copy-start.13 = (f32[2,1024,128]{2,1,0:T(8,128)}, f32[2,1024,128]{2,1,0:T(8,128)S(1)}, u32[]{:S(2)}) copy-start(f32[2,1024,128]{2,1,0:T(8,128)S(1)} %get-tuple-element.228) | copy-start | bytes 3145732
  201.7 566.6 %reduce-scatter.8.cloned.1.call-start = ((), (), s32[]{:S(2)}) async-start(), calls=%async_computation.8 | async-start | bytes 3932160 | tf_op jit(solution)/shard_map/reduce_scatter | solution.py:447
  201.9 4.9 copy-start.15
  208.8 6.2 copy-start.67
  208.8 6.2 copy-start.65
  228.1 3.7 copy-start.36
  228.6 25.6 %copy-start.50 = (bf16[2,512,128]{2,1,0:T(8,128)(2,1)}, bf16[2,512,128]{2,1,0:T(8,128)(2,1)S(1)}, u32[]{:S(2)}) copy-start(bf16[2,512,128]{2,1,0:T(8,128)(2,1)S(1)} %copy.221) | copy-start | bytes 786436
  228.6 35.8 %copy-start.52 = (f32[2048,2]{0,1:T(2,128)}, f32[2048,2]{0,1:T(2,128)S(1)}, u32[]{:S(2)}) copy-start(f32[2048,2]{0,1:T(2,128)S(1)} %add_rsqrt_fusion) | copy-start | bytes 49156
  234.5 6.0 slice-start.2
  246.4 7.8 copy-start.8
  254.2 3.9 copy-start.30
  255.2 9.2 %copy-start.1 = (f32[2,2,512,512]{2,3,1,0:T(8,128)}, f32[2,2,512,512]{2,3,1,0:T(8,128)S(1)}, u32[]{:S(2)}) copy-start(f32[2,2,512,512]{2,3,1,0:T(8,128)S(1)} %get-tuple-element.219) | copy-start | bytes 12582916
  266.3 4.7 copy-start.23
  394.7 19.7 %copy-start.77 = (bf16[2048,768]{0,1:T(8,128)(2,1)}, bf16[2048,768]{0,1:T(8,128)(2,1)S(1)}, u32[]{:S(2)}) copy-start(bf16[2048,768]{0,1:T(8,128)(2,1)S(1)} %get-tuple-element.152) | copy-start | bytes 9437188
  503.8 3.7 copy-start.27
  503.8 6.4 copy-start.25
  503.8 3.8 copy-start.2
  503.8 6.4 slice-start
  510.2 6.9 copy-start.17
  533.3 238.6 %reduce-scatter.4.cloned.1.call-start = ((), (), s32[]{:S(2)}) async-start(), calls=%async_computation.6 | async-start | bytes 3932160 | tf_op jit(solution)/shard_map/reduce_scatter | solution.py:447
  549.7 4.0 copy-start.19
  553.7 3.9 copy-start.6
  564.6 7.8 copy-start.14
  564.6 7.8 copy-start.53
  564.6 7.8 copy-start.64
  572.4 4.3 copy-start.4
  572.4 4.8 copy-start.21
  572.4 5.4 copy-start.22
  572.4 5.6 copy-start.34
  572.4 5.6 copy-start.70
  572.4 12.3 %slice-start.3 = ((s8[8388608]{0:T(1024)(128)(4,1)}), s8[4194304]{0:T(1024)(128)(4,1)S(1)}, s32[]{:S(2)}) async-start(s8[8388608]{0:T(1024)(128)(4,1)} %bitcast.279), calls=%async_computation.12 | async-start | bytes 8388608
  578.0 4.5 copy-start.32
  578.0 4.5 copy-start.40
  578.0 6.7 slice-start.4
  585.2 3.6 copy-start.55
  585.2 3.6 copy-start.66
  595.5 195.2 %reduce-scatter.6.cloned.1.call-start = ((), (), s32[]{:S(2)}) async-start(), calls=%async_computation.7 | async-start | bytes 7864320 | tf_op jit(solution)/shard_map/reduce_scatter | solution.py:447
  616.3 8.6 %copy-start.73 = (bf16[2048,768]{0,1:T(8,128)(2,1)S(1)}, bf16[2048,768]{0,1:T(8,128)(2,1)}, u32[]{:S(2)}) copy-start(bf16[2048,768]{0,1:T(8,128)(2,1)} %all-gather.7.cloned.1.call-done) | copy-start | bytes 9437188
  616.3 8.6 %copy-start.76 = (bf16[2048,768]{0,1:T(8,128)(2,1)S(1)}, bf16[2048,768]{0,1:T(8,128)(2,1)}, u32[]{:S(2)}) copy-start(bf16[2048,768]{0,1:T(8,128)(2,1)} %get-tuple-element.154) | copy-start | bytes 9437188
  634.2 82.6 %copy-start.69 = (f32[1,2048]{1,0:T(1,128)S(1)}, f32[1,2048]{1,0:T(1,128)}, u32[]{:S(2)}) copy-start(f32[1,2048]{1,0:T(1,128)} %get-tuple-element.92) | copy-start | bytes 24580
  769.5 20.8 %collective-permute-start.10 = (bf16[256,768]{1,0:T(8,128)(2,1)S(1)}, bf16[256,768]{1,0:T(8,128)(2,1)S(1)}, u32[]{:S(2)}, u32[]{:S(2)}) collective-permute-start(bf16[256,768]{1,0:T(8,128)(2,1)S(1)} %get-tuple-element.172), channel_id=1, source_target_pairs={{0,4},{4,0},{8,12},{12,8},{16,20},{20,16},{24,28},{28,24},{1,5},{5... | collective-permute-start | bytes 1179656 | tf_op jit(solution)/shard_map/ppermute | solution.py:427
  773.1 15.8 %collective-permute-start.8 = (bf16[256,768]{0,1:T(8,128)(2,1)S(1)}, bf16[256,768]{0,1:T(8,128)(2,1)S(1)}, u32[]{:S(2)}, u32[]{:S(2)}) collective-permute-start(bf16[256,768]{0,1:T(8,128)(2,1)S(1)} %get-tuple-element.180), channel_id=1, source_target_pairs={{0,4},{4,0},{8,12},{12,8},{16,20},{20,16},{24,28},{28,24},{1,5},{5... | collective-permute-start | bytes 1179656 | tf_op jit(solution)/shard_map/ppermute | solution.py:427
  793.1 18.4 %collective-permute-start.9 = (bf16[256,1536]{1,0:T(8,128)(2,1)}, bf16[256,1536]{1,0:T(8,128)(2,1)}, u32[]{:S(2)}, u32[]{:S(2)}) collective-permute-start(bf16[256,1536]{1,0:T(8,128)(2,1)} %get-tuple-element.164), channel_id=1, source_target_pairs={{0,4},{4,0},{8,12},{12,8},{16,20},{20,16},{24,28},{28,24},{1,5},{5... | collective-permute-start | bytes 2359304 | tf_op jit(solution)/shard_map/ppermute | solution.py:427
  796.8 5.8 copy-start.49
  (36 other events, 75.7 us)
Sparse Core Ops, SparseCore 0:
  25.3 64.9 all-gather.4
  92.4 114.0 all-gather.8
  208.1 61.9 all-gather.6
  533.5 59.6 reduce-scatter.7
  595.6 59.9 reduce-scatter.3
  657.8 111.8 reduce-scatter.5

commit v2 on v1

--- a/solution.py
+++ b/solution.py
@@ -28,18 +28,8 @@
     sine_table = jnp.sin(angles)
     return (
         jnp.concatenate([cosine_table, cosine_table], -1),
-        jnp.concatenate([sine_table, sine_table], -1),
-    )
-
-
-def rotate(values):
-    middle = values.shape[-1] // 2
-    return jnp.concatenate([-values[..., middle:], values[..., :middle]], -1)
-
-
-def rotate_back(values):
-    middle = values.shape[-1] // 2
-    return jnp.concatenate([values[..., middle:], -values[..., :middle]], -1)
+        jnp.concatenate([-sine_table, sine_table], -1),
+    )
 
 
 def norm_parts(values):
@@ -380,14 +370,320 @@
     )
 
 
-def scores_of(queries, keys, doc_rows, start, factor):
-    scores = jnp.einsum("sqrd,skd->srqk", queries, keys, preferred_element_type=F32) * factor
-    query_index = start + jnp.arange(queries.shape[1])
-    key_index = jnp.arange(keys.shape[1])
-    allowed = (doc_rows[:, start : start + queries.shape[1], None] == doc_rows[:, None, : keys.shape[1]]) & (
-        key_index[None, None, :] <= query_index[None, :, None]
-    )
-    return jnp.where(allowed[:, None], scores, MASKED)
+def prepare(q, k, v, o, gain, docs, pack, gains, docs_other, stage, swap, send, recv):
+    dp, mp = lax.axis_index("dp"), lax.axis_index("mp")
+    n_dp = gains.shape[0]
+    y, y_peer = dp % 2, (dp + 1 - 2 * (dp % 2), mp)
+    rows = q.shape[0]
+
+    def peer(j):
+        return (lax.rem(dp + j, n_dp), mp)
+
+    barrier = pltpu.get_barrier_semaphore()
+
+    def greet(j, carry):
+        pl.semaphore_signal(barrier, inc=1, device_id=peer(j), device_id_type=MESH)
+        return carry
+
+    lax.fori_loop(1, n_dp, greet, 0)
+    widths = [w.shape[1] // 2 for w in (q, k, v)]
+    first = sum(widths)
+
+    def fill_inputs(target, row, which):
+        at = 0
+        for w, size in zip((q, k, v), widths):
+            cols = pl.ds(pl.multiple_of(which * size, 128), size)
+            target[pl.ds(row, rows), at : at + size] = w[:, cols].astype(BF16)
+            at += size
+
+    def fill_output(target, row, which):
+        size = o.shape[0] // 2
+        part = o[pl.ds(pl.multiple_of(which * size, 128), size), :].astype(BF16)
+        target[pl.ds(row, rows), first : first + size] = part.T
+
+    mine = pl.multiple_of(y * rows, rows)
+
+    def swapped(i):
+        cols = pl.ds(0, first) if i == 0 else pl.ds(first, o.shape[0] // 2)
+        target = pack.at[pl.ds(mine, rows), cols]
+        return remote(stage.at[:, cols], target, swap.at[0, i], swap.at[1, i], y_peer)
+
+    fill_inputs(stage, 0, 1 - y)
+    pl.semaphore_wait(barrier, n_dp - 1)
+    swapped(0).start()
+    fill_output(stage, 0, 1 - y)
+    swapped(1).start()
+    docs_swapped = remote(docs, docs_other, swap.at[0, 2], swap.at[1, 2], y_peer)
+    docs_swapped.start()
+
+    def gain_to(j):
+        return remote(gain, gains.at[dp], send.at[j], recv.at[j], peer(j))
+
+    def share(j, carry):
+        gain_to(j).start()
+        return carry
+
+    lax.fori_loop(1, n_dp, share, 0)
+    gains[dp] = gain[...]
+    fill_inputs(pack, mine, y)
+    fill_output(pack, mine, y)
+
+    def settle(j, carry):
+        gain_to(j).wait()
+        return carry
+
+    lax.fori_loop(1, n_dp, settle, 0)
+    docs_swapped.wait()
+    swapped(0).wait()
+    swapped(1).wait()
+
+
+class Spread:
+    STAGES = 4
+
+    def __init__(self, mine, other, send, recv):
+        self.refs = (mine, other, send, recv)
+        self.rows = mine.shape[0] // 4 // CHUNKS
+
+    @staticmethod
+    def scratch():
+        return [
+            pltpu.SemaphoreType.DMA((Spread.STAGES, CHUNKS)),
+            pltpu.SemaphoreType.DMA((Spread.STAGES, CHUNKS)),
+        ]
+
+    def copy(self, k, i):
+        mine, other, send, recv = self.refs
+        x, c, core_peer, x_peer, y_peer = neighbours()
+
+        def rows(at_x):
+            start = (at_x * 2 + c) * (mine.shape[0] // 4) + k * self.rows
+            return pl.ds(pl.multiple_of(start, self.rows), self.rows)
+
+        at = rows(1 - x) if i == 3 else rows(x)
+        peer = (y_peer, x_peer, core_peer, core_peer)[i]
+        source = mine if i == 0 else other
+        return remote(source.at[at], other.at[at], send.at[i, k], recv.at[i, k], peer)
+
+    def pass_on(self, k):
+        self.copy(k, 0).wait_recv()
+        self.copy(k, 1).start()
+        self.copy(k, 2).start()
+
+    def pass_last(self, k):
+        self.copy(k, 1).wait_recv()
+        self.copy(k, 3).start()
+
+    def finish(self):
+        for k in range(CHUNKS):
+            for i in (2, 3):
+                self.copy(k, i).wait_recv()
+            for i in range(4):
+                self.copy(k, i).wait_send()
+
+
+def spread(tokens, gate_up_send, down_send, tokens_other, gate_up, down, send, recv, *scratch):
+    rows = Spread(tokens, tokens_other, *scratch)
+    y_peer = neighbours()[4]
+    sent = [
+        remote(gate_up_send, gate_up, send.at[0], recv.at[0], y_peer),
+        remote(down_send, down, send.at[1], recv.at[1], y_peer),
+    ]
+    enter(neighbours()[2:])
+    for k in range(CHUNKS):
+        rows.copy(k, 0).start()
+    for k in range(CHUNKS):
+        rows.pass_on(k)
+        sent[k % 2].start()
+    for k in range(CHUNKS):
+        rows.pass_last(k)
+    rows.finish()
+    for i in range(2):
+        sent[i].wait()
+
+
+def sum_gains(parts, total, got, mid, others, send, recv, send_mp, recv_mp):
+    dp, mp = lax.axis_index("dp"), lax.axis_index("mp")
+    n_dp, n_mp = parts.shape[0], others.shape[0] + 1
+    barrier = pltpu.get_barrier_semaphore()
+
+    def across(j):
+        return (lax.rem(dp + j, n_dp), mp)
+
+    def along(j):
+        return (dp, lax.rem(mp + j, n_mp))
+
+    def greet(j, carry):
+        pl.semaphore_signal(barrier, inc=1, device_id=across(j), device_id_type=MESH)
+        return carry
+
+    lax.fori_loop(1, n_dp, greet, 0)
+    for j in range(1, n_mp):
+        pl.semaphore_signal(barrier, inc=1, device_id=along(j), device_id_type=MESH)
+    pl.semaphore_wait(barrier, n_dp + n_mp - 2)
+
+    def first(j):
+        slot = lax.rem(dp + j, n_dp)
+        return remote(parts.at[slot], got.at[j], send.at[j], recv.at[j], across(j))
+
+    def start(j, carry):
+        first(j).start()
+        return carry
+
+    lax.fori_loop(1, n_dp, start, 0)
+    mid[...] = parts[dp]
+
+    def add(j, carry):
+        first(j).wait()
+        mid[...] += got[j]
+        return carry
+
+    lax.fori_loop(1, n_dp, add, 0)
+
+    def second(j):
+        return remote(mid, others.at[j - 1], send_mp.at[j], recv_mp.at[j], along(j))
+
+    for j in range(1, n_mp):
+        second(j).start()
+    result = mid[...]
+    for j in range(1, n_mp):
+        second(j).wait()
+        result += others[j - 1]
+    total[...] = result
+
+
+def finish_attention(grads, q, k, v, o, other, send, recv):
+    dp, mp = lax.axis_index("dp"), lax.axis_index("mp")
+    y, y_peer = dp % 2, (dp + 1 - 2 * (dp % 2), mp)
+    rows = q.shape[0]
+    enter([y_peer])
+    theirs = pl.multiple_of((1 - y) * rows, rows)
+    swapped = remote(grads.at[pl.ds(theirs, rows)], other, send, recv, y_peer)
+    swapped.start()
+
+    def place(source, row, which):
+        at = 0
+        for w in (q, k, v):
+            size = w.shape[1] // 2
+            cols = pl.ds(pl.multiple_of(which * size, 128), size)
+            w[:, cols] = source[pl.ds(row, rows), at : at + size].astype(F32)
+            at += size
+        size = o.shape[0] // 2
+        part = source[pl.ds(row, rows), at : at + size].astype(F32).T
+        o[pl.ds(pl.multiple_of(which * size, 128), size), :] = part
+
+    place(grads, pl.multiple_of(y * rows, rows), y)
+    swapped.wait_recv()
+    place(other, 0, 1 - y)
+    swapped.wait_send()
+
+
+QUERY_BLOCK = 256
+LONGEST = 512
+
+
+def rolled(values):
+    return pltpu.roll(values, HEAD_WIDTH // 2, 1)
+
+
+def head_norm(raw, h):
+    return norm_parts(raw[:, h * HEAD_WIDTH : (h + 1) * HEAD_WIDTH])
+
+
+def rope_into(target, at, normed, cosine, sine):
+    target[:, at : at + HEAD_WIDTH] = (normed * cosine[...] + rolled(normed) * sine[...]).astype(
+        BF16
+    )
+
+
+def blocks_of(length):
+    for start in range(0, length, QUERY_BLOCK):
+        first = max(0, start - LONGEST)
+        yield slice(start, start + QUERY_BLOCK), slice(first, start + QUERY_BLOCK)
+
+
+def weights_of(query, key, starts, rows, cols):
+    scores = dot(query, key, 1, 1) * HEAD_WIDTH ** (-0.5)
+    query_index = rows.start + lax.broadcasted_iota(jnp.int32, scores.shape, 0)
+    key_index = cols.start + lax.broadcasted_iota(jnp.int32, scores.shape, 1)
+    allowed = (key_index <= query_index) & (key_index >= starts[rows])
+    scores = jnp.where(allowed, scores, MASKED)
+    exponent = jnp.exp(scores - jnp.max(scores, -1, keepdims=True))
+    return exponent / jnp.sum(exponent, -1, keepdims=True)
+
+
+def attend_forward(raw, cosine, sine, starts, gain_query, gain_key, out, q, k):
+    for h in range(GROUP):
+        rope_into(q, h * HEAD_WIDTH, head_norm(raw, h)[0] * gain_query[...], cosine, sine)
+    rope_into(k, 0, head_norm(raw, GROUP)[0] * gain_key[...], cosine, sine)
+    at = (GROUP + 1) * HEAD_WIDTH
+    for rows, cols in blocks_of(raw.shape[0]):
+        for h in range(GROUP):
+            lanes = slice(h * HEAD_WIDTH, (h + 1) * HEAD_WIDTH)
+            weights = weights_of(q[rows, lanes], k[cols], starts, rows, cols).astype(BF16)
+            value = raw[cols, at : at + HEAD_WIDTH].astype(BF16)
+            out[rows, lanes] = dot(weights, value).astype(BF16)
+
+
+def attend_backward(
+    raw, cosine, sine, starts, gain_query, gain_key, grad, out, gains, q, k, v, dq, dk, dv
+):
+    factor = HEAD_WIDTH ** (-0.5)
+    at = (GROUP + 1) * HEAD_WIDTH
+    for h in range(GROUP):
+        rope_into(q, h * HEAD_WIDTH, head_norm(raw, h)[0] * gain_query[...], cosine, sine)
+    rope_into(k, 0, head_norm(raw, GROUP)[0] * gain_key[...], cosine, sine)
+    v[...] = raw[:, at : at + HEAD_WIDTH].astype(BF16)
+    dk[...] = jnp.zeros_like(dk)
+    dv[...] = jnp.zeros_like(dv)
+    for rows, cols in blocks_of(raw.shape[0]):
+        for h in range(GROUP):
+            lanes = slice(h * HEAD_WIDTH, (h + 1) * HEAD_WIDTH)
+            weights = weights_of(q[rows, lanes], k[cols], starts, rows, cols)
+            grad_weights = dot(grad[rows, lanes], v[cols], 1, 1)
+            inner = jnp.sum(weights * grad_weights, -1, keepdims=True)
+            grad_scores = (weights * (grad_weights - inner)).astype(BF16)
+            dq[rows, lanes] = dot(grad_scores, k[cols]) * factor
+            dk[cols] += dot(grad_scores, q[rows, lanes], 0, 0) * factor
+            dv[cols] += dot(weights.astype(BF16), grad[rows, lanes], 0, 0)
+    gains[...] = jnp.zeros_like(gains)
+
+    def undo(rot_grad, h, gain, row):
+        normed_grad = rot_grad * cosine[...] - rolled(rot_grad) * sine[...]
+        hat, inv = head_norm(raw, h)
+        gains[0, row : row + 1] += jnp.sum(normed_grad * hat, 0, keepdims=True)
+        lanes = slice(h * HEAD_WIDTH, (h + 1) * HEAD_WIDTH)
+        out[:, lanes] = norm_back(normed_grad, hat, inv, gain[...]).astype(BF16)
+
+    for h in range(GROUP):
+        undo(dq[:, h * HEAD_WIDTH : (h + 1) * HEAD_WIDTH], h, gain_query, 0)
+    undo(dk[...], GROUP, gain_key, 1)
+    out[:, at : at + HEAD_WIDTH] = dv[...].astype(BF16)
+
+
+def call_attention(kernel, length, rows, out_shape, out_specs, scratch, flops):
+    def seq(cols):
+        return pl.BlockSpec((length, cols), lambda i: (i, 0))
+
+    gain = pl.BlockSpec((1, HEAD_WIDTH), lambda i: (0, 0))
+    specs = [seq((GROUP + 2) * HEAD_WIDTH), seq(HEAD_WIDTH), seq(HEAD_WIDTH), seq(1), gain, gain]
+    if len(scratch) > 2:
+        specs.append(seq(GROUP * HEAD_WIDTH))
+    return pl.pallas_call(
+        kernel,
+        out_shape=out_shape,
+        grid=(rows // length,),
+        in_specs=specs,
+        out_specs=out_specs,
+        scratch_shapes=scratch,
+        name=kernel.__name__,
+        cost_estimate=pl.CostEstimate(
+            flops=flops, bytes_accessed=8 * MIB, transcendentals=rows * length * GROUP // 2
+        ),
+        compiler_params=pltpu.CompilerParams(
+            dimension_semantics=("arbitrary",), vmem_limit_bytes=56 * MIB
+        ),
+    )
 
 
 def on_device(
@@ -408,14 +704,13 @@
 ):
     n_dp = lax.axis_size("dp")
     dp, mp = lax.axis_index("dp"), lax.axis_index("mp")
-    y, core = dp % 2, mp % 2
+    y = dp % 2
     slabs = [[i + 2 * k for k in range(n_dp // 2)] for i in range(2)]
     rows, width = tokens.shape
     seq_length = documents.shape[1]
     seqs = 2 * documents.shape[0]
     share = rows // 4
     head = HEAD_WIDTH
-    factor = head ** (-0.5)
     query_cols, key_cols, hidden_cols = (
         query_weight.shape[1] // 2,
         key_projection.shape[1] // 2,
@@ -426,8 +721,8 @@
     def y_swap(values):
         return lax.ppermute(values, "dp", [(i, i ^ 1) for i in range(n_dp)])
 
-    def core_swap(values):
-        return lax.ppermute(values, "mp", [(i, i ^ 1) for i in range(4)])
+    def mp_swap(values, bit):
+        return lax.ppermute(values, "mp", [(i, i ^ bit) for i in range(4)])
 
     def in_order(where, mine, other, axis):
         return jnp.where(
@@ -448,15 +743,53 @@
             values, "dp", scatter_dimension=0, tiled=True, axis_index_groups=slabs
         )
 
-    attn_low = [w.astype(BF16) for w in (query_weight, key_projection, value_projection)]
-    output_low = output_weight.astype(BF16)
-
-    def attn_pack(which):
-        return jnp.concatenate(
-            [half(w, which, 1) for w in attn_low] + [half(output_low, which, 0).T], 1
+    n_gain, n_head = attn_gain.shape[0], query_gain.shape[0]
+
+    def gain_rows(*parts):
+        lead = parts[0].shape[:-1]
+        pad = [(0, 0)] * len(lead)
+        rows_of = jnp.concatenate(
+            [
+                jnp.pad(part, pad + [(0, -part.shape[-1] % 128)]).reshape(*lead, -1, 128)
+                for part in parts
+            ],
+            -2,
         )
-
-    attn_mine = in_order(y, attn_pack(y), y_swap(attn_pack(1 - y)), 0)
+        return jnp.pad(rows_of, pad + [(0, 8 - rows_of.shape[-2]), (0, 0)])
+
+    def gain_parts_of(rows_of):
+        lead, parts, at = rows_of.shape[:-2], [], 0
+        for size in (n_gain, n_gain, n_head, n_head):
+            n = -(-size // 128)
+            part = rows_of[..., at : at + n, :].reshape(*lead, n * 128)
+            parts.append(part[..., :size])
+            at += n
+        return parts
+
+    my_gains = gain_rows(
+        *(g.astype(BF16).astype(F32) for g in (attn_gain, mlp_gain, query_gain, key_norm_scale))
+    )
+    model_rows = query_weight.shape[0]
+    pack_cols = attn_cols + query_cols
+    attn_mine, gains, docs_other = call_leg(
+        prepare,
+        3,
+        "prepare",
+        [VM] * 6,
+        (
+            jax.ShapeDtypeStruct((2 * model_rows, pack_cols), BF16),
+            jax.ShapeDtypeStruct((n_dp, 8, 128), F32),
+            jax.ShapeDtypeStruct(documents.shape, jnp.int32),
+        ),
+        (VM, VM, VM),
+        [
+            pltpu.VMEM((model_rows, pack_cols), BF16),
+            pltpu.SemaphoreType.DMA((2, 3)),
+            pltpu.SemaphoreType.DMA((n_dp,)),
+            pltpu.SemaphoreType.DMA((n_dp,)),
+        ],
+        3 * MIB,
+    )(query_weight, key_projection, value_projection, output_weight, my_gains, documents)
     attn_full = slab_gather(attn_mine)
 
     mlp_low = [w.astype(BF16) for w in (gate_weight, up_weight)]
@@ -465,71 +798,58 @@
     def mlp_pack(which):
         return jnp.concatenate([half(w, which, 1) for w in mlp_low], 1)
 
-    mlp_mine = in_order(y, mlp_pack(y), y_swap(mlp_pack(1 - y)), 0)
-    down_mine = in_order(y, half(down_low, y, 0).T, y_swap(half(down_low, 1 - y, 0).T), 0)
+    pair_rows = 2 * rows
+    tokens_other, mlp_got, down_got = call_leg(
+        spread,
+        6,
+        "spread",
+        [ANY] * 3,
+        (
+            jax.ShapeDtypeStruct((rows, width), BF16),
+            jax.ShapeDtypeStruct((model_rows, 2 * hidden_cols), BF16),
+            jax.ShapeDtypeStruct((model_rows, hidden_cols), BF16),
+        ),
+        (ANY,) * 3,
+        [pltpu.SemaphoreType.DMA((2,))] * 2 + Spread.scratch(),
+        150 * MIB,
+    )(tokens, mlp_pack(1 - y), half(down_low, 1 - y, 0).T)
+    mlp_mine = in_order(y, mlp_pack(y), mlp_got, 0)
+    down_mine = in_order(y, half(down_low, y, 0).T, down_got, 0)
+    tokens_pair = jnp.concatenate([tokens, tokens_other], 0)
+
+    cot_part = lax.dynamic_slice_in_dim(cotangent, mp * share, share, 0)
+    cot_part, _ = lax.optimization_barrier((cot_part, tokens_other))
+    cot_part = y_swap(cot_part)
     gate_up_full = slab_gather(mlp_mine)
     down_full = slab_gather(down_mine)
-
-    gains = lax.all_gather(
-        jnp.concatenate(
-            [
-                g.astype(BF16).reshape(1, -1)
-                for g in (attn_gain, mlp_gain, query_gain, key_norm_scale)
-            ],
-            1,
-        ),
-        "dp",
-        axis=0,
-        tiled=True,
-    ).astype(F32)
-    n_gain, n_head = attn_gain.shape[0], query_gain.shape[0]
-    gain_one = gains[:, :n_gain].reshape(1, width)
-    gain_two = gains[:, n_gain : 2 * n_gain].reshape(1, width)
-    gain_query = gains[:, 2 * n_gain : 2 * n_gain + n_head].reshape(head)
-    gain_key = gains[:, 2 * n_gain + n_head :].reshape(head)
-
-    def partner_rows(values):
-        got = y_swap(half(values, core, 0))
-        return in_order(core, got, core_swap(got), 0)
-
-    tokens_pair = jnp.concatenate([tokens, partner_rows(tokens)], 0)
-    cot_pair = jnp.concatenate([cotangent, partner_rows(cotangent)], 0)
-    docs = jnp.concatenate([documents, y_swap(documents)], 0)
-    pair_rows = 2 * rows
+    gain_one, gain_two, gain_query, gain_key = (g.reshape(1, -1) for g in gain_parts_of(gains))
+    docs = jnp.concatenate([documents, docs_other], 0)
     tokens_share = lax.dynamic_slice_in_dim(tokens, mp * share, share, 0)
     cot_share = lax.dynamic_slice_in_dim(cotangent, mp * share, share, 0)
 
     inputs = tokens_pair.astype(F32)
     normed_one = (norm_parts(inputs)[0] * gain_one).astype(BF16)
     raw = dot(normed_one, attn_full[:, :attn_cols])
-    query_raw, key_raw = raw[:, :query_cols], raw[:, query_cols : query_cols + key_cols]
-    values = raw[:, query_cols + key_cols :].astype(BF16)
     starts = sum((docs < i).sum(1, keepdims=True) * (docs == i) for i in range(1, 4))
     positions = (jnp.arange(seq_length, dtype=jnp.int32)[None] - starts).reshape(pair_rows)
     cosine, sine = rope_tables(positions, head)
-    cosine, sine = cosine[:, None, :], sine[:, None, :]
-    query_hat, query_inv = norm_parts(query_raw.reshape(pair_rows, GROUP, head))
-    key_hat, key_inv = norm_parts(key_raw.reshape(pair_rows, 1, head))
-    query_normed, key_normed = query_hat * gain_query, key_hat * gain_key
-    queries = (query_normed * cosine + rotate(query_normed) * sine).astype(BF16)
-    keys = (key_normed * cosine + rotate(key_normed) * sine).astype(BF16)
-    queries = queries.reshape(seqs, seq_length, GROUP, head)
-    keys = keys.reshape(seqs, seq_length, head)
-    values = values.reshape(seqs, seq_length, head)
-    block = min(512, seq_length)
-    outputs, log_totals = [], []
-    for start in range(0, seq_length, block):
-        end = start + block
-        scores = scores_of(queries[:, start:end], keys[:, :end], docs, start, factor)
-        highest = jnp.max(scores, -1, keepdims=True)
-        exponent = jnp.exp(scores - highest)
-        totals = jnp.sum(exponent, -1, keepdims=True)
-        weights = (exponent / totals).astype(BF16)
-        outputs.append(
-            jnp.einsum("srqk,skd->sqrd", weights, values[:, :end], preferred_element_type=F32)
-        )
-        log_totals.append(highest + jnp.log(totals))
-    attended = jnp.concatenate(outputs, 1).reshape(pair_rows, GROUP * head).astype(BF16)
+    starts = starts.reshape(pair_rows, 1).astype(jnp.int32)
+    raw, cot_part = lax.optimization_barrier((raw, cot_part))
+    cot_pieces = in_order(mp // 2, cot_part[None], mp_swap(cot_part, 2)[None], 0)
+    attention_args = (raw, cosine, sine, starts, gain_query, gain_key)
+    pair_flops = pair_rows * seq_length * query_cols
+    attended = call_attention(
+        attend_forward,
+        seq_length,
+        pair_rows,
+        jax.ShapeDtypeStruct((pair_rows, query_cols), BF16),
+        pl.BlockSpec((seq_length, query_cols), lambda i: (i, 0)),
+        [pltpu.VMEM((seq_length, query_cols), BF16), pltpu.VMEM((seq_length, head), BF16)],
+        2 * pair_flops,
+    )(*attention_args)
+    attended, cot_pieces = lax.optimization_barrier((attended, cot_pieces))
+    cot_pieces = in_order(mp % 2, cot_pieces[:, None], mp_swap(cot_pieces, 1)[:, None], 1)
+    cot_pair = jnp.concatenate([cotangent, cot_pieces.reshape(rows, width)], 0)
     out_mat = attn_full[:, attn_cols:]
     attn_part = dot(attended, out_mat, 1, 1).astype(BF16)
 
@@ -552,13 +872,17 @@
     sigmoid = jax.nn.sigmoid(gate_pre)
     swish = gate_pre * sigmoid
     active = (swish * up_pre).astype(BF16)
-    down_grad = slab_scatter(dot(cot_pair, active, 0, 0).astype(BF16))
+    down_part = dot(cot_pair, active, 0, 0).astype(BF16)
+    down_grad = slab_scatter(down_part)
     mlp_part = dot(active, down_full, 1, 1).astype(BF16)
-    grad_active = dot(cot_pair, down_full)
+    cot_late, _ = lax.optimization_barrier((cot_pair, down_part))
+    grad_active = dot(cot_late, down_full)
     grad_gate = (grad_active * up_pre * sigmoid * (1.0 + gate_pre * (1.0 - sigmoid))).astype(BF16)
     grad_up = (grad_active * swish).astype(BF16)
     grad_gate_up = jnp.concatenate([grad_gate, grad_up], 1)
-    gate_up_grad = slab_scatter(dot(normed_two, grad_gate_up, 0, 0).astype(BF16))
+    gate_up_part = dot(normed_two, grad_gate_up, 0, 0).astype(BF16)
+    gate_up_grad = slab_scatter(gate_up_part)
+    grad_gate_up, _, _ = lax.optimization_barrier((grad_gate_up, gate_up_part, down_part))
     normed_two_part = dot(grad_gate_up, gate_up_full, 1, 1).astype(BF16)
 
     grad_hidden, mlp_gain_part, grad_hidden_low = call_leg(
@@ -579,54 +903,34 @@
 
     output_grad = dot(grad_hidden_low, attended, 0, 0).astype(BF16)
     grad_attended = dot(grad_hidden_low, out_mat).astype(BF16)
-    grad_attended = grad_attended.reshape(seqs, seq_length, GROUP, head)
-    query_grads = []
-    key_rot_grad = jnp.zeros((seqs, seq_length, head), F32)
-    value_grad = jnp.zeros((seqs, seq_length, head), F32)
-    for i, start in enumerate(range(0, seq_length, block)):
-        end = start + block
-        block_queries, block_grad = queries[:, start:end], grad_attended[:, start:end]
-        scores = scores_of(block_queries, keys[:, :end], docs, start, factor)
-        weights = jnp.exp(scores - log_totals[i])
-        grad_weights = jnp.einsum(
-            "sqrd,skd->srqk", block_grad, values[:, :end], preferred_element_type=F32
-        )
-        inner = jnp.sum(weights * grad_weights, -1, keepdims=True)
-        grad_scores = (weights * (grad_weights - inner)).astype(BF16)
-        query_grads.append(
-            jnp.einsum("srqk,skd->sqrd", grad_scores, keys[:, :end], preferred_element_type=F32)
-            * factor
-        )
-        key_rot_grad = key_rot_grad.at[:, :end].add(
-            jnp.einsum("srqk,sqrd->skd", grad_scores, block_queries, preferred_element_type=F32)
-            * factor
-        )
-        value_grad = value_grad.at[:, :end].add(
-            jnp.einsum(
-                "srqk,sqrd->skd", weights.astype(BF16), block_grad, preferred_element_type=F32
-            )
-        )
-    query_rot_grad = jnp.concatenate(query_grads, 1).reshape(pair_rows, GROUP, head)
-    key_rot_grad = key_rot_grad.reshape(pair_rows, 1, head)
-    query_norm_grad = query_rot_grad * cosine + rotate_back(query_rot_grad * sine)
-    key_norm_grad = key_rot_grad * cosine + rotate_back(key_rot_grad * sine)
-    query_gain_part = jnp.sum(query_norm_grad * query_hat, (0, 1))
-    key_gain_part = jnp.sum(key_norm_grad * key_hat, (0, 1))
-    raw_grad = jnp.concatenate(
+    raw_grad, head_gain_parts = call_attention(
+        attend_backward,
+        seq_length,
+        pair_rows,
+        (
+            jax.ShapeDtypeStruct((pair_rows, attn_cols), BF16),
+            jax.ShapeDtypeStruct((seqs, 8, head), F32),
+        ),
+        (
+            pl.BlockSpec((seq_length, attn_cols), lambda i: (i, 0)),
+            pl.BlockSpec((1, 8, head), lambda i: (i, 0, 0)),
+        ),
         [
-            norm_back(query_norm_grad, query_hat, query_inv, gain_query)
-            .reshape(pair_rows, query_cols)
-            .astype(BF16),
-            norm_back(key_norm_grad, key_hat, key_inv, gain_key)
-            .reshape(pair_rows, key_cols)
-            .astype(BF16),
-            value_grad.reshape(pair_rows, key_cols).astype(BF16),
+            pltpu.VMEM((seq_length, query_cols), BF16),
+            pltpu.VMEM((seq_length, head), BF16),
+            pltpu.VMEM((seq_length, head), BF16),
+            pltpu.VMEM((seq_length, query_cols), F32),
+            pltpu.VMEM((seq_length, head), F32),
+            pltpu.VMEM((seq_length, head), F32),
         ],
-        1,
-    )
-    attn_grad = slab_scatter(
-        jnp.concatenate([dot(normed_one, raw_grad, 0, 0).astype(BF16), output_grad], 1)
-    )
+        5 * pair_flops,
+    )(*attention_args, grad_attended)
+    head_gain_parts = head_gain_parts.sum(0)
+    attn_grad = jnp.concatenate([dot(normed_one, raw_grad, 0, 0).astype(BF16), output_grad], 1)
+    attn_grad, gate_up_grad, down_grad = lax.optimization_barrier(
+        (attn_grad, gate_up_grad, down_grad)
+    )
+    attn_grad = slab_scatter(attn_grad)
     normed_one_part = dot(raw_grad, attn_full[:, :attn_cols], 1, 1).astype(BF16)
 
     input_grad, layer_output, attn_gain_part = call_leg(
@@ -655,7 +959,23 @@
         other = y_swap(half(values, 1 - y, 0)).astype(F32)
         return half(values, y, 0).astype(F32), other
 
-    attn_own, attn_other = back(attn_grad)
+    query_grad, key_grad, value_grad, output_grad = call_leg(
+        finish_attention,
+        5,
+        "finish_attention",
+        [VM],
+        tuple(
+            jax.ShapeDtypeStruct(w.shape, F32)
+            for w in (query_weight, key_projection, value_projection, output_weight)
+        ),
+        (VM,) * 4,
+        [
+            pltpu.VMEM((model_rows, pack_cols), BF16),
+            pltpu.SemaphoreType.DMA,
+            pltpu.SemaphoreType.DMA,
+        ],
+        3 * MIB,
+    )(attn_grad)
     gate_up_own, gate_up_other = back(gate_up_grad)
     down_own, down_other = back(down_grad)
 
@@ -665,28 +985,42 @@
             own, other = own.T, other.T
         return in_order(y, own, other, axis)
 
-    gain_parts = jnp.concatenate(
+    gain_parts = gain_rows(
+        attn_gain_part.reshape(-1, n_gain),
+        mlp_gain_part.reshape(-1, n_gain),
+        head_gain_parts[0].reshape(-1, n_head),
+        head_gain_parts[1].reshape(-1, n_head),
+    )
+    gain_sums = call_leg(
+        sum_gains,
+        4,
+        "sum_gains",
+        [VM],
+        jax.ShapeDtypeStruct((8, 128), F32),
+        VM,
         [
-            attn_gain_part.reshape(-1, n_gain),
-            mlp_gain_part.reshape(-1, n_gain),
-            query_gain_part.reshape(-1, n_head),
-            key_gain_part.reshape(-1, n_head),
+            pltpu.VMEM((n_dp, 8, 128), F32),
+            pltpu.VMEM((8, 128), F32),
+            pltpu.VMEM((3, 8, 128), F32),
+            pltpu.SemaphoreType.DMA((n_dp,)),
+            pltpu.SemaphoreType.DMA((n_dp,)),
+            pltpu.SemaphoreType.DMA((4,)),
+            pltpu.SemaphoreType.DMA((4,)),
         ],
-        1,
-    )
-    gain_sums = lax.psum(gain_parts, ("dp", "mp"))
-    gain_sums = lax.dynamic_slice_in_dim(gain_sums, dp, 1, 0)[0]
+        1 * MIB,
+    )(gain_parts)
+    attn_gain_grad, mlp_gain_grad, query_gain_grad, key_gain_grad = gain_parts_of(gain_sums)
     return (
         layer_output,
         input_grad,
-        gain_sums[:n_gain],
-        gain_sums[2 * n_gain : 2 * n_gain + n_head],
-        gain_sums[2 * n_gain + n_head :],
-        columns(attn_own, attn_other, 0, query_cols),
-        columns(attn_own, attn_other, query_cols, key_cols),
-        columns(attn_own, attn_other, query_cols + key_cols, key_cols),
-        columns(attn_own, attn_other, attn_cols, query_cols, 0),
-        gain_sums[n_gain : 2 * n_gain],
+        attn_gain_grad,
+        query_gain_grad,
+        key_gain_grad,
+        query_grad,
+        key_grad,
+        value_grad,
+        output_grad,
+        mlp_gain_grad,
         columns(gate_up_own, gate_up_other, 0, hidden_cols),
         columns(gate_up_own, gate_up_other, hidden_cols, hidden_cols),
         columns(down_own, down_other, 0, hidden_cols, 0),

time: 829 us -> 643 us (0.78)
  blocking collectives: 168 us -> 0 us
  Pallas kernels: 244 us -> 375 us
  local copies, waits for them, and re-layouts: 98.1 us -> 32.7 us
  other arithmetic: 80.1 us -> 47.1 us
  matrix products: 157 us -> 133 us
  waiting for transfers between devices: 48.4 us -> 25 us
    pallas_call x0 -> x6, Pallas kernels: none -> 131 us  [the longest x1 51.1 us: on_device(): call_leg(spread, 6, 'spread', [ANY] * 3, (jax.ShapeDtypeStruct((rows, wid...]
    all_gather x1 -> x0, blocking collectives: 119 us -> none  [on_device(): lax.all_gather(jnp.concatenate([g.astype(BF16).reshape(1, -1) for g in (a...]
    psum x1 -> x0, blocking collectives: 49.5 us -> none  [on_device(): gain_sums = lax.psum(gain_parts, ('dp', 'mp'))]
    dot_general x12 -> x0, matrix products: 24.5 us -> none  [the longest x2 8.79 us: on_device(): jnp.einsum('srqk,sqrd->skd', weights.astype(BF16), block_grad, preferred_...]
    ppermute x9 -> x3, waiting for transfers between devices: 48.3 us -> 24.9 us  [y_swap(): return lax.ppermute(values, 'dp', [(i, i ^ 1) for i in range(n_dp)])]
    concatenate x9 -> x0, local copies, waits for them, and re-layouts: 21.6 us -> none  [the longest x4 8.67 us: rotate(): return jnp.concatenate([-values[..., middle:], values[..., :middle]], -1)]
    unnamed x186 -> x77, local copies, waits for them, and re-layouts: 40.9 us -> 20 us
    reshape x14 -> x4, local copies, waits for them, and re-layouts: 14.4 us -> 2.52 us  [the longest x1 1.33 us: gain_parts_of(): part = rows_of[..., at:at + n, :].reshape(*lead, n * 128)]
  transfers between devices with their start and end apart: 17 -> 11, of which waited for: 4 -> 3; matrix products, arithmetic and copies ran while one was open for 29% -> 31% of each run, Pallas kernels for 20% -> 54%
where the time goes in v2:
time: 643 us; the launch traced here: 633 us
  Pallas kernels  375 us (58%)
  matrix products  133 us (21%)
  other arithmetic  47.1 us (7%)
  local copies, waits for them, and re-layouts  32.7 us (5%)
  waiting for transfers between devices  25 us (4%)
  between operations  15 us (2%)
    dot_general x12, matrix products, dot(): lax.dot_general(left, right, (((left_dim,), (right_dim,)), ((), ())), pre...  133 us
    pallas_call x1, Pallas kernels, on_device(): call_leg(hidden_leg, 1, 'hidden_leg', [ANY, VM, VM, VM], (jax.ShapeDtypeS...  82 us
    pallas_call x1, Pallas kernels, on_device(): call_leg(attention_leg, 0, 'attention_leg', [ANY, VM, VM], (jax.ShapeDtyp...  81.5 us
    pallas_call x1, Pallas kernels, on_device(): call_leg(output_leg, 2, 'output_leg', [ANY, ANY, VM, VM, VM, VM], (jax.Sh...  80.4 us
    pallas_call x1, Pallas kernels, on_device(): call_leg(spread, 6, 'spread', [ANY] * 3, (jax.ShapeDtypeStruct((rows, wid...  51.1 us
    ppermute x3, waiting for transfers between devices, y_swap(): return lax.ppermute(values, 'dp', [(i, i ^ 1) for i in range(n_dp)])  24.9 us
    pallas_call x1, Pallas kernels, on_device(): call_attention(attend_backward, seq_length, pair_rows, (jax.ShapeDtypeStr...  22.5 us
    unnamed x77, local copies, waits for them, and re-layouts  20 us
  transfers between devices with their start and end apart: 11, of which 3 were waited for; matrix products, arithmetic and copies ran while one was open for 31% of the time, Pallas kernels for 54%

profile of v2, /device:TPU:0, one launch (start us, length us, event | category | flops | bytes accessed | tf_op | source)
XLA Modules:
  0.0 633.4 jit_solution(5856958632143388543)
XLA Ops:
  7.2 0.8 convert_element_type.110
  10.0 18.3 %prepare.1 = (bf16[512,768]{1,0:T(8,128)(2,1)}, f32[8,8,128]{2,1,0:T(8,128)}, s32[1,1024]{1,0:T(1,128)}) custom-call(f32[256,512]{1,0:T(8,128)} %q.1, f32[256,256]{1,0:T(8,128)} %k.1, f32[256,256]{1,0:T(8,128)} %v.1, f32[512,256]{1,0:T(8,128)} %o.1, f32[8,128]{1,0:T(8,128)} %fusion.22.gain, s32[1,1024]{1,0:T(1,128)} %docs.1), custom_call_target="tpu_custom_call" | custom-call | bytes 3145728 | tf_op jit(solution)/shard_map/prepare/pallas_call | solution.py:774
  28.4 1.5 convert_element_type.104
  30.0 1.7 copy.31
  31.6 0.8 dynamic-slice_bitcast_fusion
  32.6 0.9 pad_maximum_fusion.6.gate_up_send
  33.5 51.1 %spread.1 = (bf16[1024,2048]{1,0:T(8,128)(2,1)}, bf16[256,1536]{1,0:T(8,128)(2,1)}, bf16[256,768]{1,0:T(8,128)(2,1)}) custom-call(bf16[1024,2048]{1,0:T(8,128)(2,1)} %tokens.1, bf16[256,1536]{1,0:T(8,128)(2,1)} %pad_maximum_fusion.6.gate_up_send, bf16[256,768]{1,0:T(8,128)(2,1)} %get-tuple-element.117.down_send), custom_call_target="tpu_custom_call" | custom-call | bytes 157286400 | tf_op jit(solution)/shard_map/spread/pallas_call | solution.py:802
  84.6 2.9 maximum_select_fusion.2
  87.6 1.3 constant_dynamic-slice_fusion.5.cotangent
  91.0 1.3 copy.42
  92.4 4.9 fusion
  97.9 11.6 %fusion.5.raw = f32[2048,512]{1,0:T(8,128)} fusion(bf16[2048,768]{1,0:T(8,128)(2,1)} %all-gather.4.cloned.1.call-done, f32[2048]{0:T(1024)S(1)} %bitcast.84, f32[2048]{0:T(1024)S(1)} %add_rsqrt_fusion, bf16[1024,2048]{1,0:T(8,128)(2,1)} %get-tuple-element.43, bf16[1024,2048]{1,0:T(8,128)(2,1)} %tokens.1), kind=kOutput, calls=%fused_computation.26 | convolution fusion | flops 4324327424 | bytes 14696448 | tf_op jit(solution)/shard_map/dot_general | solution.py:46
  109.6 2.9 collective-permute-done
  112.5 2.5 collective-permute-start.1
  115.0 3.7 fusion.9
  118.7 1.3 pad_maximum_fusion.4.cosine
  120.0 1.3 pad_maximum_fusion.5.sine
  121.3 15.8 %attend_forward.1 = bf16[2048,256]{1,0:T(8,128)(2,1)} custom-call(f32[2048,512]{1,0:T(8,128)} %fusion.5.raw, f32[2048,128]{1,0:T(8,128)} %pad_maximum_fusion.4.cosine, f32[2048,128]{1,0:T(8,128)} %pad_maximum_fusion.5.sine, s32[2048,1]{1,0:T(8,128)} %bitcast.78, f32[1,128]{1,0:T(1,128)} %reshape.252.gain_query, f32[1,128]{1,0:T(1,128)} %reshape.254.gain_key), custom_call_target="tpu_custom_call" | custom-call | flops 1073741824 | bytes 8388608 | tf_op jit(solution)/shard_map/attend_forward/pallas_call | solution.py:841
  138.1 1.2 maximum_select_fusion.6
  139.4 2.4 constant_dynamic-slice_fusion.4.tokens
  141.8 6.9 %convolution_convert_fusion.3 = bf16[2048,2048]{1,0:T(8,128)(2,1)} fusion(bf16[2048,256]{1,0:T(8,128)(2,1)S(1)} %copy-done.4, bf16[2048,768]{1,0:T(8,128)(2,1)} %all-gather.4.cloned.1.call-done), kind=kOutput, calls=%fused_computation.10 | convolution fusion | flops 2151677952 | bytes 10485760 | tf_op jit(solution)/shard_map/dot_general | solution.py:46
  148.7 81.5 %attention_leg.1 = (f32[256,2048]{1,0:T(8,128)}, bf16[2,2,2,256,2048]{4,3,2,1,0:T(8,128)(2,1)}) custom-call(bf16[2,2,2,256,2048]{4,3,2,1,0:T(8,128)(2,1)} %bitcast.71, bf16[256,2048]{1,0:T(8,128)(2,1)} %constant_dynamic-slice_fusion.4.tokens, f32[1,2048]{1,0:T(1,128)} %bitcast.82), custom_call_target="tpu_custom_call" | custom-call | bytes 209715200 | tf_op jit(solution)/shard_map/attention_leg/pallas_call | solution.py:858
  230.2 2.7 maximum_select_fusion
  232.9 2.4 copy.33
  235.3 17.8 %fusion.30 = f32[2048,1536]{0,1:T(8,128)S(1)} fusion(bf16[2048,2048]{1,0:T(8,128)(2,1)} %bitcast.96, bf16[2048,1536]{1,0:T(8,128)(2,1)} %all-gather.6.cloned.1.call-done), kind=kOutput, calls=%fused_computation.97 | convolution fusion | flops 12884901888 | bytes 27262976 | tf_op jit(solution)/shard_map/dot_general | solution.py:46
  253.1 3.1 multiply_convert_fusion.2
  256.2 4.7 copy-done.2
  260.9 1.2 copy-done.3
  262.1 10.1 %convolution_convert_fusion.5 = bf16[2048,768]{1,0:T(8,128)(2,1)} fusion(bf16[2048,768]{0,1:T(8,128)(2,1)} %multiply_convert_fusion.2, bf16[1024,2048]{1,0:T(8,128)(2,1)S(1)} %bitcast.73, bf16[1024,2048]{1,0:T(8,128)(2,1)S(1)} %copy-done.3), kind=kOutput, calls=%fused_computation.19 | convolution fusion | flops 6460801024 | bytes 14680064 | tf_op jit(solution)/shard_map/dot_general | solution.py:46
  272.3 8.4 %pad_maximum_fusion.1 = bf16[2048,2048]{1,0:T(8,128)(2,1)} fusion(bf16[1024,2048]{1,0:T(8,128)(2,1)} %bitcast.72, bf16[1024,2048]{1,0:T(8,128)(2,1)} %param.16), kind=kLoop, calls=%fused_computation.6 | loop fusion | flops 16777216 | bytes 16777216 | tf_op jit(solution)/shard_map/concatenate | solution.py:852
  280.7 15.3 %multiply_convert_fusion.1 = (bf16[2048,768]{0,1:T(8,128)(2,1)S(1)}, bf16[2048,768]{0,1:T(8,128)(2,1)S(1)}) fusion(f32[2048,1536]{0,1:T(8,128)} %copy-done.2, bf16[2048,2048]{1,0:T(8,128)(2,1)} %pad_maximum_fusion.1, bf16[2048,768]{1,0:T(8,128)(2,1)} %all-gather.8.cloned.1.call-done), kind=kOutput, calls=%fused_computation.14 | convolution fusion | flops 6462898176 | bytes 30408704 | tf_op jit(solution)/shard_map/dot_general | solution.py:46
  296.0 1.8 copy-done.8
  297.8 17.5 %convolution_convert_fusion.4 = bf16[2048,1536]{1,0:T(8,128)(2,1)} fusion(bf16[2048,2048]{1,0:T(8,128)(2,1)} %bitcast.97, bf16[2048,768]{0,1:T(8,128)(2,1)S(1)} %get-tuple-element.107, bf16[2048,768]{0,1:T(8,128)(2,1)S(1)} %get-tuple-element.106), kind=kOutput, calls=%fused_computation.11 | convolution fusion | flops 12900630528 | bytes 20971520 | tf_op jit(solution)/shard_map/dot_general | solution.py:46
  315.4 2.8 pad_maximum_fusion.2
  318.3 17.7 %convolution_convert_fusion.2 = bf16[2048,2048]{1,0:T(8,128)(2,1)} fusion(bf16[2048,1536]{0,1:T(8,128)(2,1)S(1)} %pad_maximum_fusion.2, bf16[2048,1536]{1,0:T(8,128)(2,1)} %all-gather.6.cloned.1.call-done), kind=kOutput, calls=%fused_computation.9 | convolution fusion | flops 12889096192 | bytes 20971520 | tf_op jit(solution)/shard_map/dot_general | solution.py:46
  336.0 82.0 %hidden_leg.1 = (f32[256,2048]{1,0:T(8,128)}, f32[1,2048]{1,0:T(1,128)}, bf16[2,2,2,256,2048]{4,3,2,1,0:T(8,128)(2,1)}) custom-call(bf16[2,2,2,256,2048]{4,3,2,1,0:T(8,128)(2,1)} %bitcast.76, f32[256,2048]{1,0:T(8,128)} %get-tuple-element.57.hidden, bf16[256,2048]{1,0:T(8,128)(2,1)} %copy-done.6, f32[1,2048]{1,0:T(1,128)} %bitcast.83), custom_call_target="tpu_custom_call" | custom-call | bytes 209715200 | tf_op jit(solution)/shard_map/hidden_leg/pallas_call | solution.py:888
  418.0 6.8 %convolution_convert_fusion.8.grad = bf16[2048,256]{1,0:T(8,128)(2,1)} fusion(bf16[2048,2048]{1,0:T(8,128)(2,1)} %bitcast.98, bf16[2048,768]{1,0:T(8,128)(2,1)S(1)} %copy-done.19), kind=kOutput, calls=%fused_computation.23 | convolution fusion | flops 2148007936 | bytes 10485760 | tf_op jit(solution)/shard_map/dot_general | solution.py:46
  424.9 22.5 %attend_backward.1 = (bf16[2048,512]{1,0:T(8,128)(2,1)}, f32[2,8,128]{2,1,0:T(8,128)}) custom-call(f32[2048,512]{1,0:T(8,128)} %fusion.5.raw, f32[2048,128]{1,0:T(8,128)} %pad_maximum_fusion.4.cosine, f32[2048,128]{1,0:T(8,128)} %pad_maximum_fusion.5.sine, s32[2048,1]{1,0:T(8,128)} %bitcast.79, f32[1,128]{1,0:T(1,128)} %reshape.252.gain_query, ...), custom_call_target="tpu_custom_call" | custom-call | flops 2684354560 | bytes 8388608 | tf_op jit(solution)/shard_map/attend_backward/pallas_call | solution.py:906
  447.5 6.1 convolution_convert_fusion.7
  453.9 5.4 convolution_convert_fusion.6
  459.3 1.8 pad_maximum_fusion.3
  461.5 8.6 %convolution_convert_fusion.1 = bf16[2048,2048]{1,0:T(8,128)(2,1)} fusion(bf16[2048,512]{1,0:T(8,128)(2,1)} %get-tuple-element.59, bf16[2048,768]{1,0:T(8,128)(2,1)S(1)} %copy-done.19), kind=kOutput, calls=%fused_computation.8 | convolution fusion | flops 4299161600 | bytes 12582912 | tf_op jit(solution)/shard_map/dot_general | solution.py:46
  470.1 9.3 %convolution_convert_fusion = bf16[2048,2048]{1,0:T(8,128)(2,1)} fusion(bf16[2048,768]{0,1:T(8,128)(2,1)S(1)} %copy-done.9, bf16[2048,768]{1,0:T(8,128)(2,1)S(1)} %copy-done.31), kind=kOutput, calls=%fused_computation.7 | convolution fusion | flops 6446645248 | bytes 14680064 | tf_op jit(solution)/shard_map/dot_general | solution.py:46
  479.4 80.4 %output_leg.1 = (f32[256,2048]{1,0:T(8,128)}, bf16[256,2048]{1,0:T(8,128)(2,1)}, f32[1,2048]{1,0:T(1,128)}) custom-call(bf16[2,2,2,256,2048]{4,3,2,1,0:T(8,128)(2,1)} %bitcast.74, bf16[2,2,2,256,2048]{4,3,2,1,0:T(8,128)(2,1)} %bitcast.75, bf16[256,2048]{1,0:T(8,128)(2,1)} %constant_dynamic-slice_fusion.4.tokens, f32[256,2048]{1,0:T(8,128)} %get-tuple-element.57.hidden, ...), custom_call_target="tpu_custom_call" | custom-call | bytes 209715200 | tf_op jit(solution)/shard_map/output_leg/pallas_call | solution.py:936
  559.8 1.3 select_maximum_fusion.parts
  561.2 10.5 %sum_gains.1 = f32[8,128]{1,0:T(8,128)} custom-call(f32[8,8,128]{2,1,0:T(8,128)} %select_maximum_fusion.parts), custom_call_target="tpu_custom_call" | custom-call | bytes 1048576 | tf_op jit(solution)/shard_map/sum_gains/pallas_call | solution.py:994
  571.7 1.3 slice_bitcast_fusion.2
  573.0 1.3 slice_bitcast_fusion
  574.4 1.1 collective-permute-start.4
  575.5 1.1 dynamic-slice_convert_fusion
  576.5 1.0 collective-permute-start.3
  577.5 1.0 fusion.26
  578.5 7.9 %collective-permute-done.4 = bf16[256,768]{1,0:T(8,128)(2,1)S(1)} collective-permute-done((bf16[256,768]{1,0:T(8,128)(2,1)S(1)}, bf16[256,768]{1,0:T(8,128)(2,1)S(1)}, u32[]{:S(2)}, u32[]{:S(2)}) %collective-permute-start.4) | collective-permute-done | bytes 393248 | tf_op jit(solution)/shard_map/ppermute | solution.py:722
  586.7 1.6 copy.37
  588.3 14.1 %collective-permute-done.3 = bf16[256,1536]{1,0:T(8,128)(2,1)S(1)} collective-permute-done((bf16[256,1536]{1,0:T(8,128)(2,1)}, bf16[256,1536]{1,0:T(8,128)(2,1)S(1)}, u32[]{:S(2)}, u32[]{:S(2)}) %collective-permute-start.3) | collective-permute-done | bytes 786464 | tf_op jit(solution)/shard_map/ppermute | solution.py:722
  602.5 2.9 maximum_select_fusion.4
  605.4 1.3 maximum_select_fusion.3
  606.8 12.8 %finish_attention.1 = (f32[256,512]{1,0:T(8,128)}, f32[256,256]{1,0:T(8,128)}, f32[256,256]{1,0:T(8,128)}, f32[512,256]{1,0:T(8,128)}) custom-call(bf16[512,768]{1,0:T(8,128)(2,1)} %reduce-scatter.8.cloned.1.call-done.grads), custom_call_target="tpu_custom_call" | custom-call | bytes 3145728 | tf_op jit(solution)/shard_map/finish_attention/pallas_call | solution.py:962
  619.6 2.4 copy.51
  622.0 1.3 copy.52
  623.4 0.8 copy.53
  624.1 0.7 copy.54
  624.9 0.7 copy.55
  625.6 0.8 copy.56
  (112 shorter events, 7.2 us)
Async XLA Ops:
  7.2 22.7 %copy-start.11 = (f32[256,1536]{1,0:T(8,128)S(1)}, f32[256,1536]{1,0:T(8,128)}, u32[]{:S(2)}) copy-start(f32[256,1536]{1,0:T(8,128)} %param.26) | copy-start | bytes 4718596
  7.2 90.7 %all-gather.4.cloned.1.call-start = ((), (), s32[]{:S(2)}) async-start(), calls=%async_computation.3 | async-start | bytes 3932160 | tf_op jit(solution)/shard_map/all_gather | solution.py:739
  28.3 207.0 %all-gather.6.cloned.1.call-start = ((), (), s32[]{:S(2)}) async-start(), calls=%async_computation.4 | async-start | bytes 7864320 | tf_op jit(solution)/shard_map/all_gather | solution.py:739
  84.6 5.0 copy-start.25
  84.6 6.2 copy-start.22
  84.6 6.2 copy-start.26
  87.6 193.1 %all-gather.8.cloned.1.call-start = ((), (), s32[]{:S(2)}) async-start(), calls=%async_computation.5 | async-start | bytes 3932160 | tf_op jit(solution)/shard_map/all_gather | solution.py:739
  88.9 8.3 %copy-start.6 = (bf16[256,2048]{1,0:T(8,128)(2,1)}, bf16[256,2048]{1,0:T(8,128)(2,1)S(1)}, u32[]{:S(2)}) copy-start(bf16[256,2048]{1,0:T(8,128)(2,1)S(1)} %constant_dynamic-slice_fusion.5.cotangent) | copy-start | bytes 3145732
  88.9 23.5 %collective-permute-start = (bf16[256,2048]{1,0:T(8,128)(2,1)S(1)}, bf16[256,2048]{1,0:T(8,128)(2,1)S(1)}, u32[]{:S(2)}, u32[]{:S(2)}) collective-permute-start(bf16[256,2048]{1,0:T(8,128)(2,1)S(1)} %constant_dynamic-slice_fusion.5.cotangent), channel_id=1, source_target_pairs={{0,4},{4,0},{8,12},{12,8},{16,20},{20,16},{24,28},{28,24},{1,5},{5... | collective-permute-start | bytes 3145736 | tf_op jit(solution)/shard_map/ppermute | solution.py:722
  97.3 12.3 %copy-start.28 = (f32[2048]{0:T(1024)}, f32[2048]{0:T(1024)S(1)}, u32[]{:S(2)}) copy-start(f32[2048]{0:T(1024)S(1)} %add_rsqrt_fusion) | copy-start | bytes 24580
  97.9 11.6 %copy-start.23 = (f32[8,2,128]{2,1,0:T(2,128)}, f32[8,2,128]{2,1,0:T(2,128)S(1)}, u32[]{:S(2)}) copy-start(f32[8,2,128]{2,1,0:T(2,128)S(1)} %get-tuple-element.123) | copy-start | bytes 24580
  112.4 8.9 %copy-start.13 = (bf16[256,2048]{1,0:T(8,128)(2,1)}, bf16[256,2048]{1,0:T(8,128)(2,1)S(1)}, u32[]{:S(2)}) copy-start(bf16[256,2048]{1,0:T(8,128)(2,1)S(1)} %collective-permute-done) | copy-start | bytes 3145732
  112.5 24.7 %collective-permute-start.1 = (bf16[256,2048]{1,0:T(8,128)(2,1)S(1)}, bf16[256,2048]{1,0:T(8,128)(2,1)S(1)}, u32[]{:S(2)}, u32[]{:S(2)}) collective-permute-start(bf16[256,2048]{1,0:T(8,128)(2,1)S(1)} %collective-permute-done), channel_id=1, source_target_pairs={{0,2},{1,3},{2,0},{3,1},{4,6},{5,7},{6,4},{7,5},{8,10},{9,11},{10,... | collective-permute-start | bytes 3145736 | tf_op jit(solution)/shard_map/ppermute | solution.py:725
  121.3 15.8 %copy-start.14 = (bf16[256,2048]{1,0:T(8,128)(2,1)S(1)}, bf16[256,2048]{1,0:T(8,128)(2,1)}, u32[]{:S(2)}) copy-start(bf16[256,2048]{1,0:T(8,128)(2,1)} %copy-done.13) | copy-start | bytes 3145732
  137.1 1.0 copy-start.18
  137.1 4.6 copy-start.4
  137.5 92.7 %collective-permute-start.2 = (bf16[2,256,2048]{2,1,0:T(8,128)(2,1)S(1)}, bf16[2,256,2048]{2,1,0:T(8,128)(2,1)}, u32[]{:S(2)}, u32[]{:S(2)}) collective-permute-start(bf16[2,256,2048]{2,1,0:T(8,128)(2,1)S(1)} %maximum_select_fusion.1), channel_id=1, source_target_pairs={{0,1},{1,0},{2,3},{3,2},{4,5},{5,4},{6,7},{7,6},{8,9},{9,8},{10,11... | collective-permute-start | bytes 6291464 | tf_op jit(solution)/shard_map/ppermute | solution.py:725
  139.3 321.8 %reduce-scatter.6.cloned.1.call-start = ((), (), s32[]{:S(2)}) async-start(), calls=%async_computation.7 | async-start | bytes 3932160 | tf_op jit(solution)/shard_map/reduce_scatter | solution.py:742
  253.0 7.9 %copy-start.2 = (f32[2048,1536]{0,1:T(8,128)}, f32[2048,1536]{0,1:T(8,128)S(1)}, u32[]{:S(2)}) copy-start(f32[2048,1536]{0,1:T(8,128)S(1)} %fusion.30) | copy-start | bytes 37748740
  253.1 7.9 %copy-start.1 = (bf16[2,2,256,2048]{3,2,1,0:T(8,128)(2,1)S(1)}, bf16[2,2,256,2048]{3,2,1,0:T(8,128)(2,1)}, u32[]{:S(2)}) copy-start(bf16[2,2,256,2048]{3,2,1,0:T(8,128)(2,1)} %copy.33) | copy-start | bytes 12582916
  253.1 9.0 %copy-start.3 = (bf16[1024,2048]{1,0:T(8,128)(2,1)S(1)}, bf16[1024,2048]{1,0:T(8,128)(2,1)}, u32[]{:S(2)}) copy-start(bf16[1024,2048]{1,0:T(8,128)(2,1)} %param.16) | copy-start | bytes 12582916
  272.2 189.0 %reduce-scatter.4.cloned.1.call-start = ((), (), s32[]{:S(2)}) async-start(), calls=%async_computation.6 | async-start | bytes 7864320 | tf_op jit(solution)/shard_map/reduce_scatter | solution.py:742
  296.0 1.8 copy-start.8
  315.4 291.4 %reduce-scatter.8.cloned.1.call-start = ((), (), s32[]{:S(2)}) async-start(), calls=%async_computation.8 | async-start | bytes 3932160 | tf_op jit(solution)/shard_map/reduce_scatter | solution.py:742
  336.0 82.0 %copy-start.19 = (bf16[2048,768]{1,0:T(8,128)(2,1)S(1)}, bf16[2048,768]{1,0:T(8,128)(2,1)}, u32[]{:S(2)}) copy-start(bf16[2048,768]{1,0:T(8,128)(2,1)} %all-gather.4.cloned.1.call-done) | copy-start | bytes 9437188
  424.9 22.5 %copy-start.5 = (bf16[2048,256]{1,0:T(8,128)(2,1)S(1)}, bf16[2048,256]{1,0:T(8,128)(2,1)}, u32[]{:S(2)}) copy-start(bf16[2048,256]{1,0:T(8,128)(2,1)} %attend_forward.1) | copy-start | bytes 3145732
  447.4 6.1 copy-start
  447.4 6.1 copy-start.7
  447.4 6.1 copy-start.24
  447.4 6.1 copy-start.29
  447.4 6.4 %copy-start.32 = (bf16[2048,512]{1,0:T(8,128)(2,1)S(1)}, bf16[2048,512]{1,0:T(8,128)(2,1)}, u32[]{:S(2)}) copy-start(bf16[2048,512]{1,0:T(8,128)(2,1)} %get-tuple-element.59) | copy-start | bytes 6291460
  459.3 1.9 copy-start.30
  461.4 8.6 %copy-start.9 = (bf16[2048,768]{0,1:T(8,128)(2,1)S(1)}, bf16[2048,768]{0,1:T(8,128)(2,1)}, u32[]{:S(2)}) copy-start(bf16[2048,768]{0,1:T(8,128)(2,1)} %multiply_convert_fusion.2) | copy-start | bytes 9437188
  461.5 8.6 %copy-start.31 = (bf16[2048,768]{1,0:T(8,128)(2,1)S(1)}, bf16[2048,768]{1,0:T(8,128)(2,1)}, u32[]{:S(2)}) copy-start(bf16[2048,768]{1,0:T(8,128)(2,1)} %all-gather.8.cloned.1.call-done) | copy-start | bytes 9437188
  479.4 80.4 %copy-start.27 = (f32[1,2048]{1,0:T(1,128)S(1)}, f32[1,2048]{1,0:T(1,128)}, u32[]{:S(2)}) copy-start(f32[1,2048]{1,0:T(1,128)} %get-tuple-element.64) | copy-start | bytes 24580
  479.4 94.9 %copy-start.15 = (bf16[512,768]{1,0:T(8,128)(2,1)S(1)}, bf16[512,768]{1,0:T(8,128)(2,1)}, u32[]{:S(2)}) copy-start(bf16[512,768]{1,0:T(8,128)(2,1)} %reduce-scatter.6.cloned.1.call-done) | copy-start | bytes 2359300
  479.4 96.1 %copy-start.12 = (bf16[512,1536]{1,0:T(8,128)(2,1)S(1)}, bf16[512,1536]{1,0:T(8,128)(2,1)}, u32[]{:S(2)}) copy-start(bf16[512,1536]{1,0:T(8,128)(2,1)} %reduce-scatter.4.cloned.1.call-done) | copy-start | bytes 4718596
  574.4 12.0 %collective-permute-start.4 = (bf16[256,768]{1,0:T(8,128)(2,1)S(1)}, bf16[256,768]{1,0:T(8,128)(2,1)S(1)}, u32[]{:S(2)}, u32[]{:S(2)}) collective-permute-start(bf16[256,768]{1,0:T(8,128)(2,1)S(1)} %get-tuple-element.113), channel_id=1, source_target_pairs={{0,4},{4,0},{8,12},{12,8},{16,20},{20,16},{24,28},{28,24},{1,5},{5... | collective-permute-start | bytes 1179656 | tf_op jit(solution)/shard_map/ppermute | solution.py:722
  576.5 25.9 %collective-permute-start.3 = (bf16[256,1536]{1,0:T(8,128)(2,1)}, bf16[256,1536]{1,0:T(8,128)(2,1)S(1)}, u32[]{:S(2)}, u32[]{:S(2)}) collective-permute-start(bf16[256,1536]{1,0:T(8,128)(2,1)} %get-tuple-element.111), channel_id=1, source_target_pairs={{0,4},{4,0},{8,12},{12,8},{16,20},{20,16},{24,28},{28,24},{1,5},{5... | collective-permute-start | bytes 2359304 | tf_op jit(solution)/shard_map/ppermute | solution.py:722
  602.5 19.5 %copy-start.10 = (f32[256,2048]{1,0:T(8,128)S(1)}, f32[256,2048]{1,0:T(8,128)}, u32[]{:S(2)}) copy-start(f32[256,2048]{1,0:T(8,128)} %get-tuple-element.153) | copy-start | bytes 6291460
  619.6 3.8 copy-start.17
  619.6 4.6 copy-start.21
  619.6 5.3 copy-start.20
  619.6 6.0 copy-start.16
Sparse Core Ops, SparseCore 0:
  28.4 61.6 all-gather.3
  92.3 113.9 all-gather.5
  208.4 61.7 all-gather.7
  272.4 58.8 reduce-scatter.5
  333.5 110.7 reduce-scatter.3
  461.3 57.4 reduce-scatter.7

commit v3 on v2

--- a/solution.py
+++ b/solution.py
@@ -50,6 +50,7 @@
 
 CHUNKS = 2
 TILE = 32
+COLUMNS = 512
 
 
 def neighbours():
@@ -64,11 +65,14 @@
     )
 
 
-def enter(peers):
+def greet(peers):
     barrier = pltpu.get_barrier_semaphore()
     for peer in peers:
         pl.semaphore_signal(barrier, inc=1, device_id=peer, device_id_type=MESH)
-    pl.semaphore_wait(barrier, len(peers))
+
+
+def meet(count):
+    pl.semaphore_wait(pltpu.get_barrier_semaphore(), count)
 
 
 def remote(src, dst, send, recv, peer):
@@ -88,36 +92,38 @@
 class Reduce:
     STAGES = 5
 
-    def __init__(self, part, mine, got, gx, gy, fx, fy, local, send, recv):
-        self.refs = (part, mine, got, gx, gy, fx, fy, local, send, recv)
-        self.rows = part.shape[3] // CHUNKS
-        self.half = part.shape[4] // 2
+    def __init__(self, left, right, low, part, mine, got, gx, gy, fx, fy, send, recv):
+        self.left, self.right, self.low = left, right, low
+        self.refs = (part, mine, got, gx, gy, fx, fy, send, recv)
+        self.rows = mine.shape[2] // CHUNKS
+        self.width = mine.shape[3]
 
     @staticmethod
-    def scratch(rows, width):
-        half = width // 2
-        return [
+    def scratch(rows, width, low, part=True):
+        high = width - low
+        return [pltpu.VMEM((2, 2, rows, width), BF16)] * part + [
             pltpu.VMEM((2, 2, rows, width), BF16),
             pltpu.VMEM((2, 2, rows, width), BF16),
-            pltpu.VMEM((2, rows, half), BF16),
-            pltpu.VMEM((2, rows, half), BF16),
-            pltpu.VMEM((rows, half), BF16),
-            pltpu.VMEM((rows, half), BF16),
-            pltpu.SemaphoreType.DMA((CHUNKS,)),
+            pltpu.VMEM((2, rows, low), BF16),
+            pltpu.VMEM((2, rows, high), BF16),
+            pltpu.VMEM((rows, high), BF16),
+            pltpu.VMEM((rows, low), BF16),
             pltpu.SemaphoreType.DMA((Reduce.STAGES, CHUNKS)),
             pltpu.SemaphoreType.DMA((Reduce.STAGES, CHUNKS)),
         ]
 
+    def lanes(self):
+        return pl.ds(0, self.low), pl.ds(self.low, self.width - self.low)
+
     def copy(self, k, i):
-        part, mine, got, gx, gy, fx, fy, local, send, recv = self.refs
-        x, c, core_peer, x_peer, y_peer = neighbours()
+        part, mine, got, gx, gy, fx, fy, send, recv = self.refs
+        x, _, core_peer, x_peer, y_peer = neighbours()
         rows = pl.ds(k * self.rows, self.rows)
-        low, high = pl.ds(0, self.half), pl.ds(self.half, self.half)
+        low, high = self.lanes()
         s = [send.at[j, k] for j in range(self.STAGES)]
         r = [recv.at[j, k] for j in range(self.STAGES)]
         all_copies = (
-            lambda: pltpu.make_async_copy(part.at[:, :, c, rows], mine.at[:, :, rows], local.at[k]),
-            lambda: remote(part.at[:, :, 1 - c, rows], got.at[:, :, rows], s[0], r[0], core_peer),
+            lambda: remote(part.at[:, :, rows], got.at[:, :, rows], s[0], r[0], core_peer),
             lambda: remote(mine.at[:, 1 - x, rows, low], gx.at[:, rows], s[1], r[1], x_peer),
             lambda: remote(mine.at[1, :, rows, high], gy.at[:, rows], s[2], r[2], y_peer),
             lambda: remote(mine.at[1, x, rows, low], fy.at[rows], s[3], r[3], y_peer),
@@ -125,14 +131,31 @@
         )
         return all_copies[i]()
 
+    def produce(self, k, own):
+        target = self.refs[1] if own else self.refs[0]
+        core = neighbours()[1]
+        core = core if own else 1 - core
+        rows = pl.ds(k * self.rows, self.rows)
+        depth = self.left.shape[4]
+
+        def tile(j, carry):
+            cols = pl.ds(pl.multiple_of(j * COLUMNS, COLUMNS), COLUMNS)
+            left = self.left[:, :, core, rows, :].reshape(4 * self.rows, depth)
+            product = dot(left, self.right[cols, :], 1, 1).astype(BF16)
+            target[:, :, rows, cols] = product.reshape(2, 2, self.rows, COLUMNS)
+            return carry
+
+        lax.fori_loop(0, self.width // COLUMNS, tile, 0)
+
     def begin(self, k):
-        self.copy(k, 1).start()
         self.copy(k, 0).start()
 
+    def release(self, k):
+        self.copy(k, 0).wait_send()
+
     def first(self, k):
-        _, mine, got = self.refs[:3]
-        self.copy(k, 0).wait()
-        self.copy(k, 1).wait_recv()
+        mine, got = self.refs[1:3]
+        self.copy(k, 0).wait_recv()
 
         def add(i, carry):
             def step(rows):
@@ -143,15 +166,15 @@
             return carry
 
         lax.fori_loop(0, 4, add, 0)
+        self.copy(k, 1).start()
         self.copy(k, 2).start()
-        self.copy(k, 3).start()
 
     def second(self, k):
-        _, mine, _, gx, gy = self.refs[:5]
+        mine, _, gx, gy = self.refs[1:5]
         x = neighbours()[0]
-        low, high = pl.ds(0, self.half), pl.ds(self.half, self.half)
+        low, high = self.lanes()
+        self.copy(k, 1).wait_recv()
         self.copy(k, 2).wait_recv()
-        self.copy(k, 3).wait_recv()
 
         def step(rows):
             for i in range(2):
@@ -161,17 +184,17 @@
                 mine[at] = (mine[at].astype(F32) + gy[i, rows].astype(F32)).astype(BF16)
 
         tiles(k * self.rows, self.rows, step)
+        self.copy(k, 3).start()
         self.copy(k, 4).start()
-        self.copy(k, 5).start()
 
     def arrive(self, k):
+        self.copy(k, 3).wait_recv()
         self.copy(k, 4).wait_recv()
-        self.copy(k, 5).wait_recv()
 
     def take(self, rows):
-        _, mine, _, _, _, fx, fy = self.refs[:7]
+        mine, fx, fy = self.refs[1], *self.refs[5:7]
         x = neighbours()[0]
-        low, high = pl.ds(0, self.half), pl.ds(self.half, self.half)
+        low, high = self.lanes()
         return jnp.concatenate(
             [
                 mine[0, x, rows, low].astype(F32) + fy[rows].astype(F32),
@@ -182,7 +205,7 @@
 
     def finish(self):
         for k in range(CHUNKS):
-            for i in range(1, 6):
+            for i in range(1, 5):
                 self.copy(k, i).wait_send()
 
 
@@ -255,100 +278,296 @@
                 self.copy(k, i).wait_send()
 
 
-def attention_leg(part, tokens, gain, hidden, normed, *scratch):
-    n = len(Reduce.scratch(32, 256))
-    reduce, gather = Reduce(part, *scratch[:n]), Gather(scratch[n], normed, *scratch[n + 1 :])
-    mine = scratch[n]
-    enter(neighbours()[2:])
-    for k in range(CHUNKS):
+N_REDUCE = len(Reduce.scratch(32, 256, 128))
+
+
+def nothing():
+    pass
+
+
+def leg(left, right, low, full, step, scratch, at_start=nothing, at_middle=nothing):
+    reduce = Reduce(left, right, low, *scratch[:N_REDUCE])
+    gather = Gather(scratch[N_REDUCE], full, *scratch[N_REDUCE + 1 :])
+    mine = scratch[N_REDUCE]
+    greet(neighbours()[2:])
+    for k in range(CHUNKS):
+        reduce.produce(k, False)
+        if k == 0:
+            meet(3)
         reduce.begin(k)
     for k in range(CHUNKS):
+        reduce.produce(k, True)
         reduce.first(k)
+    at_start()
     for k in range(CHUNKS):
         reduce.second(k)
-
-    def step(rows):
-        h = tokens[rows].astype(F32) + reduce.take(rows)
-        hidden[rows] = h
-        mine[rows] = (norm_parts(h)[0] * gain[...]).astype(BF16)
+    at_middle()
+
+    def step_at(rows):
+        mine[rows] = step(rows, reduce.take(rows)).astype(BF16)
 
     for k in range(CHUNKS):
         reduce.arrive(k)
-        tiles(k * reduce.rows, reduce.rows, step)
+        tiles(k * reduce.rows, reduce.rows, step_at)
         gather.begin(k)
     for k in range(CHUNKS):
         gather.second(k)
     for k in range(CHUNKS):
         gather.third(k)
     gather.finish()
+    for k in range(CHUNKS):
+        reduce.release(k)
     reduce.finish()
 
 
-def hidden_leg(part, hidden, cotangent, gain, grad_hidden, gain_grad, full, *scratch):
-    n = len(Reduce.scratch(32, 256))
-    reduce, gather = Reduce(part, *scratch[:n]), Gather(scratch[n], full, *scratch[n + 1 :])
-    mine = scratch[n]
-    enter(neighbours()[2:])
-    for k in range(CHUNKS):
-        reduce.begin(k)
+def attention_leg(
+    left,
+    packed,
+    tokens,
+    gain,
+    cotangent,
+    cot_part,
+    cot_across,
+    hidden,
+    normed,
+    cot_pair,
+    cot_buffer,
+    cot_in,
+    cot_out,
+    cot_send,
+    cot_recv,
+    *scratch
+):
+    def step(rows, total):
+        h = tokens[rows].astype(F32) + total
+        hidden[rows] = h
+        return norm_parts(h)[0] * gain[...]
+
+    x, core, core_peer = neighbours()[:3]
+    own, share = cotangent.shape[0], cot_part.shape[0]
+
+    def place(at_x, at_core):
+        start = own + (at_x * 2 + at_core) * share
+        return pl.ds(pl.multiple_of(start, share), share)
+
+    sources = (cotangent, cot_part, cot_across)
+    starts = (0, own, own + share)
+    places = (pl.ds(0, own), place(x, core), place(1 - x, core))
+    loads, stores, sends = [], [], []
+    for i in range(3):
+        held = cot_buffer.at[pl.ds(starts[i], sources[i].shape[0])]
+        loads.append(pltpu.make_async_copy(sources[i], held, cot_in.at[i]))
+        stores.append(pltpu.make_async_copy(held, cot_pair.at[places[i]], cot_out.at[i]))
+        if i > 0:
+            to = cot_pair.at[places[i]]
+            sends.append(remote(sources[i], to, cot_send.at[i - 1], cot_recv.at[i - 1], core_peer))
+
+    def at_start():
+        for copy in loads + sends:
+            copy.start()
+
+    def at_middle():
+        for load, store in zip(loads, stores):
+            load.wait()
+            store.start()
+
+    depth = left.shape[4]
+    right = packed.at[:, pl.ds(packed.shape[1] - depth, depth)]
+    leg(left, right, right.shape[0] // 2, normed, step, scratch, at_start, at_middle)
+    for copy in stores + sends:
+        copy.wait()
+
+
+def hidden_leg(left, right, hidden, cotangent, gain, grad_hidden, gain_grad, full, *scratch):
     gain_grad[...] = jnp.zeros_like(gain_grad)
-    for k in range(CHUNKS):
-        reduce.first(k)
-    for k in range(CHUNKS):
-        reduce.second(k)
-
-    def step(rows):
-        grad = reduce.take(rows)
+
+    def step(rows, grad):
         hat, inv = norm_parts(hidden[rows])
         gain_grad[...] += jnp.sum(grad * hat, 0, keepdims=True)
         grad = cotangent[rows].astype(F32) + norm_back(grad, hat, inv, gain[...])
         grad_hidden[rows] = grad
-        mine[rows] = grad.astype(BF16)
-
-    for k in range(CHUNKS):
-        reduce.arrive(k)
-        tiles(k * reduce.rows, reduce.rows, step)
-        gather.begin(k)
-    for k in range(CHUNKS):
-        gather.second(k)
-    for k in range(CHUNKS):
-        gather.third(k)
-    gather.finish()
-    reduce.finish()
+        return grad
+
+    leg(left, right, right.shape[0] // 2, full, step, scratch)
+
+
+class SumGains:
+    def __init__(self, parts, total, got, mid, others, send, recv, send_mp, recv_mp):
+        self.refs = (parts, total, got, mid, others, send, recv, send_mp, recv_mp)
+        self.n_dp, self.n_mp = parts.shape[0], others.shape[0] + 1
+
+    @staticmethod
+    def scratch(n_dp, n_mp):
+        return [
+            pltpu.VMEM((n_dp, 8, 128), F32),
+            pltpu.VMEM((8, 128), F32),
+            pltpu.VMEM((n_mp - 1, 8, 128), F32),
+            pltpu.SemaphoreType.DMA((n_dp,)),
+            pltpu.SemaphoreType.DMA((n_dp,)),
+            pltpu.SemaphoreType.DMA((n_mp,)),
+            pltpu.SemaphoreType.DMA((n_mp,)),
+        ]
+
+    def across(self, j):
+        return (lax.rem(lax.axis_index("dp") + j, self.n_dp), lax.axis_index("mp"))
+
+    def along(self, j):
+        return (lax.axis_index("dp"), lax.rem(lax.axis_index("mp") + j, self.n_mp))
+
+    def greet(self):
+        barrier = pltpu.get_barrier_semaphore()
+
+        def one(j, carry):
+            pl.semaphore_signal(barrier, inc=1, device_id=self.across(j), device_id_type=MESH)
+            return carry
+
+        lax.fori_loop(1, self.n_dp, one, 0)
+        greet([self.along(j) for j in range(1, self.n_mp)])
+
+    def first(self, j):
+        parts, _, got, _, _, send, recv = self.refs[:7]
+        to = self.across(j)
+        return remote(parts.at[to[0]], got.at[j], send.at[j], recv.at[j], to)
+
+    def second(self, j):
+        mid, others = self.refs[3:5]
+        send, recv = self.refs[7:]
+        return remote(mid, others.at[j - 1], send.at[j], recv.at[j], self.along(j))
+
+    def begin(self):
+        def start(j, carry):
+            self.first(j).start()
+            return carry
+
+        lax.fori_loop(1, self.n_dp, start, 0)
+
+    def pass_on(self):
+        parts, _, got, mid = self.refs[:4]
+        mid[...] = parts[lax.axis_index("dp")]
+
+        def add(j, carry):
+            self.first(j).wait()
+            mid[...] += got[j]
+            return carry
+
+        lax.fori_loop(1, self.n_dp, add, 0)
+        for j in range(1, self.n_mp):
+            self.second(j).start()
+
+    def finish(self):
+        _, total, _, mid, others = self.refs[:5]
+        result = mid[...]
+        for j in range(1, self.n_mp):
+            self.second(j).wait()
+            result += others[j - 1]
+        total[...] = result
 
 
 def output_leg(
-    part, mlp_part, tokens, hidden, grad_hidden, gain, input_grad, output, gain_grad, *scratch
+    left,
+    packed,
+    mlp_left,
+    mlp_right,
+    tokens,
+    hidden,
+    grad_hidden,
+    gain,
+    gain_parts,
+    gate_up_grad,
+    down_grad,
+    input_grad,
+    output,
+    gain_total,
+    gate,
+    up,
+    down,
+    part,
+    gain_grad,
+    slots,
+    gate_up_other,
+    down_other,
+    swap_send,
+    swap_recv,
+    *scratch
 ):
-    n = len(Reduce.scratch(32, 256))
-    legs = Reduce(part, *scratch[:n]), Reduce(mlp_part, *scratch[n:])
-    enter(neighbours()[2:])
-    for reduce in legs:
-        for k in range(CHUNKS):
-            reduce.begin(k)
-    gain_grad[...] = jnp.zeros_like(gain_grad)
-    for reduce in legs:
-        for k in range(CHUNKS):
-            reduce.first(k)
-    for reduce in legs:
-        for k in range(CHUNKS):
-            reduce.second(k)
+    low = scratch[2].shape[2]
+    n = N_REDUCE - 1
+    first = Reduce(left, packed.at[:, pl.ds(0, left.shape[4])], low, part, *scratch[:n])
+    second = Reduce(mlp_left, mlp_right, low, part, *scratch[n : 2 * n])
+    sums = SumGains(slots, gain_total, *scratch[2 * n :])
+    y, y_peer = lax.axis_index("dp") % 2, neighbours()[4]
+    half = gate.shape[0]
+    mine, theirs = (pl.ds(pl.multiple_of(i * half, half), half) for i in (y, 1 - y))
+    swaps = [
+        remote(gate_up_grad.at[theirs], gate_up_other, swap_send.at[0], swap_recv.at[0], y_peer),
+        remote(down_grad.at[theirs], down_other, swap_send.at[1], swap_recv.at[1], y_peer),
+    ]
+
+    def place(source, down_source, which):
+        size = gate.shape[1] // 2
+        cols = pl.ds(pl.multiple_of(which * size, 128), size)
+        gate[:, cols] = source[:, :size].astype(F32)
+        up[:, cols] = source[:, size:].astype(F32)
+        down[cols, :] = down_source[...].T.astype(F32)
 
     def step_grad(rows):
-        grad = legs[0].take(rows)
+        grad = first.take(rows)
         hat, inv = norm_parts(tokens[rows].astype(F32))
         gain_grad[...] += jnp.sum(grad * hat, 0, keepdims=True)
         input_grad[rows] = grad_hidden[rows] + norm_back(grad, hat, inv, gain[...])
 
     def step_output(rows):
-        output[rows] = (hidden[rows] + legs[1].take(rows)).astype(BF16)
-
-    for reduce, step in zip(legs, (step_grad, step_output)):
-        for k in range(CHUNKS):
-            reduce.arrive(k)
-            tiles(k * reduce.rows, reduce.rows, step)
-    for reduce in legs:
-        reduce.finish()
+        output[rows] = (hidden[rows] + second.take(rows)).astype(BF16)
+
+    sums.greet()
+    gain_grad[...] = jnp.zeros_like(gain_grad)
+    slots[...] = gain_parts[...]
+    for k in range(CHUNKS):
+        first.produce(k, False)
+        if k == 0:
+            meet(sums.n_dp + sums.n_mp - 2)
+        first.begin(k)
+    for k in range(CHUNKS):
+        first.produce(k, True)
+        first.first(k)
+    for copy in swaps:
+        copy.start()
+    for k in range(CHUNKS):
+        first.release(k)
+        second.produce(k, False)
+        second.begin(k)
+    for k in range(CHUNKS):
+        first.second(k)
+    for k in range(CHUNKS):
+        second.produce(k, True)
+        second.first(k)
+    for k in range(CHUNKS):
+        first.arrive(k)
+        tiles(k * first.rows, first.rows, step_grad)
+    owned = gain_grad.shape[1] // sums.n_dp
+    for i in range(sums.n_dp):
+        for j in range(-(-owned // 128)):
+            size = min(128, owned - j * 128)
+            at = i * owned + j * 128
+            slots[i, j : j + 1, :size] = gain_grad[:, at : at + size]
+    sums.begin()
+    place(gate_up_grad.at[mine], down_grad.at[mine], y)
+    for k in range(CHUNKS):
+        second.second(k)
+    sums.pass_on()
+    for copy in swaps:
+        copy.wait_recv()
+    place(gate_up_other, down_other, 1 - y)
+    for k in range(CHUNKS):
+        second.arrive(k)
+        tiles(k * second.rows, second.rows, step_output)
+    sums.finish()
+    for k in range(CHUNKS):
+        second.release(k)
+    for copy in swaps:
+        copy.wait_send()
+    first.finish()
+    second.finish()
 
 
 ANY = pl.BlockSpec(memory_space=pl.ANY)
@@ -365,77 +584,9 @@
         name=name,
         cost_estimate=pl.CostEstimate(flops=0, bytes_accessed=bytes_moved, transcendentals=0),
         compiler_params=pltpu.CompilerParams(
-            collective_id=ident, has_side_effects=True, vmem_limit_bytes=56 * MIB
+            collective_id=ident, has_side_effects=True, vmem_limit_bytes=60 * MIB
         ),
     )
-
-
-def prepare(q, k, v, o, gain, docs, pack, gains, docs_other, stage, swap, send, recv):
-    dp, mp = lax.axis_index("dp"), lax.axis_index("mp")
-    n_dp = gains.shape[0]
-    y, y_peer = dp % 2, (dp + 1 - 2 * (dp % 2), mp)
-    rows = q.shape[0]
-
-    def peer(j):
-        return (lax.rem(dp + j, n_dp), mp)
-
-    barrier = pltpu.get_barrier_semaphore()
-
-    def greet(j, carry):
-        pl.semaphore_signal(barrier, inc=1, device_id=peer(j), device_id_type=MESH)
-        return carry
-
-    lax.fori_loop(1, n_dp, greet, 0)
-    widths = [w.shape[1] // 2 for w in (q, k, v)]
-    first = sum(widths)
-
-    def fill_inputs(target, row, which):
-        at = 0
-        for w, size in zip((q, k, v), widths):
-            cols = pl.ds(pl.multiple_of(which * size, 128), size)
-            target[pl.ds(row, rows), at : at + size] = w[:, cols].astype(BF16)
-            at += size
-
-    def fill_output(target, row, which):
-        size = o.shape[0] // 2
-        part = o[pl.ds(pl.multiple_of(which * size, 128), size), :].astype(BF16)
-        target[pl.ds(row, rows), first : first + size] = part.T
-
-    mine = pl.multiple_of(y * rows, rows)
-
-    def swapped(i):
-        cols = pl.ds(0, first) if i == 0 else pl.ds(first, o.shape[0] // 2)
-        target = pack.at[pl.ds(mine, rows), cols]
-        return remote(stage.at[:, cols], target, swap.at[0, i], swap.at[1, i], y_peer)
-
-    fill_inputs(stage, 0, 1 - y)
-    pl.semaphore_wait(barrier, n_dp - 1)
-    swapped(0).start()
-    fill_output(stage, 0, 1 - y)
-    swapped(1).start()
-    docs_swapped = remote(docs, docs_other, swap.at[0, 2], swap.at[1, 2], y_peer)
-    docs_swapped.start()
-
-    def gain_to(j):
-        return remote(gain, gains.at[dp], send.at[j], recv.at[j], peer(j))
-
-    def share(j, carry):
-        gain_to(j).start()
-        return carry
-
-    lax.fori_loop(1, n_dp, share, 0)
-    gains[dp] = gain[...]
-    fill_inputs(pack, mine, y)
-    fill_output(pack, mine, y)
-
-    def settle(j, carry):
-        gain_to(j).wait()
-        return carry
-
-    lax.fori_loop(1, n_dp, settle, 0)
-    docs_swapped.wait()
-    swapped(0).wait()
-    swapped(1).wait()
 
 
 class Spread:
@@ -482,81 +633,213 @@
                 self.copy(k, i).wait_send()
 
 
-def spread(tokens, gate_up_send, down_send, tokens_other, gate_up, down, send, recv, *scratch):
-    rows = Spread(tokens, tokens_other, *scratch)
-    y_peer = neighbours()[4]
-    sent = [
-        remote(gate_up_send, gate_up, send.at[0], recv.at[0], y_peer),
-        remote(down_send, down, send.at[1], recv.at[1], y_peer),
+def front(
+    q,
+    k,
+    v,
+    o,
+    gain,
+    docs,
+    tokens,
+    gate,
+    up,
+    down,
+    full,
+    gains,
+    docs_other,
+    normed,
+    gate_up_mine,
+    down_mine,
+    stage,
+    gate_up_stage,
+    down_stage,
+    tokens_mine,
+    tokens_other,
+    gate_in,
+    up_in,
+    down_in,
+    local,
+    swap,
+    gain_send,
+    gain_recv,
+    ring_send,
+    ring_recv,
+    *scratch
+):
+    dp, mp = lax.axis_index("dp"), lax.axis_index("mp")
+    _, _, core_peer, x_peer, y_peer = neighbours()
+    n_dp = gains.shape[0]
+    n_slabs = n_dp // 2
+    y, z = dp % 2, dp // 2
+    rows = q.shape[0]
+    spread = Spread(tokens, tokens_other, *scratch)
+
+    def peer(j):
+        return (lax.rem(dp + j, n_dp), mp)
+
+    def greet_one(j, carry):
+        barrier = pltpu.get_barrier_semaphore()
+        pl.semaphore_signal(barrier, inc=1, device_id=peer(j), device_id_type=MESH)
+        return carry
+
+    lax.fori_loop(1, n_dp, greet_one, 0)
+    greet([core_peer, x_peer])
+    loads = [
+        pltpu.make_async_copy(source, target, local.at[i])
+        for i, (source, target) in enumerate(
+            ((tokens, tokens_mine), (gate, gate_in), (up, up_in), (down, down_in))
+        )
     ]
-    enter(neighbours()[2:])
-    for k in range(CHUNKS):
-        rows.copy(k, 0).start()
-    for k in range(CHUNKS):
-        rows.pass_on(k)
-        sent[k % 2].start()
-    for k in range(CHUNKS):
-        rows.pass_last(k)
-    rows.finish()
-    for i in range(2):
-        sent[i].wait()
-
-
-def sum_gains(parts, total, got, mid, others, send, recv, send_mp, recv_mp):
-    dp, mp = lax.axis_index("dp"), lax.axis_index("mp")
-    n_dp, n_mp = parts.shape[0], others.shape[0] + 1
-    barrier = pltpu.get_barrier_semaphore()
-
-    def across(j):
-        return (lax.rem(dp + j, n_dp), mp)
-
-    def along(j):
-        return (dp, lax.rem(mp + j, n_mp))
-
-    def greet(j, carry):
-        pl.semaphore_signal(barrier, inc=1, device_id=across(j), device_id_type=MESH)
+    for load in loads:
+        load.start()
+    widths = [w.shape[1] // 2 for w in (q, k, v)]
+    first = sum(widths)
+
+    def fill(target, row, which):
+        at = 0
+        for w, size in zip((q, k, v), widths):
+            cols = pl.ds(pl.multiple_of(which * size, 128), size)
+            target[pl.ds(row, rows), at : at + size] = w[:, cols].astype(BF16)
+            at += size
+        size = o.shape[0] // 2
+        part = o[pl.ds(pl.multiple_of(which * size, 128), size), :].astype(BF16)
+        target[pl.ds(row, rows), first : first + size] = part.T
+
+    def block(slab, pair):
+        return pl.ds(pl.multiple_of((slab * 2 + pair) * rows, rows), rows)
+
+    swapped = remote(stage, full.at[block(z, y)], swap.at[0, 0], swap.at[1, 0], y_peer)
+    docs_swapped = remote(docs, docs_other, swap.at[0, 1], swap.at[1, 1], y_peer)
+    mine = pl.ds(pl.multiple_of(y * rows, rows), rows)
+    gate_up_swapped = remote(
+        gate_up_stage, gate_up_mine.at[mine], swap.at[0, 2], swap.at[1, 2], y_peer
+    )
+    down_swapped = remote(down_stage, down_mine.at[mine], swap.at[0, 3], swap.at[1, 3], y_peer)
+
+    def ring(step, i):
+        slab = lax.rem(z - step + n_slabs, n_slabs)
+        at = full.at[block(slab, y if i == 0 else 1 - y)]
+        to = (lax.rem(dp + 2, n_dp), mp)
+        return remote(at, at, ring_send.at[step, i], ring_recv.at[step, i], to)
+
+    def ring_next(step, i):
+        slab = lax.rem(z - step - 1 + 2 * n_slabs, n_slabs)
+        at = full.at[block(slab, y if i == 0 else 1 - y)]
+        to = (lax.rem(dp + 2, n_dp), mp)
+        came = remote(at, at, ring_send.at[step, i], ring_recv.at[step, i], to)
+        came.wait_recv()
+        if isinstance(step, int) and step + 1 >= n_slabs - 1:
+            return
+        ring(step + 1, i).start()
+
+    def gain_to(j):
+        return remote(gain, gains.at[dp], gain_send.at[j], gain_recv.at[j], peer(j))
+
+    def share(j, carry):
+        gain_to(j).start()
         return carry
 
-    lax.fori_loop(1, n_dp, greet, 0)
-    for j in range(1, n_mp):
-        pl.semaphore_signal(barrier, inc=1, device_id=along(j), device_id_type=MESH)
-    pl.semaphore_wait(barrier, n_dp + n_mp - 2)
-
-    def first(j):
-        slot = lax.rem(dp + j, n_dp)
-        return remote(parts.at[slot], got.at[j], send.at[j], recv.at[j], across(j))
-
-    def start(j, carry):
-        first(j).start()
+    def settle(j, carry):
+        gain_to(j).wait()
         return carry
 
-    lax.fori_loop(1, n_dp, start, 0)
-    mid[...] = parts[dp]
-
-    def add(j, carry):
-        first(j).wait()
-        mid[...] += got[j]
+    def fill_mlp(gate_up_to, down_to, row, which):
+        size = gate.shape[1] // 2
+        cols = pl.ds(pl.multiple_of(which * size, 128), size)
+        gate_up_to[pl.ds(row, rows), :size] = gate_in[:, cols].astype(BF16)
+        gate_up_to[pl.ds(row, rows), size:] = up_in[:, cols].astype(BF16)
+        down_to[pl.ds(row, rows), :] = down_in[cols, :].astype(BF16).T
+
+    fill(stage, 0, 1 - y)
+    meet(n_dp - 1 + 2)
+    swapped.start()
+    fill(full, block(z, y).start, y)
+    ring(0, 0).start()
+    docs_swapped.start()
+    lax.fori_loop(1, n_dp, share, 0)
+    for c in range(CHUNKS):
+        spread.copy(c, 0).start()
+    gains[dp] = gain[...]
+    for load in loads[1:]:
+        load.wait()
+    fill_mlp(gate_up_stage, down_stage, 0, 1 - y)
+    gate_up_swapped.start()
+    down_swapped.start()
+    swapped.wait_recv()
+    ring(0, 1).start()
+    lax.fori_loop(1, n_dp, settle, 0)
+    owned = gain_rows_of(full.shape[0] // n_dp)
+    gain_row = jnp.concatenate(
+        [gains[i, j : j + 1, :size] for i in range(n_dp) for j, size in owned], -1
+    )
+
+    def norm(source, base, start, count):
+        def step(at):
+            hat = norm_parts(source[at].astype(F32))[0]
+            to = pl.ds(pl.multiple_of(base + at.start, TILE), TILE)
+            normed[to] = (hat * gain_row).astype(BF16)
+
+        tiles(start, count, step)
+
+    total = tokens.shape[0]
+    quarter = total // 4
+    loads[0].wait()
+    work = [functools.partial(norm, tokens_mine, 0, i * quarter, quarter) for i in range(4)]
+    work[0:0] = [functools.partial(fill_mlp, gate_up_mine, down_mine, mine.start, y)]
+    for c in range(CHUNKS):
+        work.append(functools.partial(spread.pass_on, c))
+    for c in range(CHUNKS):
+        work.append(functools.partial(spread.pass_last, c))
+    events = [(step, i) for step in range(n_slabs - 1) for i in range(2)]
+    if len(events) <= len(work):
+        for n, event in enumerate(events):
+            ring_next(*event)
+            if n < 2:
+                work.pop(0)()
+                work.pop(0)()
+            elif n < 4:
+                for _ in range(2):
+                    if work:
+                        work.pop(0)()
+        for job in work:
+            job()
+    else:
+        for job in work:
+            job()
+
+        def turn(step, carry):
+            for i in range(2):
+                ring_next(step, i)
+            return carry
+
+        lax.fori_loop(0, n_slabs - 2, turn, 0)
+        for i in range(2):
+            ring_next(n_slabs - 2, i)
+    spread.finish()
+    norm(tokens_other, total, 0, total)
+    docs_swapped.wait()
+    swapped.wait_send()
+    gate_up_swapped.wait()
+    down_swapped.wait()
+
+    def sent(step, carry):
+        for i in range(2):
+            ring(step, i).wait_send()
         return carry
 
-    lax.fori_loop(1, n_dp, add, 0)
-
-    def second(j):
-        return remote(mid, others.at[j - 1], send_mp.at[j], recv_mp.at[j], along(j))
-
-    for j in range(1, n_mp):
-        second(j).start()
-    result = mid[...]
-    for j in range(1, n_mp):
-        second(j).wait()
-        result += others[j - 1]
-    total[...] = result
+    lax.fori_loop(0, n_slabs - 1, sent, 0)
+
+
+def gain_rows_of(size):
+    return [(j, min(128, size - j * 128)) for j in range(-(-size // 128))]
 
 
 def finish_attention(grads, q, k, v, o, other, send, recv):
     dp, mp = lax.axis_index("dp"), lax.axis_index("mp")
     y, y_peer = dp % 2, (dp + 1 - 2 * (dp % 2), mp)
     rows = q.shape[0]
-    enter([y_peer])
+    greet([y_peer])
+    meet(1)
     theirs = pl.multiple_of((1 - y) * rows, rows)
     swapped = remote(grads.at[pl.ds(theirs, rows)], other, send, recv, y_peer)
     swapped.start()
@@ -771,54 +1054,55 @@
     )
     model_rows = query_weight.shape[0]
     pack_cols = attn_cols + query_cols
-    attn_mine, gains, docs_other = call_leg(
-        prepare,
+    pair_rows = 2 * rows
+    n_slabs = n_dp // 2
+    attn_full, gains, docs_other, normed_one, mlp_mine, down_mine = call_leg(
+        front,
         3,
-        "prepare",
-        [VM] * 6,
+        "front",
+        [VM] * 6 + [ANY] * 4,
         (
-            jax.ShapeDtypeStruct((2 * model_rows, pack_cols), BF16),
+            jax.ShapeDtypeStruct((width, pack_cols), BF16),
             jax.ShapeDtypeStruct((n_dp, 8, 128), F32),
             jax.ShapeDtypeStruct(documents.shape, jnp.int32),
+            jax.ShapeDtypeStruct((pair_rows, width), BF16),
+            jax.ShapeDtypeStruct((2 * model_rows, 2 * hidden_cols), BF16),
+            jax.ShapeDtypeStruct((2 * model_rows, hidden_cols), BF16),
         ),
-        (VM, VM, VM),
+        (VM,) * 6,
         [
             pltpu.VMEM((model_rows, pack_cols), BF16),
-            pltpu.SemaphoreType.DMA((2, 3)),
+            pltpu.VMEM((model_rows, 2 * hidden_cols), BF16),
+            pltpu.VMEM((model_rows, hidden_cols), BF16),
+            pltpu.VMEM((rows, width), BF16),
+            pltpu.VMEM((rows, width), BF16),
+            pltpu.VMEM(gate_weight.shape, F32),
+            pltpu.VMEM(up_weight.shape, F32),
+            pltpu.VMEM(down_weight.shape, F32),
+            pltpu.SemaphoreType.DMA((4,)),
+            pltpu.SemaphoreType.DMA((2, 4)),
             pltpu.SemaphoreType.DMA((n_dp,)),
             pltpu.SemaphoreType.DMA((n_dp,)),
-        ],
-        3 * MIB,
-    )(query_weight, key_projection, value_projection, output_weight, my_gains, documents)
-    attn_full = slab_gather(attn_mine)
-
-    mlp_low = [w.astype(BF16) for w in (gate_weight, up_weight)]
-    down_low = down_weight.astype(BF16)
-
-    def mlp_pack(which):
-        return jnp.concatenate([half(w, which, 1) for w in mlp_low], 1)
-
-    pair_rows = 2 * rows
-    tokens_other, mlp_got, down_got = call_leg(
-        spread,
-        6,
-        "spread",
-        [ANY] * 3,
-        (
-            jax.ShapeDtypeStruct((rows, width), BF16),
-            jax.ShapeDtypeStruct((model_rows, 2 * hidden_cols), BF16),
-            jax.ShapeDtypeStruct((model_rows, hidden_cols), BF16),
-        ),
-        (ANY,) * 3,
-        [pltpu.SemaphoreType.DMA((2,))] * 2 + Spread.scratch(),
-        150 * MIB,
-    )(tokens, mlp_pack(1 - y), half(down_low, 1 - y, 0).T)
-    mlp_mine = in_order(y, mlp_pack(y), mlp_got, 0)
-    down_mine = in_order(y, half(down_low, y, 0).T, down_got, 0)
-    tokens_pair = jnp.concatenate([tokens, tokens_other], 0)
+            pltpu.SemaphoreType.DMA((n_slabs, 2)),
+            pltpu.SemaphoreType.DMA((n_slabs, 2)),
+        ]
+        + Spread.scratch(),
+        250 * MIB,
+    )(
+        query_weight,
+        key_projection,
+        value_projection,
+        output_weight,
+        my_gains,
+        documents,
+        tokens,
+        gate_weight,
+        up_weight,
+        down_weight,
+    )
 
     cot_part = lax.dynamic_slice_in_dim(cotangent, mp * share, share, 0)
-    cot_part, _ = lax.optimization_barrier((cot_part, tokens_other))
+    cot_part, _ = lax.optimization_barrier((cot_part, docs_other))
     cot_part = y_swap(cot_part)
     gate_up_full = slab_gather(mlp_mine)
     down_full = slab_gather(down_mine)
@@ -827,15 +1111,13 @@
     tokens_share = lax.dynamic_slice_in_dim(tokens, mp * share, share, 0)
     cot_share = lax.dynamic_slice_in_dim(cotangent, mp * share, share, 0)
 
-    inputs = tokens_pair.astype(F32)
-    normed_one = (norm_parts(inputs)[0] * gain_one).astype(BF16)
     raw = dot(normed_one, attn_full[:, :attn_cols])
     starts = sum((docs < i).sum(1, keepdims=True) * (docs == i) for i in range(1, 4))
     positions = (jnp.arange(seq_length, dtype=jnp.int32)[None] - starts).reshape(pair_rows)
     cosine, sine = rope_tables(positions, head)
     starts = starts.reshape(pair_rows, 1).astype(jnp.int32)
     raw, cot_part = lax.optimization_barrier((raw, cot_part))
-    cot_pieces = in_order(mp // 2, cot_part[None], mp_swap(cot_part, 2)[None], 0)
+    cot_across = mp_swap(cot_part, 2)
     attention_args = (raw, cosine, sine, starts, gain_query, gain_key)
     pair_flops = pair_rows * seq_length * query_cols
     attended = call_attention(
@@ -847,24 +1129,42 @@
         [pltpu.VMEM((seq_length, query_cols), BF16), pltpu.VMEM((seq_length, head), BF16)],
         2 * pair_flops,
     )(*attention_args)
-    attended, cot_pieces = lax.optimization_barrier((attended, cot_pieces))
-    cot_pieces = in_order(mp % 2, cot_pieces[:, None], mp_swap(cot_pieces, 1)[:, None], 1)
-    cot_pair = jnp.concatenate([cotangent, cot_pieces.reshape(rows, width)], 0)
-    out_mat = attn_full[:, attn_cols:]
-    attn_part = dot(attended, out_mat, 1, 1).astype(BF16)
-
-    grouped = (2, 2, 2, share, width)
-    reduce_scratch, gather_scratch = Reduce.scratch(share, width), Gather.scratch(share, width)
-    hidden, normed_two = call_leg(
+    attended, cot_across = lax.optimization_barrier((attended, cot_across))
+
+    def grouped(cols):
+        return (2, 2, 2, share, cols)
+
+    half_width = width // 2
+    leg_scratch = Reduce.scratch(share, width, half_width) + Gather.scratch(share, width)
+    hidden, normed_two, cot_pair = call_leg(
         attention_leg,
         0,
         "attention_leg",
-        [ANY, VM, VM],
-        (jax.ShapeDtypeStruct((share, width), F32), jax.ShapeDtypeStruct(grouped, BF16)),
-        (VM, ANY),
-        reduce_scratch + gather_scratch,
+        [VM] * 4 + [ANY] * 3,
+        (
+            jax.ShapeDtypeStruct((share, width), F32),
+            jax.ShapeDtypeStruct(grouped(width), BF16),
+            jax.ShapeDtypeStruct((pair_rows, width), BF16),
+        ),
+        (VM, ANY, ANY),
+        [
+            pltpu.VMEM((rows + 2 * share, width), BF16),
+            pltpu.SemaphoreType.DMA((3,)),
+            pltpu.SemaphoreType.DMA((3,)),
+            pltpu.SemaphoreType.DMA((2,)),
+            pltpu.SemaphoreType.DMA((2,)),
+        ]
+        + leg_scratch,
         200 * MIB,
-    )(attn_part.reshape(grouped), tokens_share, gain_two)
+    )(
+        attended.reshape(grouped(query_cols)),
+        attn_full,
+        tokens_share,
+        gain_two,
+        cotangent,
+        cot_part,
+        cot_across,
+    )
     normed_two = normed_two.reshape(pair_rows, width)
 
     gate_up = dot(normed_two, gate_up_full)
@@ -874,7 +1174,6 @@
     active = (swish * up_pre).astype(BF16)
     down_part = dot(cot_pair, active, 0, 0).astype(BF16)
     down_grad = slab_scatter(down_part)
-    mlp_part = dot(active, down_full, 1, 1).astype(BF16)
     cot_late, _ = lax.optimization_barrier((cot_pair, down_part))
     grad_active = dot(cot_late, down_full)
     grad_gate = (grad_active * up_pre * sigmoid * (1.0 + gate_pre * (1.0 - sigmoid))).astype(BF16)
@@ -883,26 +1182,30 @@
     gate_up_part = dot(normed_two, grad_gate_up, 0, 0).astype(BF16)
     gate_up_grad = slab_scatter(gate_up_part)
     grad_gate_up, _, _ = lax.optimization_barrier((grad_gate_up, gate_up_part, down_part))
-    normed_two_part = dot(grad_gate_up, gate_up_full, 1, 1).astype(BF16)
-
     grad_hidden, mlp_gain_part, grad_hidden_low = call_leg(
         hidden_leg,
         1,
         "hidden_leg",
-        [ANY, VM, VM, VM],
+        [VM] * 5,
         (
             jax.ShapeDtypeStruct((share, width), F32),
             jax.ShapeDtypeStruct((1, width), F32),
-            jax.ShapeDtypeStruct(grouped, BF16),
+            jax.ShapeDtypeStruct(grouped(width), BF16),
         ),
         (VM, VM, ANY),
-        reduce_scratch + gather_scratch,
+        leg_scratch,
         200 * MIB,
-    )(normed_two_part.reshape(grouped), hidden, cot_share, gain_two)
+    )(
+        grad_gate_up.reshape(grouped(2 * hidden_cols)),
+        gate_up_full,
+        hidden,
+        cot_share,
+        gain_two,
+    )
     grad_hidden_low = grad_hidden_low.reshape(pair_rows, width)
 
     output_grad = dot(grad_hidden_low, attended, 0, 0).astype(BF16)
-    grad_attended = dot(grad_hidden_low, out_mat).astype(BF16)
+    grad_attended = dot(grad_hidden_low, attn_full[:, attn_cols:]).astype(BF16)
     raw_grad, head_gain_parts = call_attention(
         attend_backward,
         seq_length,
@@ -927,37 +1230,57 @@
     )(*attention_args, grad_attended)
     head_gain_parts = head_gain_parts.sum(0)
     attn_grad = jnp.concatenate([dot(normed_one, raw_grad, 0, 0).astype(BF16), output_grad], 1)
-    attn_grad, gate_up_grad, down_grad = lax.optimization_barrier(
-        (attn_grad, gate_up_grad, down_grad)
+    attn_grad, raw_grad, gate_up_grad, down_grad = lax.optimization_barrier(
+        (attn_grad, raw_grad, gate_up_grad, down_grad)
     )
     attn_grad = slab_scatter(attn_grad)
-    normed_one_part = dot(raw_grad, attn_full[:, :attn_cols], 1, 1).astype(BF16)
-
-    input_grad, layer_output, attn_gain_part = call_leg(
+
+    gain_parts = gain_rows(
+        jnp.zeros((n_dp, n_gain), F32),
+        mlp_gain_part.reshape(n_dp, n_gain),
+        head_gain_parts[0].reshape(n_dp, n_head),
+        head_gain_parts[1].reshape(n_dp, n_head),
+    )
+    low = 3 * width // 4
+    input_grad, layer_output, gain_sums, gate_grad, up_grad, down_grad = call_leg(
         output_leg,
         2,
         "output_leg",
-        [ANY, ANY, VM, VM, VM, VM],
+        [VM] * 11,
         (
             jax.ShapeDtypeStruct((share, width), F32),
             jax.ShapeDtypeStruct((share, width), BF16),
-            jax.ShapeDtypeStruct((1, width), F32),
+            jax.ShapeDtypeStruct((8, 128), F32),
+            jax.ShapeDtypeStruct(gate_weight.shape, F32),
+            jax.ShapeDtypeStruct(up_weight.shape, F32),
+            jax.ShapeDtypeStruct(down_weight.shape, F32),
         ),
-        (VM, VM, VM),
-        reduce_scratch + reduce_scratch,
+        (VM,) * 6,
+        [
+            pltpu.VMEM((2, 2, share, width), BF16),
+            pltpu.VMEM((1, width), F32),
+            pltpu.VMEM((n_dp, 8, 128), F32),
+            pltpu.VMEM((model_rows, 2 * hidden_cols), BF16),
+            pltpu.VMEM((model_rows, hidden_cols), BF16),
+            pltpu.SemaphoreType.DMA((2,)),
+            pltpu.SemaphoreType.DMA((2,)),
+        ]
+        + Reduce.scratch(share, width, low, False) * 2
+        + SumGains.scratch(n_dp, 4),
         200 * MIB,
     )(
-        normed_one_part.reshape(grouped),
-        mlp_part.reshape(grouped),
+        raw_grad.reshape(grouped(attn_cols)),
+        attn_full,
+        active.reshape(grouped(hidden_cols)),
+        down_full,
         tokens_share,
         hidden,
         grad_hidden,
         gain_one,
-    )
-
-    def back(values):
-        other = y_swap(half(values, 1 - y, 0)).astype(F32)
-        return half(values, y, 0).astype(F32), other
+        gain_parts,
+        gate_up_grad,
+        down_grad,
+    )
 
     query_grad, key_grad, value_grad, output_grad = call_leg(
         finish_attention,
@@ -976,39 +1299,6 @@
         ],
         3 * MIB,
     )(attn_grad)
-    gate_up_own, gate_up_other = back(gate_up_grad)
-    down_own, down_other = back(down_grad)
-
-    def columns(own, other, start, size, axis=1):
-        own, other = own[:, start : start + size], other[:, start : start + size]
-        if axis == 0:
-            own, other = own.T, other.T
-        return in_order(y, own, other, axis)
-
-    gain_parts = gain_rows(
-        attn_gain_part.reshape(-1, n_gain),
-        mlp_gain_part.reshape(-1, n_gain),
-        head_gain_parts[0].reshape(-1, n_head),
-        head_gain_parts[1].reshape(-1, n_head),
-    )
-    gain_sums = call_leg(
-        sum_gains,
-        4,
-        "sum_gains",
-        [VM],
-        jax.ShapeDtypeStruct((8, 128), F32),
-        VM,
-        [
-            pltpu.VMEM((n_dp, 8, 128), F32),
-            pltpu.VMEM((8, 128), F32),
-            pltpu.VMEM((3, 8, 128), F32),
-            pltpu.SemaphoreType.DMA((n_dp,)),
-            pltpu.SemaphoreType.DMA((n_dp,)),
-            pltpu.SemaphoreType.DMA((4,)),
-            pltpu.SemaphoreType.DMA((4,)),
-        ],
-        1 * MIB,
-    )(gain_parts)
     attn_gain_grad, mlp_gain_grad, query_gain_grad, key_gain_grad = gain_parts_of(gain_sums)
     return (
         layer_output,
@@ -1021,9 +1311,9 @@
         value_grad,
         output_grad,
         mlp_gain_grad,
-        columns(gate_up_own, gate_up_other, 0, hidden_cols),
-        columns(gate_up_own, gate_up_other, hidden_cols, hidden_cols),
-        columns(down_own, down_other, 0, hidden_cols, 0),
+        gate_grad,
+        up_grad,
+        down_grad,
     )
 
 

time: 643 us -> 575 us (0.89)
  matrix products: 133 us -> 89.3 us
  other arithmetic: 47.1 us -> 19 us
  Pallas kernels: 375 us -> 396 us
  waiting for transfers between devices: 25 us -> 13.9 us
    dot_general x12 -> x8, matrix products: 133 us -> 89.3 us  [dot(): lax.dot_general(left, right, (((left_dim,), (right_dim,)), ((), ())), pre...]
    pallas_call x6 -> x4, Pallas kernels: 324 us -> 349 us  [the longest x1 102 us: on_device(): call_leg(output_leg, 2, 'output_leg', [VM] * 11, (jax.ShapeDtypeStruct((s...]
    ppermute x3 -> x1, waiting for transfers between devices: 24.9 us -> 6.82 us  [y_swap(): return lax.ppermute(values, 'dp', [(i, i ^ 1) for i in range(n_dp)])]
    select_n x7 -> x0, other arithmetic: 11.6 us -> none  [in_order(): jnp.where(where == 0, jnp.concatenate([mine, other], axis), jnp.concatena...]
    concatenate x2 -> x0, other arithmetic: 9.38 us -> none  [the longest x1 8.45 us: on_device(): cot_pair = jnp.concatenate([cotangent, cot_pieces.reshape(rows, width)], 0)]
    unnamed x77 -> x50, local copies, waits for them, and re-layouts: 20 us -> 23.1 us
  transfers between devices with their start and end apart: 11 -> 7, of which waited for: 3 -> 3; matrix products, arithmetic and copies ran while one was open for 31% -> 21% of each run, Pallas kernels for 54% -> 55%
where the time goes in v3:
time: 575 us; the launch traced here: 571 us
  Pallas kernels  396 us (69%)
  matrix products  89.3 us (16%)
  local copies, waits for them, and re-layouts  35 us (6%)
  other arithmetic  19 us (3%)
  between operations  14.5 us (3%)
  waiting for transfers between devices  13.9 us (2%)
    pallas_call x1, Pallas kernels, on_device(): call_leg(output_leg, 2, 'output_leg', [VM] * 11, (jax.ShapeDtypeStruct((s...  102 us
    pallas_call x1, Pallas kernels, on_device(): call_leg(hidden_leg, 1, 'hidden_leg', [VM] * 5, (jax.ShapeDtypeStruct((sh...  92.5 us
    dot_general x8, matrix products, dot(): lax.dot_general(left, right, (((left_dim,), (right_dim,)), ((), ())), pre...  89.3 us
    pallas_call x1, Pallas kernels, on_device(): call_leg(attention_leg, 0, 'attention_leg', [VM] * 4 + [ANY] * 3, (jax.Sh...  82.7 us
    pallas_call x1, Pallas kernels, on_device(): call_leg(front, 3, 'front', [VM] * 6 + [ANY] * 4, (jax.ShapeDtypeStruct((...  71.5 us
    unnamed x50, local copies, waits for them, and re-layouts  23.1 us
    pallas_call x1, Pallas kernels, on_device(): call_attention(attend_backward, seq_length, pair_rows, (jax.ShapeDtypeStr...  22.2 us
    pallas_call x1, Pallas kernels, on_device(): call_attention(attend_forward, seq_length, pair_rows, jax.ShapeDtypeStruc...  15.4 us
  transfers between devices with their start and end apart: 7, of which 3 were waited for; matrix products, arithmetic and copies ran while one was open for 21% of the time, Pallas kernels for 55%

profile of v3, /device:TPU:0, one launch (start us, length us, event | category | flops | bytes accessed | tf_op | source)
XLA Modules:
  0.0 570.7 jit_solution(16958537404067685730)
XLA Ops:
  7.2 0.0 all-gather.3.cloned.1.call-start
  7.2 0.7 convert_element_type.71
  7.9 0.7 convert_element_type.72
  8.5 0.7 convert_bitcast_fusion.1
  9.2 0.6 fusion.17.gain
  9.9 71.5 %front.1 = (bf16[2048,768]{1,0:T(8,128)(2,1)}, f32[8,8,128]{2,1,0:T(8,128)}, s32[1,1024]{1,0:T(1,128)}, bf16[2048,2048]{1,0:T(8,128)(2,1)}, bf16[512,1536]{1,0:T(8,128)(2,1)}, /*index=5*/bf16[512,768]{1,0:T(8,128)(2,1)}) custom-call(f32[256,512]{1,0:T(8,128)} %q.1, f32[256,256]{1,0:T(8,128)} %k.1, f32[256,256]{1,0:T(8,128)} %v.1, f32[512,256]{1,0:T(8,128)} %o.1, ...), custom_call_target="tpu_custom_call" | custom-call | bytes 262144000 | tf_op jit(solution)/shard_map/front/pallas_call | solution.py:1059
  81.4 0.0 all-gather.5.cloned.1.call-start
  81.4 2.5 constant_dynamic-slice_fusion.1.cotangent
  83.9 0.9 collective-permute-start
  84.8 0.0 reduce-scatter.6.cloned.1.call-start
  84.9 0.8 fusion.7
  85.8 0.9 fusion.20
  86.6 1.4 fusion.19
  88.0 2.4 constant_dynamic-slice_fusion.tokens
  90.5 0.1 convert_bitcast_fusion
  90.6 1.3 copy.42
  92.0 0.6 reshape.236.gain_query
  92.5 0.6 reshape.238.gain_key
  93.1 9.7 %fusion.1.raw = f32[2048,512]{1,0:T(8,128)} fusion(bf16[2048,2048]{1,0:T(8,128)(2,1)} %get-tuple-element.48, bf16[2048,768]{1,0:T(8,128)(2,1)S(1)} %copy-done.1), kind=kOutput, calls=%fused_computation.12 | convolution fusion | flops 4294967296 | bytes 14680064 | tf_op jit(solution)/shard_map/dot_general | solution.py:46
  102.8 6.8 %collective-permute-done.cot_part = bf16[256,2048]{1,0:T(8,128)(2,1)} collective-permute-done((bf16[256,2048]{1,0:T(8,128)(2,1)}, bf16[256,2048]{1,0:T(8,128)(2,1)}, u32[]{:S(2)}, u32[]{:S(2)}) %collective-permute-start) | collective-permute-done | bytes 1048608 | tf_op jit(solution)/shard_map/ppermute | solution.py:1005
  109.6 1.4 collective-permute-start.1
  111.1 3.7 fusion.4
  114.8 1.3 pad_maximum_fusion.2.cosine
  116.1 1.3 pad_maximum_fusion.3.sine
  117.4 15.4 %attend_forward.1 = bf16[2048,256]{1,0:T(8,128)(2,1)} custom-call(f32[2048,512]{1,0:T(8,128)} %fusion.1.raw, f32[2048,128]{1,0:T(8,128)} %pad_maximum_fusion.2.cosine, f32[2048,128]{1,0:T(8,128)} %pad_maximum_fusion.3.sine, s32[2048,1]{1,0:T(8,128)} %bitcast.56, f32[1,128]{1,0:T(1,128)} %reshape.236.gain_query, f32[1,128]{1,0:T(1,128)} %reshape.238.gain_key), custom_call_target="tpu_custom_call" | custom-call | flops 1073741824 | bytes 8388608 | tf_op jit(solution)/shard_map/attend_forward/pallas_call | solution.py:1123
  132.8 1.7 collective-permute-done.1.cot_across
  134.5 1.0 copy-done.9
  135.5 82.7 %attention_leg.1 = (f32[256,2048]{1,0:T(8,128)}, bf16[2,2,2,256,2048]{4,3,2,1,0:T(8,128)(2,1)}, bf16[2048,2048]{1,0:T(8,128)(2,1)}) custom-call(bf16[2,2,2,256,256]{4,3,2,1,0:T(8,128)(2,1)} %bitcast.55, bf16[2048,768]{1,0:T(8,128)(2,1)} %get-tuple-element.49.packed, bf16[256,2048]{1,0:T(8,128)(2,1)} %constant_dynamic-slice_fusion.tokens, ...), custom_call_target="tpu_custom_call" | custom-call | bytes 209715200 | tf_op jit(solution)/shard_map/attention_leg/pallas_call | solution.py:1139
  218.1 0.0 all-gather.3.cloned.1.call-done.right
  218.2 17.4 %fusion.21 = f32[2048,1536]{1,0:T(8,128)S(1)} fusion(bf16[2048,2048]{1,0:T(8,128)(2,1)} %bitcast.70, bf16[2048,1536]{1,0:T(8,128)(2,1)} %all-gather.3.cloned.1.call-done.right), kind=kOutput, calls=%fused_computation.59 | convolution fusion | flops 12884901888 | bytes 27262976 | tf_op jit(solution)/shard_map/dot_general | solution.py:46
  235.6 2.1 multiply_convert_fusion.2
  237.7 4.3 copy-done
  242.0 2.7 copy-done.18
  244.7 8.5 %convolution_convert_fusion.1 = bf16[2048,768]{1,0:T(8,128)(2,1)} fusion(bf16[2048,2048]{1,0:T(8,128)(2,1)S(1)} %copy-done.18, bf16[2048,768]{1,0:T(8,128)(2,1)S(1)} %multiply_convert_fusion.2), kind=kOutput, calls=%fused_computation.7 | convolution fusion | flops 6444023808 | bytes 14680064 | tf_op jit(solution)/shard_map/dot_general | solution.py:46
  253.2 0.0 reduce-scatter.4.cloned.1.call-start
  253.3 5.3 all-gather.5.cloned.1.call-done.mlp_right
  258.6 14.4 %multiply_convert_fusion.1 = (bf16[2048,768]{1,0:T(8,128)(2,1)S(1)}, bf16[2048,768]{1,0:T(8,128)(2,1)S(1)}) fusion(f32[2048,1536]{1,0:T(8,128)} %copy-done, bf16[2048,2048]{1,0:T(8,128)(2,1)} %get-tuple-element.60, bf16[2048,768]{1,0:T(8,128)(2,1)} %all-gather.5.cloned.1.call-done.mlp_right), kind=kOutput, calls=%fused_computation.3 | convolution fusion | flops 6462898176 | bytes 30408704 | tf_op jit(solution)/shard_map/dot_general | solution.py:46
  272.9 1.6 copy-done.4
  274.6 17.7 %convolution_convert_fusion = bf16[2048,1536]{1,0:T(8,128)(2,1)} fusion(bf16[2048,2048]{1,0:T(8,128)(2,1)} %bitcast.71, bf16[2048,768]{1,0:T(8,128)(2,1)S(1)} %get-tuple-element.91, bf16[2048,768]{1,0:T(8,128)(2,1)S(1)} %get-tuple-element.90), kind=kOutput, calls=%fused_computation | convolution fusion | flops 12900630528 | bytes 20971520 | tf_op jit(solution)/shard_map/dot_general | solution.py:46
  292.2 0.0 reduce-scatter.8.cloned.1.call-start
  292.3 5.0 pad_maximum_fusion
  297.3 92.5 %hidden_leg.1 = (f32[256,2048]{1,0:T(8,128)}, f32[1,2048]{1,0:T(1,128)}, bf16[2,2,2,256,2048]{4,3,2,1,0:T(8,128)(2,1)}) custom-call(bf16[2,2,2,256,1536]{4,3,2,1,0:T(8,128)(2,1)} %bitcast.53, bf16[2048,1536]{1,0:T(8,128)(2,1)} %all-gather.3.cloned.1.call-done.right, f32[256,2048]{1,0:T(8,128)} %get-tuple-element.63.hidden, ...), custom_call_target="tpu_custom_call" | custom-call | bytes 209715200 | tf_op jit(solution)/shard_map/hidden_leg/pallas_call | solution.py:1185
  389.8 6.9 %convolution_convert_fusion.4.grad = bf16[2048,256]{1,0:T(8,128)(2,1)} fusion(bf16[2048,2048]{1,0:T(8,128)(2,1)} %bitcast.72, bf16[2048,768]{1,0:T(8,128)(2,1)} %get-tuple-element.49.packed), kind=kOutput, calls=%fused_computation.11 | convolution fusion | flops 2148007936 | bytes 10485760 | tf_op jit(solution)/shard_map/dot_general | solution.py:46
  396.8 22.2 %attend_backward.1 = (bf16[2048,512]{1,0:T(8,128)(2,1)}, f32[2,8,128]{2,1,0:T(8,128)}) custom-call(f32[2048,512]{1,0:T(8,128)} %fusion.1.raw, f32[2048,128]{1,0:T(8,128)} %pad_maximum_fusion.2.cosine, f32[2048,128]{1,0:T(8,128)} %pad_maximum_fusion.3.sine, s32[2048,1]{1,0:T(8,128)} %bitcast.57, f32[1,128]{1,0:T(1,128)} %reshape.236.gain_query, ...), custom_call_target="tpu_custom_call" | custom-call | flops 2684354560 | bytes 8388608 | tf_op jit(solution)/shard_map/attend_backward/pallas_call | solution.py:1209
  419.0 6.0 %convolution_convert_fusion.3 = bf16[2048,256]{1,0:T(8,128)(2,1)S(1)} fusion(bf16[2048,2048]{1,0:T(8,128)(2,1)} %bitcast.73, bf16[2048,256]{1,0:T(8,128)(2,1)S(1)} %copy-done.3), kind=kOutput, calls=%fused_computation.10 | convolution fusion | flops 2148007936 | bytes 10485760 | tf_op jit(solution)/shard_map/dot_general | solution.py:46
  425.0 8.7 %convolution_convert_fusion.2 = bf16[2048,512]{1,0:T(8,128)(2,1)S(1)} fusion(bf16[2048,2048]{1,0:T(8,128)(2,1)} %get-tuple-element.48, bf16[2048,512]{1,0:T(8,128)(2,1)S(1)} %copy-done.5), kind=kOutput, calls=%fused_computation.9 | convolution fusion | flops 4296015872 | bytes 12582912 | tf_op jit(solution)/shard_map/dot_general | solution.py:46
  433.8 1.9 pad_maximum_fusion.1
  435.7 0.1 reshape_squeeze.6
  435.8 0.1 reshape_squeeze.7
  435.9 0.1 pad_maximum_fusion.4
  436.0 0.6 pad.32.gain_parts
  436.6 102.0 %output_leg.1 = (f32[256,2048]{1,0:T(8,128)}, bf16[256,2048]{1,0:T(8,128)(2,1)}, f32[8,128]{1,0:T(8,128)}, f32[256,1536]{1,0:T(8,128)}, f32[256,1536]{1,0:T(8,128)}, /*index=5*/f32[1536,256]{1,0:T(8,128)}) custom-call(bf16[2,2,2,256,512]{4,3,2,1,0:T(8,128)(2,1)} %bitcast.58, bf16[2048,768]{1,0:T(8,128)(2,1)} %get-tuple-element.49.packed, ...), custom_call_target="tpu_custom_call" | custom-call | bytes 209715200 | tf_op jit(solution)/shard_map/output_leg/pallas_call | solution.py:1245
  538.6 1.3 slice_bitcast_fusion.2
  539.9 1.3 slice_bitcast_fusion
  541.2 10.3 %finish_attention.1 = (f32[256,512]{1,0:T(8,128)}, f32[256,256]{1,0:T(8,128)}, f32[256,256]{1,0:T(8,128)}, f32[512,256]{1,0:T(8,128)}) custom-call(bf16[512,768]{1,0:T(8,128)(2,1)} %reduce-scatter.8.cloned.1.call-done.grads), custom_call_target="tpu_custom_call" | custom-call | bytes 3145728 | tf_op jit(solution)/shard_map/finish_attention/pallas_call | solution.py:1285
  551.5 2.5 copy.54
  554.0 3.3 copy.55
  557.3 0.8 copy.56
  558.1 0.7 copy.57
  558.8 0.7 copy.58
  559.5 0.8 copy.59
  560.3 1.1 copy.60
  561.4 1.1 copy.61
  562.6 1.1 copy.62
  (52 shorter events, 0.2 us)
Async XLA Ops:
  7.2 211.0 %all-gather.3.cloned.1.call-start = ((), (), s32[]{:S(2)}) async-start(), calls=%async_computation.3 | async-start | bytes 7864320 | tf_op jit(solution)/shard_map/all_gather | solution.py:1022
  9.9 75.0 %copy-start.14 = (s32[1,1024]{1,0:T(1,128)S(1)}, s32[1,1024]{1,0:T(1,128)}, u32[]{:S(2)}) copy-start(s32[1,1024]{1,0:T(1,128)} %docs.1) | copy-start | bytes 12292
  81.3 9.2 %copy-start.15 = (s32[1,1024]{1,0:T(1,128)S(1)}, s32[1,1024]{1,0:T(1,128)}, u32[]{:S(2)}) copy-start(s32[1,1024]{1,0:T(1,128)} %get-tuple-element.50) | copy-start | bytes 12292
  81.3 11.8 %copy-start.1 = (bf16[2048,768]{1,0:T(8,128)(2,1)S(1)}, bf16[2048,768]{1,0:T(8,128)(2,1)}, u32[]{:S(2)}) copy-start(bf16[2048,768]{1,0:T(8,128)(2,1)} %get-tuple-element.49.packed) | copy-start | bytes 9437188
  81.4 177.2 %all-gather.5.cloned.1.call-start = ((), (), s32[]{:S(2)}) async-start(), calls=%async_computation.4 | async-start | bytes 3932160 | tf_op jit(solution)/shard_map/all_gather | solution.py:1022
  83.9 25.8 %collective-permute-start = (bf16[256,2048]{1,0:T(8,128)(2,1)}, bf16[256,2048]{1,0:T(8,128)(2,1)}, u32[]{:S(2)}, u32[]{:S(2)}) collective-permute-start(bf16[256,2048]{1,0:T(8,128)(2,1)} %constant_dynamic-slice_fusion.1.cotangent), channel_id=1, source_target_pairs={{0,4},{4,0},{8,12},{12,8},{16,20},{20,16},{24,28},{28,24},{1,5},{5... | collective-permute-start | bytes 3145736 | tf_op jit(solution)/shard_map/ppermute | solution.py:1005
  84.8 350.8 %reduce-scatter.6.cloned.1.call-start = ((), (), s32[]{:S(2)}) async-start(), calls=%async_computation.6 | async-start | bytes 3932160 | tf_op jit(solution)/shard_map/reduce_scatter | solution.py:1025
  109.6 24.8 %collective-permute-start.1 = (bf16[256,2048]{1,0:T(8,128)(2,1)}, bf16[256,2048]{1,0:T(8,128)(2,1)S(1)}, u32[]{:S(2)}, u32[]{:S(2)}) collective-permute-start(bf16[256,2048]{1,0:T(8,128)(2,1)} %collective-permute-done.cot_part), channel_id=1, source_target_pairs={{0,2},{1,3},{2,0},{3,1},{4,6},{5,7},{6,4},{7,5},{8,10},{9,11},{10,... | collective-permute-start | bytes 3145736 | tf_op jit(solution)/shard_map/ppermute | solution.py:1008
  134.5 1.0 copy-start.9
  235.6 6.4 %copy-start = (f32[2048,1536]{1,0:T(8,128)}, f32[2048,1536]{1,0:T(8,128)S(1)}, u32[]{:S(2)}) copy-start(f32[2048,1536]{1,0:T(8,128)S(1)} %fusion.21) | copy-start | bytes 37748740
  235.6 9.1 %copy-start.18 = (bf16[2048,2048]{1,0:T(8,128)(2,1)S(1)}, bf16[2048,2048]{1,0:T(8,128)(2,1)}, u32[]{:S(2)}) copy-start(bf16[2048,2048]{1,0:T(8,128)(2,1)} %get-tuple-element.60) | copy-start | bytes 25165828
  242.0 11.2 %copy-start.2 = (bf16[2048,768]{1,0:T(8,128)(2,1)}, bf16[2048,768]{1,0:T(8,128)(2,1)S(1)}, u32[]{:S(2)}) copy-start(bf16[2048,768]{1,0:T(8,128)(2,1)S(1)} %multiply_convert_fusion.2) | copy-start | bytes 9437188
  253.2 182.4 %reduce-scatter.4.cloned.1.call-start = ((), (), s32[]{:S(2)}) async-start(), calls=%async_computation.5 | async-start | bytes 7864320 | tf_op jit(solution)/shard_map/reduce_scatter | solution.py:1025
  272.9 1.6 copy-start.4
  292.2 249.0 %reduce-scatter.8.cloned.1.call-start = ((), (), s32[]{:S(2)}) async-start(), calls=%async_computation.7 | async-start | bytes 3932160 | tf_op jit(solution)/shard_map/reduce_scatter | solution.py:1025
  396.8 22.2 %copy-start.3 = (bf16[2048,256]{1,0:T(8,128)(2,1)S(1)}, bf16[2048,256]{1,0:T(8,128)(2,1)}, u32[]{:S(2)}) copy-start(bf16[2048,256]{1,0:T(8,128)(2,1)} %attend_forward.1) | copy-start | bytes 3145732
  418.9 6.1 %copy-start.5 = (bf16[2048,512]{1,0:T(8,128)(2,1)S(1)}, bf16[2048,512]{1,0:T(8,128)(2,1)}, u32[]{:S(2)}) copy-start(bf16[2048,512]{1,0:T(8,128)(2,1)} %get-tuple-element.66) | copy-start | bytes 6291460
  433.7 2.0 copy-start.17
  433.7 2.2 copy-start.16
  538.6 21.7 %copy-start.8 = (f32[256,1536]{1,0:T(8,128)S(1)}, f32[256,1536]{1,0:T(8,128)}, u32[]{:S(2)}) copy-start(f32[256,1536]{1,0:T(8,128)} %get-tuple-element.130) | copy-start | bytes 4718596
  551.5 5.8 %copy-start.11 = (f32[256,512]{1,0:T(8,128)S(1)}, f32[256,512]{1,0:T(8,128)}, u32[]{:S(2)}) copy-start(f32[256,512]{1,0:T(8,128)} %get-tuple-element.125) | copy-start | bytes 1572868
  551.5 6.5 %copy-start.13 = (f32[256,256]{1,0:T(8,128)S(1)}, f32[256,256]{1,0:T(8,128)}, u32[]{:S(2)}) copy-start(f32[256,256]{1,0:T(8,128)} %get-tuple-element.126) | copy-start | bytes 786436
  551.5 7.2 %copy-start.12 = (f32[256,256]{1,0:T(8,128)S(1)}, f32[256,256]{1,0:T(8,128)}, u32[]{:S(2)}) copy-start(f32[256,256]{1,0:T(8,128)} %get-tuple-element.127) | copy-start | bytes 786436
  551.5 7.9 %copy-start.10 = (f32[512,256]{1,0:T(8,128)S(1)}, f32[512,256]{1,0:T(8,128)}, u32[]{:S(2)}) copy-start(f32[512,256]{1,0:T(8,128)} %get-tuple-element.128) | copy-start | bytes 1572868
  551.5 9.9 %copy-start.7 = (f32[256,1536]{1,0:T(8,128)S(1)}, f32[256,1536]{1,0:T(8,128)}, u32[]{:S(2)}) copy-start(f32[256,1536]{1,0:T(8,128)} %get-tuple-element.131) | copy-start | bytes 4718596
  554.0 8.6 %copy-start.6 = (f32[1536,256]{1,0:T(8,128)S(1)}, f32[1536,256]{1,0:T(8,128)}, u32[]{:S(2)}) copy-start(f32[1536,256]{1,0:T(8,128)} %get-tuple-element.132) | copy-start | bytes 4718596
Sparse Core Ops, SparseCore 0:
  81.5 113.6 all-gather.2
  196.8 61.7 all-gather.4
  260.9 58.8 reduce-scatter.5
  322.0 110.7 reduce-scatter.3
  435.8 59.9 reduce-scatter.7

commit v4 on v3

--- a/solution.py
+++ b/solution.py
@@ -48,7 +48,8 @@
     )
 
 
-CHUNKS = 2
+CHUNKS = 4
+FEW = 2
 TILE = 32
 COLUMNS = 512
 
@@ -92,28 +93,50 @@
 class Reduce:
     STAGES = 5
 
-    def __init__(self, left, right, low, part, mine, got, gx, gy, fx, fy, send, recv):
-        self.left, self.right, self.low = left, right, low
+    def __init__(self, left, right, low, part, mine, got, gx, gy, fx, fy, send, recv, load=None):
+        self.left, self.right, self.low, self.load = left, right, low, load
         self.refs = (part, mine, got, gx, gy, fx, fy, send, recv)
-        self.rows = mine.shape[2] // CHUNKS
+        self.chunks = send.shape[1]
+        self.rows = mine.shape[2] // self.chunks
         self.width = mine.shape[3]
 
     @staticmethod
-    def scratch(rows, width, low, part=True):
+    def scratch(rows, width, low, chunks=CHUNKS):
         high = width - low
-        return [pltpu.VMEM((2, 2, rows, width), BF16)] * part + [
+        return [
+            pltpu.VMEM((2, 2, rows, width), BF16),
             pltpu.VMEM((2, 2, rows, width), BF16),
             pltpu.VMEM((2, 2, rows, width), BF16),
             pltpu.VMEM((2, rows, low), BF16),
             pltpu.VMEM((2, rows, high), BF16),
             pltpu.VMEM((rows, high), BF16),
             pltpu.VMEM((rows, low), BF16),
-            pltpu.SemaphoreType.DMA((Reduce.STAGES, CHUNKS)),
-            pltpu.SemaphoreType.DMA((Reduce.STAGES, CHUNKS)),
+            pltpu.SemaphoreType.DMA((Reduce.STAGES, chunks)),
+            pltpu.SemaphoreType.DMA((Reduce.STAGES, chunks)),
         ]
 
     def lanes(self):
         return pl.ds(0, self.low), pl.ds(self.low, self.width - self.low)
+
+    def load_left(self, k, own):
+        source, _, sems, _ = self.load
+        core = neighbours()[1]
+        at = (slice(None), slice(None), core if own else 1 - core, pl.ds(k * self.rows, self.rows))
+        return pltpu.make_async_copy(source.at[at], self.left.at[at], sems.at[int(own), k])
+
+    def load_right(self, j):
+        _, source, _, sems = self.load
+        at = pl.ds(pl.multiple_of(j * COLUMNS, COLUMNS), COLUMNS)
+        return pltpu.make_async_copy(source.at[at], self.right.at[at], sems.at[j])
+
+    def start_loads(self):
+        self.load_left(0, False).start()
+        for j in range(self.width // COLUMNS):
+            self.load_right(j).start()
+        self.load_left(0, True).start()
+        for k in range(1, self.chunks):
+            for own in (False, True):
+                self.load_left(k, own).start()
 
     def copy(self, k, i):
         part, mine, got, gx, gy, fx, fy, send, recv = self.refs
@@ -137,8 +160,12 @@
         core = core if own else 1 - core
         rows = pl.ds(k * self.rows, self.rows)
         depth = self.left.shape[4]
+        if self.load is not None:
+            self.load_left(k, own).wait()
 
         def tile(j, carry):
+            if self.load is not None and k == 0 and not own:
+                self.load_right(j).wait()
             cols = pl.ds(pl.multiple_of(j * COLUMNS, COLUMNS), COLUMNS)
             left = self.left[:, :, core, rows, :].reshape(4 * self.rows, depth)
             product = dot(left, self.right[cols, :], 1, 1).astype(BF16)
@@ -160,7 +187,7 @@
         def add(i, carry):
             def step(rows):
                 at = (i // 2, i % 2, rows)
-                mine[at] = (mine[at].astype(F32) + got[at].astype(F32)).astype(BF16)
+                mine[at] = mine[at] + got[at]
 
             tiles(k * self.rows, self.rows, step)
             return carry
@@ -174,17 +201,22 @@
         x = neighbours()[0]
         low, high = self.lanes()
         self.copy(k, 1).wait_recv()
-        self.copy(k, 2).wait_recv()
-
-        def step(rows):
+
+        def step_low(rows):
             for i in range(2):
                 at = (i, x, rows, low)
-                mine[at] = (mine[at].astype(F32) + gx[i, rows].astype(F32)).astype(BF16)
+                mine[at] = mine[at] + gx[i, rows]
+
+        tiles(k * self.rows, self.rows, step_low)
+        self.copy(k, 3).start()
+        self.copy(k, 2).wait_recv()
+
+        def step_high(rows):
+            for i in range(2):
                 at = (0, i, rows, high)
-                mine[at] = (mine[at].astype(F32) + gy[i, rows].astype(F32)).astype(BF16)
-
-        tiles(k * self.rows, self.rows, step)
-        self.copy(k, 3).start()
+                mine[at] = mine[at] + gy[i, rows]
+
+        tiles(k * self.rows, self.rows, step_high)
         self.copy(k, 4).start()
 
     def arrive(self, k):
@@ -204,7 +236,7 @@
         )
 
     def finish(self):
-        for k in range(CHUNKS):
+        for k in range(self.chunks):
             for i in range(1, 5):
                 self.copy(k, i).wait_send()
 
@@ -285,8 +317,10 @@
     pass
 
 
-def leg(left, right, low, full, step, scratch, at_start=nothing, at_middle=nothing):
-    reduce = Reduce(left, right, low, *scratch[:N_REDUCE])
+def leg(left, right, low, full, step, scratch, at_start=nothing, at_middle=nothing, load=None):
+    reduce = Reduce(left, right, low, *scratch[:N_REDUCE], load=load)
+    if load is not None:
+        reduce.start_loads()
     gather = Gather(scratch[N_REDUCE], full, *scratch[N_REDUCE + 1 :])
     mine = scratch[N_REDUCE]
     greet(neighbours()[2:])
@@ -295,7 +329,6 @@
         if k == 0:
             meet(3)
         reduce.begin(k)
-    for k in range(CHUNKS):
         reduce.produce(k, True)
         reduce.first(k)
     at_start()
@@ -378,9 +411,21 @@
         copy.wait()
 
 
-def hidden_leg(left, right, hidden, cotangent, gain, grad_hidden, gain_grad, full, *scratch):
-    gain_grad[...] = jnp.zeros_like(gain_grad)
-
+def hidden_leg(
+    left,
+    right,
+    hidden,
+    cotangent,
+    gain,
+    grad_hidden,
+    gain_grad,
+    full,
+    left_held,
+    right_held,
+    left_sems,
+    right_sems,
+    *scratch
+):
     def step(rows, grad):
         hat, inv = norm_parts(hidden[rows])
         gain_grad[...] += jnp.sum(grad * hat, 0, keepdims=True)
@@ -388,7 +433,9 @@
         grad_hidden[rows] = grad
         return grad
 
-    leg(left, right, right.shape[0] // 2, full, step, scratch)
+    gain_grad[...] = jnp.zeros_like(gain_grad)
+    load = (left, right, left_sems, right_sems)
+    leg(left_held, right_held, right.shape[0] // 2, full, step, scratch, load=load)
 
 
 class SumGains:
@@ -466,108 +513,66 @@
 def output_leg(
     left,
     packed,
-    mlp_left,
-    mlp_right,
     tokens,
-    hidden,
-    grad_hidden,
     gain,
     gain_parts,
+    weight_grads,
+    grad_hidden,
     gate_up_grad,
-    down_grad,
     input_grad,
-    output,
     gain_total,
-    gate,
-    up,
-    down,
-    part,
-    gain_grad,
+    gate_up_other,
     slots,
-    gate_up_other,
-    down_other,
     swap_send,
     swap_recv,
     *scratch
 ):
-    low = scratch[2].shape[2]
-    n = N_REDUCE - 1
-    first = Reduce(left, packed.at[:, pl.ds(0, left.shape[4])], low, part, *scratch[:n])
-    second = Reduce(mlp_left, mlp_right, low, part, *scratch[n : 2 * n])
-    sums = SumGains(slots, gain_total, *scratch[2 * n :])
+    low = scratch[3].shape[2]
+    depth = left.shape[4]
+    right = packed.at[:, pl.ds(0, depth)]
+    reduce = Reduce(left, right, low, *scratch[:N_REDUCE])
+    sums = SumGains(slots, gain_total, *scratch[N_REDUCE:])
     y, y_peer = lax.axis_index("dp") % 2, neighbours()[4]
-    half = gate.shape[0]
-    mine, theirs = (pl.ds(pl.multiple_of(i * half, half), half) for i in (y, 1 - y))
-    swaps = [
-        remote(gate_up_grad.at[theirs], gate_up_other, swap_send.at[0], swap_recv.at[0], y_peer),
-        remote(down_grad.at[theirs], down_other, swap_send.at[1], swap_recv.at[1], y_peer),
-    ]
-
-    def place(source, down_source, which):
-        size = gate.shape[1] // 2
-        cols = pl.ds(pl.multiple_of(which * size, 128), size)
-        gate[:, cols] = source[:, :size].astype(F32)
-        up[:, cols] = source[:, size:].astype(F32)
-        down[cols, :] = down_source[...].T.astype(F32)
-
-    def step_grad(rows):
-        grad = first.take(rows)
+    half = gate_up_other.shape[0]
+    theirs = pl.ds(pl.multiple_of((1 - y) * half, half), half)
+    swap = remote(gate_up_grad.at[theirs], gate_up_other, swap_send, swap_recv, y_peer)
+
+    def step(rows):
+        grad = reduce.take(rows)
         hat, inv = norm_parts(tokens[rows].astype(F32))
-        gain_grad[...] += jnp.sum(grad * hat, 0, keepdims=True)
         input_grad[rows] = grad_hidden[rows] + norm_back(grad, hat, inv, gain[...])
 
-    def step_output(rows):
-        output[rows] = (hidden[rows] + second.take(rows)).astype(BF16)
-
     sums.greet()
-    gain_grad[...] = jnp.zeros_like(gain_grad)
     slots[...] = gain_parts[...]
-    for k in range(CHUNKS):
-        first.produce(k, False)
-        if k == 0:
-            meet(sums.n_dp + sums.n_mp - 2)
-        first.begin(k)
-    for k in range(CHUNKS):
-        first.produce(k, True)
-        first.first(k)
-    for copy in swaps:
-        copy.start()
-    for k in range(CHUNKS):
-        first.release(k)
-        second.produce(k, False)
-        second.begin(k)
-    for k in range(CHUNKS):
-        first.second(k)
-    for k in range(CHUNKS):
-        second.produce(k, True)
-        second.first(k)
-    for k in range(CHUNKS):
-        first.arrive(k)
-        tiles(k * first.rows, first.rows, step_grad)
-    owned = gain_grad.shape[1] // sums.n_dp
+    meet(sums.n_dp + sums.n_mp - 2)
+    swap.start()
+    for k in range(reduce.chunks):
+        reduce.produce(k, False)
+        reduce.begin(k)
+        reduce.produce(k, True)
+        reduce.first(k)
+    owned = weight_grads.shape[2]
+    diagonal = lax.broadcasted_iota(jnp.int32, (owned, owned), 0) == lax.broadcasted_iota(
+        jnp.int32, (owned, owned), 1
+    )
     for i in range(sums.n_dp):
-        for j in range(-(-owned // 128)):
-            size = min(128, owned - j * 128)
-            at = i * owned + j * 128
-            slots[i, j : j + 1, :size] = gain_grad[:, at : at + size]
+        product = dot(right[i * owned : (i + 1) * owned, :], weight_grads[i, :depth, :])
+        sums_of = jnp.sum(jnp.where(diagonal, product, 0.0), 0, keepdims=True)
+        sums_of = sums_of / gain[:, i * owned : (i + 1) * owned]
+        for j, size in gain_rows_of(owned):
+            slots[i, j : j + 1, :size] = sums_of[:, j * 128 : j * 128 + size]
     sums.begin()
-    place(gate_up_grad.at[mine], down_grad.at[mine], y)
-    for k in range(CHUNKS):
-        second.second(k)
+    for k in range(reduce.chunks):
+        reduce.second(k)
     sums.pass_on()
-    for copy in swaps:
-        copy.wait_recv()
-    place(gate_up_other, down_other, 1 - y)
-    for k in range(CHUNKS):
-        second.arrive(k)
-        tiles(k * second.rows, second.rows, step_output)
+    for k in range(reduce.chunks):
+        reduce.arrive(k)
+        tiles(k * reduce.rows, reduce.rows, step)
     sums.finish()
-    for k in range(CHUNKS):
-        second.release(k)
-    for copy in swaps:
-        copy.wait_send()
-    first.finish()
-    second.finish()
+    for k in range(reduce.chunks):
+        reduce.release(k)
+    swap.wait()
+    reduce.finish()
 
 
 ANY = pl.BlockSpec(memory_space=pl.ANY)
@@ -594,13 +599,13 @@
 
     def __init__(self, mine, other, send, recv):
         self.refs = (mine, other, send, recv)
-        self.rows = mine.shape[0] // 4 // CHUNKS
+        self.rows = mine.shape[0] // 4 // FEW
 
     @staticmethod
     def scratch():
         return [
-            pltpu.SemaphoreType.DMA((Spread.STAGES, CHUNKS)),
-            pltpu.SemaphoreType.DMA((Spread.STAGES, CHUNKS)),
+            pltpu.SemaphoreType.DMA((Spread.STAGES, FEW)),
+            pltpu.SemaphoreType.DMA((Spread.STAGES, FEW)),
         ]
 
     def copy(self, k, i):
@@ -626,9 +631,7 @@
         self.copy(k, 3).start()
 
     def finish(self):
-        for k in range(CHUNKS):
-            for i in (2, 3):
-                self.copy(k, i).wait_recv()
+        for k in range(FEW):
             for i in range(4):
                 self.copy(k, i).wait_send()
 
@@ -638,7 +641,10 @@
     k,
     v,
     o,
-    gain,
+    attn_gain,
+    mlp_gain,
+    query_gain,
+    key_gain,
     docs,
     tokens,
     gate,
@@ -647,10 +653,12 @@
     full,
     gains,
     docs_other,
-    normed,
+    normed_out,
     gate_up_mine,
     down_mine,
     stage,
+    gain,
+    normed,
     gate_up_stage,
     down_stage,
     tokens_mine,
@@ -659,6 +667,7 @@
     up_in,
     down_in,
     local,
+    stores,
     swap,
     gain_send,
     gain_recv,
@@ -751,13 +760,19 @@
         down_to[pl.ds(row, rows), :] = down_in[cols, :].astype(BF16).T
 
     fill(stage, 0, 1 - y)
+    row = 0
+    for values in (attn_gain, mlp_gain, query_gain, key_gain):
+        for j, size in gain_rows_of(values.shape[1]):
+            part = values[:, j * 128 : j * 128 + size]
+            gain[row : row + 1, :size] = part.astype(BF16).astype(F32)
+            row += 1
     meet(n_dp - 1 + 2)
     swapped.start()
     fill(full, block(z, y).start, y)
     ring(0, 0).start()
     docs_swapped.start()
     lax.fori_loop(1, n_dp, share, 0)
-    for c in range(CHUNKS):
+    for c in range(FEW):
         spread.copy(c, 0).start()
     gains[dp] = gain[...]
     for load in loads[1:]:
@@ -783,29 +798,50 @@
 
     total = tokens.shape[0]
     quarter = total // 4
+
+    def store(i):
+        at = pl.ds(i * quarter, quarter)
+        return pltpu.make_async_copy(normed.at[at], normed_out.at[at], stores.at[i])
+
+    def norm_mine(i):
+        norm(tokens_mine, 0, i * quarter, quarter)
+        store(i).start()
+
+    def norm_other():
+        for c in range(FEW):
+            for i in (2, 3):
+                spread.copy(c, i).wait_recv()
+        for i in range(4):
+            norm(tokens_other, total, i * quarter, quarter)
+            store(4 + i).start()
+
     loads[0].wait()
-    work = [functools.partial(norm, tokens_mine, 0, i * quarter, quarter) for i in range(4)]
-    work[0:0] = [functools.partial(fill_mlp, gate_up_mine, down_mine, mine.start, y)]
-    for c in range(CHUNKS):
-        work.append(functools.partial(spread.pass_on, c))
-    for c in range(CHUNKS):
-        work.append(functools.partial(spread.pass_last, c))
-    events = [(step, i) for step in range(n_slabs - 1) for i in range(2)]
-    if len(events) <= len(work):
-        for n, event in enumerate(events):
-            ring_next(*event)
-            if n < 2:
-                work.pop(0)()
-                work.pop(0)()
-            elif n < 4:
-                for _ in range(2):
-                    if work:
-                        work.pop(0)()
-        for job in work:
+    early = [functools.partial(fill_mlp, gate_up_mine, down_mine, mine.start, y)]
+    early += [functools.partial(norm_mine, i) for i in range(4)]
+    late = [functools.partial(spread.pass_on, c) for c in range(FEW)]
+    late += [functools.partial(spread.pass_last, c) for c in range(FEW)]
+
+    def run(jobs):
+        for job in jobs:
             job()
+
+    if n_slabs == 4:
+        ring_next(0, 0)
+        run(early[:3])
+        ring_next(0, 1)
+        run(early[3:])
+        spread.pass_on(0)
+        ring_next(1, 0)
+        spread.pass_on(1)
+        spread.pass_last(0)
+        ring_next(1, 1)
+        spread.pass_last(1)
+        norm_other()
+        ring_next(2, 0)
+        ring_next(2, 1)
     else:
-        for job in work:
-            job()
+        run(early)
+        run(late)
 
         def turn(step, carry):
             for i in range(2):
@@ -815,8 +851,10 @@
         lax.fori_loop(0, n_slabs - 2, turn, 0)
         for i in range(2):
             ring_next(n_slabs - 2, i)
+        norm_other()
     spread.finish()
-    norm(tokens_other, total, 0, total)
+    for i in range(8):
+        store(i).wait()
     docs_swapped.wait()
     swapped.wait_send()
     gate_up_swapped.wait()
@@ -834,33 +872,6 @@
     return [(j, min(128, size - j * 128)) for j in range(-(-size // 128))]
 
 
-def finish_attention(grads, q, k, v, o, other, send, recv):
-    dp, mp = lax.axis_index("dp"), lax.axis_index("mp")
-    y, y_peer = dp % 2, (dp + 1 - 2 * (dp % 2), mp)
-    rows = q.shape[0]
-    greet([y_peer])
-    meet(1)
-    theirs = pl.multiple_of((1 - y) * rows, rows)
-    swapped = remote(grads.at[pl.ds(theirs, rows)], other, send, recv, y_peer)
-    swapped.start()
-
-    def place(source, row, which):
-        at = 0
-        for w in (q, k, v):
-            size = w.shape[1] // 2
-            cols = pl.ds(pl.multiple_of(which * size, 128), size)
-            w[:, cols] = source[pl.ds(row, rows), at : at + size].astype(F32)
-            at += size
-        size = o.shape[0] // 2
-        part = source[pl.ds(row, rows), at : at + size].astype(F32).T
-        o[pl.ds(pl.multiple_of(which * size, 128), size), :] = part
-
-    place(grads, pl.multiple_of(y * rows, rows), y)
-    swapped.wait_recv()
-    place(other, 0, 1 - y)
-    swapped.wait_send()
-
-
 QUERY_BLOCK = 256
 LONGEST = 512
 
@@ -869,14 +880,21 @@
     return pltpu.roll(values, HEAD_WIDTH // 2, 1)
 
 
+def lane_mean(values):
+    high = values.astype(BF16)
+    low = (values - high.astype(F32)).astype(BF16)
+    share = jnp.full((HEAD_WIDTH, HEAD_WIDTH), 1.0 / HEAD_WIDTH, BF16)
+    return dot(high, share) + dot(low, share)
+
+
 def head_norm(raw, h):
-    return norm_parts(raw[:, h * HEAD_WIDTH : (h + 1) * HEAD_WIDTH])
-
-
-def rope_into(target, at, normed, cosine, sine):
-    target[:, at : at + HEAD_WIDTH] = (normed * cosine[...] + rolled(normed) * sine[...]).astype(
-        BF16
-    )
+    values = raw[:, h * HEAD_WIDTH : (h + 1) * HEAD_WIDTH]
+    scaling = lax.rsqrt(lane_mean(values * values) + EPSILON)
+    return (values * scaling, scaling)
+
+
+def rope_of(normed, cosine, sine):
+    return (normed * cosine[...] + rolled(normed) * sine[...]).astype(BF16)
 
 
 def blocks_of(length):
@@ -885,50 +903,161 @@
         yield slice(start, start + QUERY_BLOCK), slice(first, start + QUERY_BLOCK)
 
 
+def together(values, rows):
+    return values[:, rows].reshape(GROUP * QUERY_BLOCK, HEAD_WIDTH)
+
+
 def weights_of(query, key, starts, rows, cols):
-    scores = dot(query, key, 1, 1) * HEAD_WIDTH ** (-0.5)
-    query_index = rows.start + lax.broadcasted_iota(jnp.int32, scores.shape, 0)
-    key_index = cols.start + lax.broadcasted_iota(jnp.int32, scores.shape, 1)
+    size = cols.stop - cols.start
+    scores = dot(query, key, 1, 1).reshape(GROUP, QUERY_BLOCK, size)
+    shape = (QUERY_BLOCK, size)
+    query_index = rows.start + lax.broadcasted_iota(jnp.int32, shape, 0)
+    key_index = cols.start + lax.broadcasted_iota(jnp.int32, shape, 1)
     allowed = (key_index <= query_index) & (key_index >= starts[rows])
-    scores = jnp.where(allowed, scores, MASKED)
-    exponent = jnp.exp(scores - jnp.max(scores, -1, keepdims=True))
-    return exponent / jnp.sum(exponent, -1, keepdims=True)
+    scores = jnp.where(allowed[None], scores, MASKED)
+    highest = jnp.max(scores, -1, keepdims=True)
+    exponent = jnp.exp((scores - highest) * HEAD_WIDTH ** (-0.5))
+    weights = exponent * (1.0 / jnp.sum(exponent, -1, keepdims=True))
+    return weights.reshape(GROUP * QUERY_BLOCK, size)
+
+
+def prepare_heads(raw, cosine, sine, gain_query, gain_key, q, k):
+    for h in range(GROUP):
+        q[h] = rope_of(head_norm(raw, h)[0] * gain_query[...], cosine, sine)
+    k[...] = rope_of(head_norm(raw, GROUP)[0] * gain_key[...], cosine, sine)
 
 
 def attend_forward(raw, cosine, sine, starts, gain_query, gain_key, out, q, k):
-    for h in range(GROUP):
-        rope_into(q, h * HEAD_WIDTH, head_norm(raw, h)[0] * gain_query[...], cosine, sine)
-    rope_into(k, 0, head_norm(raw, GROUP)[0] * gain_key[...], cosine, sine)
+    prepare_heads(raw, cosine, sine, gain_query, gain_key, q, k)
     at = (GROUP + 1) * HEAD_WIDTH
     for rows, cols in blocks_of(raw.shape[0]):
+        weights = weights_of(together(q, rows), k[cols], starts, rows, cols).astype(BF16)
+        value = raw[cols, at : at + HEAD_WIDTH].astype(BF16)
+        result = dot(weights, value).astype(BF16).reshape(GROUP, QUERY_BLOCK, HEAD_WIDTH)
         for h in range(GROUP):
-            lanes = slice(h * HEAD_WIDTH, (h + 1) * HEAD_WIDTH)
-            weights = weights_of(q[rows, lanes], k[cols], starts, rows, cols).astype(BF16)
-            value = raw[cols, at : at + HEAD_WIDTH].astype(BF16)
-            out[rows, lanes] = dot(weights, value).astype(BF16)
+            out[rows, h * HEAD_WIDTH : (h + 1) * HEAD_WIDTH] = result[h]
 
 
 def attend_backward(
-    raw, cosine, sine, starts, gain_query, gain_key, grad, out, gains, q, k, v, dq, dk, dv
+    raw,
+    cosine,
+    sine,
+    starts,
+    gain_query,
+    gain_key,
+    grad_hidden,
+    normed,
+    attended,
+    packed,
+    mlp_left,
+    mlp_right,
+    hidden,
+    down_grad,
+    out,
+    gains,
+    weight_grads,
+    output,
+    down_other,
+    q,
+    k,
+    v,
+    dq,
+    dk,
+    dv,
+    grad,
+    total,
+    normed_held,
+    mlp_left_held,
+    mlp_right_held,
+    hidden_held,
+    loads,
+    swap,
+    *scratch
 ):
     factor = HEAD_WIDTH ** (-0.5)
     at = (GROUP + 1) * HEAD_WIDTH
-    for h in range(GROUP):
-        rope_into(q, h * HEAD_WIDTH, head_norm(raw, h)[0] * gain_query[...], cosine, sine)
-    rope_into(k, 0, head_norm(raw, GROUP)[0] * gain_key[...], cosine, sine)
+    inputs = (GROUP + 2) * HEAD_WIDTH
+    mlp = Reduce(mlp_left_held, mlp_right_held, mlp_right.shape[0] // 2, *scratch)
+    length = raw.shape[0]
+    here = pl.ds(pl.multiple_of(pl.program_id(0) * length, length), length)
+    normed_load = pltpu.make_async_copy(normed.at[here], normed_held, loads.at[0])
+    mlp_loads = [
+        pltpu.make_async_copy(source, target, loads.at[i + 1])
+        for i, (source, target) in enumerate(
+            ((mlp_left, mlp_left_held), (mlp_right, mlp_right_held), (hidden, hidden_held))
+        )
+    ]
+
+    theirs = pl.ds(
+        pl.multiple_of((1 - lax.axis_index("dp") % 2) * down_other.shape[0], down_other.shape[0]),
+        down_other.shape[0],
+    )
+    swapped = remote(down_grad.at[theirs], down_other, swap.at[0], swap.at[1], neighbours()[4])
+
+    def mlp_load():
+        greet(neighbours()[2:])
+        for load in mlp_loads:
+            load.start()
+
+    def mlp_begin():
+        for load in mlp_loads[:2]:
+            load.wait()
+        for c in range(FEW):
+            mlp.produce(c, False)
+            if c == 0:
+                meet(3)
+            mlp.begin(c)
+        swapped.start()
+
+    def mlp_first():
+        for c in range(FEW):
+            mlp.produce(c, True)
+            mlp.first(c)
+
+    def mlp_second():
+        for c in range(FEW):
+            mlp.second(c)
+
+    def mlp_end():
+        def step(rows):
+            output[rows] = (hidden_held[rows] + mlp.take(rows)).astype(BF16)
+
+        mlp_loads[2].wait()
+
+        for c in range(FEW):
+            mlp.arrive(c)
+            tiles(c * mlp.rows, mlp.rows, step)
+        for c in range(FEW):
+            mlp.release(c)
+        mlp.finish()
+        swapped.wait()
+
+    def at_step(step, job):
+        pl.when(pl.program_id(0) == step)(job)
+
+    at_step(0, mlp_load)
+    normed_load.start()
+    prepare_heads(raw, cosine, sine, gain_query, gain_key, q, k)
     v[...] = raw[:, at : at + HEAD_WIDTH].astype(BF16)
     dk[...] = jnp.zeros_like(dk)
     dv[...] = jnp.zeros_like(dv)
-    for rows, cols in blocks_of(raw.shape[0]):
-        for h in range(GROUP):
-            lanes = slice(h * HEAD_WIDTH, (h + 1) * HEAD_WIDTH)
-            weights = weights_of(q[rows, lanes], k[cols], starts, rows, cols)
-            grad_weights = dot(grad[rows, lanes], v[cols], 1, 1)
-            inner = jnp.sum(weights * grad_weights, -1, keepdims=True)
-            grad_scores = (weights * (grad_weights - inner)).astype(BF16)
-            dq[rows, lanes] = dot(grad_scores, k[cols]) * factor
-            dk[cols] += dot(grad_scores, q[rows, lanes], 0, 0) * factor
-            dv[cols] += dot(weights.astype(BF16), grad[rows, lanes], 0, 0)
+    for h in range(GROUP):
+        lanes = slice(inputs + h * HEAD_WIDTH, inputs + (h + 1) * HEAD_WIDTH)
+        grad[h] = dot(grad_hidden[...], packed[:, lanes]).astype(BF16)
+    at_step(0, mlp_begin)
+    for n, (rows, cols) in enumerate(blocks_of(length)):
+        query, block_grad = together(q, rows), together(grad, rows)
+        weights = weights_of(query, k[cols], starts, rows, cols)
+        grad_weights = dot(block_grad, v[cols], 1, 1)
+        inner = jnp.sum(weights * grad_weights, -1, keepdims=True)
+        grad_scores = (weights * (grad_weights - inner)).astype(BF16)
+        dq[:, rows] = (dot(grad_scores, k[cols]) * factor).reshape(GROUP, QUERY_BLOCK, HEAD_WIDTH)
+        dk[cols] += dot(grad_scores, query, 0, 0) * factor
+        dv[cols] += dot(weights.astype(BF16), block_grad, 0, 0)
+        if n == 0:
+            at_step(0, mlp_first)
+        if n == 1:
+            at_step(1, mlp_second)
     gains[...] = jnp.zeros_like(gains)
 
     def undo(rot_grad, h, gain, row):
@@ -936,37 +1065,91 @@
         hat, inv = head_norm(raw, h)
         gains[0, row : row + 1] += jnp.sum(normed_grad * hat, 0, keepdims=True)
         lanes = slice(h * HEAD_WIDTH, (h + 1) * HEAD_WIDTH)
-        out[:, lanes] = norm_back(normed_grad, hat, inv, gain[...]).astype(BF16)
+        scaled = normed_grad * gain[...]
+        out[:, lanes] = (inv * (scaled - hat * lane_mean(scaled * hat))).astype(BF16)
 
     for h in range(GROUP):
-        undo(dq[:, h * HEAD_WIDTH : (h + 1) * HEAD_WIDTH], h, gain_query, 0)
+        undo(dq[h], h, gain_query, 0)
     undo(dk[...], GROUP, gain_key, 1)
     out[:, at : at + HEAD_WIDTH] = dv[...].astype(BF16)
 
-
-def call_attention(kernel, length, rows, out_shape, out_specs, scratch, flops):
-    def seq(cols):
-        return pl.BlockSpec((length, cols), lambda i: (i, 0))
-
-    gain = pl.BlockSpec((1, HEAD_WIDTH), lambda i: (0, 0))
-    specs = [seq((GROUP + 2) * HEAD_WIDTH), seq(HEAD_WIDTH), seq(HEAD_WIDTH), seq(1), gain, gain]
-    if len(scratch) > 2:
-        specs.append(seq(GROUP * HEAD_WIDTH))
+    @pl.when(pl.program_id(0) == 0)
+    def _():
+        total[...] = jnp.zeros_like(total)
+
+    out_turned, attended_turned = out[...].T, attended[...].T
+    normed_load.wait()
+    for start in range(0, normed.shape[1], COLUMNS):
+        cols = slice(start, start + COLUMNS)
+        total[:inputs, cols] += dot(out_turned, normed_held[:, cols])
+        total[inputs:, cols] += dot(attended_turned, grad_hidden[:, cols])
+
+    @pl.when(pl.program_id(0) == pl.num_programs(0) - 1)
+    def _():
+        size = weight_grads.shape[2]
+        for i in range(weight_grads.shape[0]):
+            weight_grads[i] = total[:, i * size : (i + 1) * size].astype(BF16)
+
+    at_step(1, mlp_end)
+
+
+def once(spec):
+    return pl.BlockSpec(spec.block_shape, spec.index_map, pipeline_mode=pl.Buffered(1))
+
+
+def by_rows(rows, cols):
+    return pl.BlockSpec((rows, cols), lambda i: (i, 0))
+
+
+def whole(*shape):
+    return pl.BlockSpec(shape, lambda i: (0,) * len(shape))
+
+
+def call_blocks(
+    kernel, steps, in_specs, out_shape, out_specs, scratch, flops, bytes_accessed, **remote_params
+):
     return pl.pallas_call(
         kernel,
         out_shape=out_shape,
-        grid=(rows // length,),
-        in_specs=specs,
+        grid=(steps,),
+        in_specs=in_specs,
         out_specs=out_specs,
         scratch_shapes=scratch,
         name=kernel.__name__,
         cost_estimate=pl.CostEstimate(
-            flops=flops, bytes_accessed=8 * MIB, transcendentals=rows * length * GROUP // 2
+            flops=flops, bytes_accessed=bytes_accessed, transcendentals=0
         ),
         compiler_params=pltpu.CompilerParams(
-            dimension_semantics=("arbitrary",), vmem_limit_bytes=56 * MIB
+            dimension_semantics=("arbitrary",), vmem_limit_bytes=60 * MIB, **remote_params
         ),
     )
+
+
+TOKEN_BLOCK = 512
+HIDDEN_BLOCK = 256
+
+
+def mlp_forward(normed, weights, active, gate_slope, up_slope):
+    size = active.shape[1]
+    for start in range(0, size, HIDDEN_BLOCK):
+        cols = slice(start, start + HIDDEN_BLOCK)
+        gate = dot(normed[...], weights[:, cols])
+        up = dot(normed[...], weights[:, size + start : size + start + HIDDEN_BLOCK])
+        sigmoid = jax.nn.sigmoid(gate)
+        swish = gate * sigmoid
+        active[:, cols] = (swish * up).astype(BF16)
+        gate_slope[:, cols] = up * sigmoid * (1.0 + gate * (1.0 - sigmoid))
+        up_slope[:, cols] = swish
+
+
+def mlp_backward(cotangent, weights, gate_slope, up_slope, grads):
+    size = gate_slope.shape[1]
+    for start in range(0, size, HIDDEN_BLOCK):
+        cols = slice(start, start + HIDDEN_BLOCK)
+        grad = dot(cotangent[...], weights[:, cols])
+        grads[:, cols] = (grad * gate_slope[:, cols]).astype(BF16)
+        up_cols = slice(size + start, size + start + HIDDEN_BLOCK)
+        grads[:, up_cols] = (grad * up_slope[:, cols]).astype(BF16)
 
 
 def on_device(
@@ -1049,9 +1232,6 @@
             at += n
         return parts
 
-    my_gains = gain_rows(
-        *(g.astype(BF16).astype(F32) for g in (attn_gain, mlp_gain, query_gain, key_norm_scale))
-    )
     model_rows = query_weight.shape[0]
     pack_cols = attn_cols + query_cols
     pair_rows = 2 * rows
@@ -1060,7 +1240,7 @@
         front,
         3,
         "front",
-        [VM] * 6 + [ANY] * 4,
+        [VM] * 9 + [ANY] * 4,
         (
             jax.ShapeDtypeStruct((width, pack_cols), BF16),
             jax.ShapeDtypeStruct((n_dp, 8, 128), F32),
@@ -1069,9 +1249,11 @@
             jax.ShapeDtypeStruct((2 * model_rows, 2 * hidden_cols), BF16),
             jax.ShapeDtypeStruct((2 * model_rows, hidden_cols), BF16),
         ),
-        (VM,) * 6,
+        (VM, VM, VM, ANY, VM, VM),
         [
             pltpu.VMEM((model_rows, pack_cols), BF16),
+            pltpu.VMEM((8, 128), F32),
+            pltpu.VMEM((pair_rows, width), BF16),
             pltpu.VMEM((model_rows, 2 * hidden_cols), BF16),
             pltpu.VMEM((model_rows, hidden_cols), BF16),
             pltpu.VMEM((rows, width), BF16),
@@ -1080,6 +1262,7 @@
             pltpu.VMEM(up_weight.shape, F32),
             pltpu.VMEM(down_weight.shape, F32),
             pltpu.SemaphoreType.DMA((4,)),
+            pltpu.SemaphoreType.DMA((8,)),
             pltpu.SemaphoreType.DMA((2, 4)),
             pltpu.SemaphoreType.DMA((n_dp,)),
             pltpu.SemaphoreType.DMA((n_dp,)),
@@ -1093,7 +1276,10 @@
         key_projection,
         value_projection,
         output_weight,
-        my_gains,
+        attn_gain.reshape(1, -1),
+        mlp_gain.reshape(1, -1),
+        query_gain.reshape(1, -1),
+        key_norm_scale.reshape(1, -1),
         documents,
         tokens,
         gate_weight,
@@ -1116,18 +1302,27 @@
     positions = (jnp.arange(seq_length, dtype=jnp.int32)[None] - starts).reshape(pair_rows)
     cosine, sine = rope_tables(positions, head)
     starts = starts.reshape(pair_rows, 1).astype(jnp.int32)
-    raw, cot_part = lax.optimization_barrier((raw, cot_part))
+    raw, sine, cot_part = lax.optimization_barrier((raw, sine, cot_part))
     cot_across = mp_swap(cot_part, 2)
     attention_args = (raw, cosine, sine, starts, gain_query, gain_key)
+    attention_specs = [
+        by_rows(seq_length, attn_cols),
+        by_rows(seq_length, head),
+        by_rows(seq_length, head),
+        by_rows(seq_length, 1),
+        whole(1, head),
+        whole(1, head),
+    ]
     pair_flops = pair_rows * seq_length * query_cols
-    attended = call_attention(
+    attended = call_blocks(
         attend_forward,
-        seq_length,
-        pair_rows,
+        seqs,
+        attention_specs,
         jax.ShapeDtypeStruct((pair_rows, query_cols), BF16),
-        pl.BlockSpec((seq_length, query_cols), lambda i: (i, 0)),
-        [pltpu.VMEM((seq_length, query_cols), BF16), pltpu.VMEM((seq_length, head), BF16)],
+        by_rows(seq_length, query_cols),
+        [pltpu.VMEM((GROUP, seq_length, head), BF16), pltpu.VMEM((seq_length, head), BF16)],
         2 * pair_flops,
+        20 * MIB,
     )(*attention_args)
     attended, cot_across = lax.optimization_barrier((attended, cot_across))
 
@@ -1167,18 +1362,37 @@
     )
     normed_two = normed_two.reshape(pair_rows, width)
 
-    gate_up = dot(normed_two, gate_up_full)
-    gate_pre, up_pre = gate_up[:, :hidden_cols], gate_up[:, hidden_cols:]
-    sigmoid = jax.nn.sigmoid(gate_pre)
-    swish = gate_pre * sigmoid
-    active = (swish * up_pre).astype(BF16)
+    blocks = pair_rows // TOKEN_BLOCK
+    hidden_block = by_rows(TOKEN_BLOCK, hidden_cols)
+    hidden_shape = (pair_rows, hidden_cols)
+    mlp_flops = 2 * pair_rows * width * hidden_cols
+    active, gate_slope, up_slope = call_blocks(
+        mlp_forward,
+        blocks,
+        [by_rows(TOKEN_BLOCK, width), whole(width, 2 * hidden_cols)],
+        (
+            jax.ShapeDtypeStruct(hidden_shape, BF16),
+            jax.ShapeDtypeStruct(hidden_shape, F32),
+            jax.ShapeDtypeStruct(hidden_shape, F32),
+        ),
+        (hidden_block,) * 3,
+        [],
+        2 * mlp_flops,
+        30 * MIB,
+    )(normed_two, gate_up_full)
     down_part = dot(cot_pair, active, 0, 0).astype(BF16)
     down_grad = slab_scatter(down_part)
     cot_late, _ = lax.optimization_barrier((cot_pair, down_part))
-    grad_active = dot(cot_late, down_full)
-    grad_gate = (grad_active * up_pre * sigmoid * (1.0 + gate_pre * (1.0 - sigmoid))).astype(BF16)
-    grad_up = (grad_active * swish).astype(BF16)
-    grad_gate_up = jnp.concatenate([grad_gate, grad_up], 1)
+    grad_gate_up = call_blocks(
+        mlp_backward,
+        blocks,
+        [by_rows(TOKEN_BLOCK, width), whole(width, hidden_cols), hidden_block, hidden_block],
+        jax.ShapeDtypeStruct((pair_rows, 2 * hidden_cols), BF16),
+        by_rows(TOKEN_BLOCK, 2 * hidden_cols),
+        [],
+        mlp_flops,
+        30 * MIB,
+    )(cot_late, down_full, gate_slope, up_slope)
     gate_up_part = dot(normed_two, grad_gate_up, 0, 0).astype(BF16)
     gate_up_grad = slab_scatter(gate_up_part)
     grad_gate_up, _, _ = lax.optimization_barrier((grad_gate_up, gate_up_part, down_part))
@@ -1186,14 +1400,20 @@
         hidden_leg,
         1,
         "hidden_leg",
-        [VM] * 5,
+        [ANY] * 2 + [VM] * 3,
         (
             jax.ShapeDtypeStruct((share, width), F32),
             jax.ShapeDtypeStruct((1, width), F32),
             jax.ShapeDtypeStruct(grouped(width), BF16),
         ),
         (VM, VM, ANY),
-        leg_scratch,
+        [
+            pltpu.VMEM(grouped(2 * hidden_cols), BF16),
+            pltpu.VMEM((width, 2 * hidden_cols), BF16),
+            pltpu.SemaphoreType.DMA((2, CHUNKS)),
+            pltpu.SemaphoreType.DMA((width // COLUMNS,)),
+        ]
+        + leg_scratch,
         200 * MIB,
     )(
         grad_gate_up.reshape(grouped(2 * hidden_cols)),
@@ -1204,101 +1424,139 @@
     )
     grad_hidden_low = grad_hidden_low.reshape(pair_rows, width)
 
-    output_grad = dot(grad_hidden_low, attended, 0, 0).astype(BF16)
-    grad_attended = dot(grad_hidden_low, attn_full[:, attn_cols:]).astype(BF16)
-    raw_grad, head_gain_parts = call_attention(
+    raw_grad, head_gain_parts, attn_grad, layer_output, down_other = call_blocks(
         attend_backward,
-        seq_length,
-        pair_rows,
+        seqs,
+        [once(spec) for spec in attention_specs]
+        + [
+            once(by_rows(seq_length, width)),
+            ANY,
+            once(by_rows(seq_length, query_cols)),
+            once(whole(width, pack_cols)),
+            ANY,
+            ANY,
+            ANY,
+            ANY,
+        ],
         (
             jax.ShapeDtypeStruct((pair_rows, attn_cols), BF16),
             jax.ShapeDtypeStruct((seqs, 8, head), F32),
+            jax.ShapeDtypeStruct((n_dp, pack_cols, model_rows), BF16),
+            jax.ShapeDtypeStruct((share, width), BF16),
+            jax.ShapeDtypeStruct((model_rows, hidden_cols), BF16),
         ),
         (
-            pl.BlockSpec((seq_length, attn_cols), lambda i: (i, 0)),
+            once(by_rows(seq_length, attn_cols)),
             pl.BlockSpec((1, 8, head), lambda i: (i, 0, 0)),
+            once(whole(n_dp, pack_cols, model_rows)),
+            once(whole(share, width)),
+            ANY,
         ),
         [
-            pltpu.VMEM((seq_length, query_cols), BF16),
+            pltpu.VMEM((GROUP, seq_length, head), BF16),
             pltpu.VMEM((seq_length, head), BF16),
             pltpu.VMEM((seq_length, head), BF16),
-            pltpu.VMEM((seq_length, query_cols), F32),
+            pltpu.VMEM((GROUP, seq_length, head), F32),
             pltpu.VMEM((seq_length, head), F32),
             pltpu.VMEM((seq_length, head), F32),
-        ],
-        5 * pair_flops,
-    )(*attention_args, grad_attended)
+            pltpu.VMEM((GROUP, seq_length, head), BF16),
+            pltpu.VMEM((pack_cols, width), F32),
+            pltpu.VMEM((seq_length, width), BF16),
+            pltpu.VMEM(grouped(hidden_cols), BF16),
+            pltpu.VMEM((width, hidden_cols), BF16),
+            pltpu.VMEM((share, width), F32),
+            pltpu.SemaphoreType.DMA((4,)),
+            pltpu.SemaphoreType.DMA((2,)),
+        ]
+        + Reduce.scratch(share, width, half_width, FEW),
+        5 * pair_flops + 2 * pair_rows * width * (pack_cols + query_cols + hidden_cols),
+        80 * MIB,
+        collective_id=4,
+        has_side_effects=True,
+    )(
+        *attention_args,
+        grad_hidden_low,
+        normed_one,
+        attended,
+        attn_full,
+        active.reshape(grouped(hidden_cols)),
+        down_full,
+        hidden,
+        down_grad,
+    )
     head_gain_parts = head_gain_parts.sum(0)
-    attn_grad = jnp.concatenate([dot(normed_one, raw_grad, 0, 0).astype(BF16), output_grad], 1)
+    attn_grad = attn_grad.reshape(n_dp * pack_cols, model_rows)
     attn_grad, raw_grad, gate_up_grad, down_grad = lax.optimization_barrier(
         (attn_grad, raw_grad, gate_up_grad, down_grad)
     )
-    attn_grad = slab_scatter(attn_grad)
-
+    attn_parts = attn_grad.reshape(n_dp, pack_cols, model_rows)
+    attn_grad = slab_scatter(attn_grad).reshape(2, pack_cols, model_rows)
     gain_parts = gain_rows(
         jnp.zeros((n_dp, n_gain), F32),
         mlp_gain_part.reshape(n_dp, n_gain),
         head_gain_parts[0].reshape(n_dp, n_head),
         head_gain_parts[1].reshape(n_dp, n_head),
     )
+
     low = 3 * width // 4
-    input_grad, layer_output, gain_sums, gate_grad, up_grad, down_grad = call_leg(
+    input_grad, gain_sums, gate_up_other = call_leg(
         output_leg,
         2,
         "output_leg",
-        [VM] * 11,
+        [VM] * 7 + [ANY],
         (
             jax.ShapeDtypeStruct((share, width), F32),
-            jax.ShapeDtypeStruct((share, width), BF16),
             jax.ShapeDtypeStruct((8, 128), F32),
-            jax.ShapeDtypeStruct(gate_weight.shape, F32),
-            jax.ShapeDtypeStruct(up_weight.shape, F32),
-            jax.ShapeDtypeStruct(down_weight.shape, F32),
+            jax.ShapeDtypeStruct((model_rows, 2 * hidden_cols), BF16),
         ),
-        (VM,) * 6,
+        (VM, VM, ANY),
         [
-            pltpu.VMEM((2, 2, share, width), BF16),
-            pltpu.VMEM((1, width), F32),
             pltpu.VMEM((n_dp, 8, 128), F32),
-            pltpu.VMEM((model_rows, 2 * hidden_cols), BF16),
-            pltpu.VMEM((model_rows, hidden_cols), BF16),
-            pltpu.SemaphoreType.DMA((2,)),
-            pltpu.SemaphoreType.DMA((2,)),
+            pltpu.SemaphoreType.DMA,
+            pltpu.SemaphoreType.DMA,
         ]
-        + Reduce.scratch(share, width, low, False) * 2
+        + Reduce.scratch(share, width, low)
         + SumGains.scratch(n_dp, 4),
         200 * MIB,
     )(
         raw_grad.reshape(grouped(attn_cols)),
         attn_full,
-        active.reshape(grouped(hidden_cols)),
-        down_full,
         tokens_share,
-        hidden,
-        grad_hidden,
         gain_one,
         gain_parts,
+        attn_parts,
+        grad_hidden,
         gate_up_grad,
-        down_grad,
-    )
-
-    query_grad, key_grad, value_grad, output_grad = call_leg(
-        finish_attention,
-        5,
-        "finish_attention",
-        [VM],
-        tuple(
-            jax.ShapeDtypeStruct(w.shape, F32)
-            for w in (query_weight, key_projection, value_projection, output_weight)
-        ),
-        (VM,) * 4,
-        [
-            pltpu.VMEM((model_rows, pack_cols), BF16),
-            pltpu.SemaphoreType.DMA,
-            pltpu.SemaphoreType.DMA,
-        ],
-        3 * MIB,
-    )(attn_grad)
+    )
+    attn_given = lax.dynamic_index_in_dim(attn_grad, 1 - y, 0, False)
+    attn_given, gate_up_other, down_other = lax.optimization_barrier(
+        (attn_given, gate_up_other, down_other)
+    )
+
+    def columns(own, other, start, axis=1):
+        own = half(own, y, 0)[:, start : start + hidden_cols]
+        other = other[:, start : start + hidden_cols]
+        if axis == 0:
+            own, other = own.T, other.T
+        return in_order(y, own, other, axis).astype(F32)
+
+    gate_grad = columns(gate_up_grad, gate_up_other, 0)
+    up_grad = columns(gate_up_grad, gate_up_other, hidden_cols)
+    down_grad = columns(down_grad, down_other, 0, 0)
+
+    attn_other = y_swap(attn_given)
+    attn_own = lax.dynamic_index_in_dim(attn_grad, y, 0, False)
+
+    def attn_columns(start, size, turn=True):
+        own, other = attn_own[start : start + size], attn_other[start : start + size]
+        if turn:
+            own, other = own.T, other.T
+        return in_order(y, own, other, int(turn)).astype(F32)
+
+    query_grad = attn_columns(0, query_cols)
+    key_grad = attn_columns(query_cols, key_cols)
+    value_grad = attn_columns(query_cols + key_cols, key_cols)
+    output_grad = attn_columns(attn_cols, query_cols, False)
     attn_gain_grad, mlp_gain_grad, query_gain_grad, key_gain_grad = gain_parts_of(gain_sums)
     return (
         layer_output,

time: 575 us -> 531 us (0.923); the launches traced: 571 us -> 521 us
  matrix products: 89.3 us -> 41 us
  waiting for transfers between devices: 13.9 us -> 28.9 us
  other arithmetic: 19 us -> 10.7 us
  local copies, waits for them, and re-layouts: 35 us -> 27.6 us
    dot_general x8 -> x3, matrix products: 89.3 us -> 41 us  [dot(): lax.dot_general(left, right, (((left_dim,), (right_dim,)), ((), ())), pre...]
    unnamed x50 -> x31, local copies, waits for them, and re-layouts: 23.1 us -> 10.9 us
    all_gather x2, waiting for transfers between devices: 5.34 us -> 14.4 us  [slab_gather(): lax.all_gather(values, 'dp', axis=0, tiled=True, axis_index_groups=slabs)]
    concatenate x2 -> x0, other arithmetic: 6.91 us -> none  [the longest x1 5.03 us: on_device(): grad_gate_up = jnp.concatenate([grad_gate, grad_up], 1)]
    pallas_call x6 -> x7, Pallas kernels: 314 us -> 313 us  [the longest x1 84.2 us: on_device(): call_leg(hidden_leg, 1, 'hidden_leg', [ANY] * 2 + [VM] * 3, (jax.ShapeDty...]
  transfers between devices with their start and end apart: 7 -> 8, of which waited for: 3 -> 4; matrix products, arithmetic and copies ran while one was open for 21% -> 13% of each run, Pallas kernels for 55% -> 63%
where the time goes in v4:
time: 531 us; the launch traced here: 521 us
  Pallas kernels  394 us (74%)
  matrix products  41 us (8%)
  waiting for transfers between devices  28.9 us (5%)
  local copies, waits for them, and re-layouts  27.6 us (5%)
  between operations  14.6 us (3%)
  other arithmetic  10.7 us (2%)
    pallas_call x1, Pallas kernels, on_device(): call_leg(hidden_leg, 1, 'hidden_leg', [ANY] * 2 + [VM] * 3, (jax.ShapeDty...  84.2 us
    pallas_call x1, Pallas kernels, on_device(): call_leg(attention_leg, 0, 'attention_leg', [VM] * 4 + [ANY] * 3, (jax.Sh...  80.3 us
    pallas_call x1, Pallas kernels, on_device(): call_leg(front, 3, 'front', [VM] * 9 + [ANY] * 4, (jax.ShapeDtypeStruct((...  68 us
    pallas_call x1, Pallas kernels, on_device(): call_blocks(attend_backward, seqs, [once(spec) for spec in attention_spec...  60.7 us
    pallas_call x1, Pallas kernels, on_device(): call_leg(output_leg, 2, 'output_leg', [VM] * 7 + [ANY], (jax.ShapeDtypeSt...  55.6 us
    dot_general x3, matrix products, dot(): lax.dot_general(left, right, (((left_dim,), (right_dim,)), ((), ())), pre...  41 us
    pallas_call x1, Pallas kernels, on_device(): call_blocks(mlp_forward, blocks, [by_rows(TOKEN_BLOCK, width), whole(widt...  19.4 us
    pallas_call x1, Pallas kernels, on_device(): call_blocks(mlp_backward, blocks, [by_rows(TOKEN_BLOCK, width), whole(wid...  14.7 us
  transfers between devices with their start and end apart: 8, of which 4 were waited for; matrix products, arithmetic and copies ran while one was open for 13% of the time, Pallas kernels for 63%

profile of v4, /device:TPU:0, one launch (start us, length us, event | category | flops | bytes accessed | tf_op | source)
XLA Modules:
  0.0 520.7 jit_solution(766994397266063635)
XLA Ops:
  7.2 0.0 all-gather.3.cloned.1.call-start
  7.2 68.0 %front.1 = (bf16[2048,768]{1,0:T(8,128)(2,1)}, f32[8,8,128]{2,1,0:T(8,128)}, s32[1,1024]{1,0:T(1,128)}, bf16[2048,2048]{1,0:T(8,128)(2,1)}, bf16[512,1536]{1,0:T(8,128)(2,1)}, /*index=5*/bf16[512,768]{1,0:T(8,128)(2,1)}) custom-call(f32[256,512]{1,0:T(8,128)} %q.1, f32[256,256]{1,0:T(8,128)} %k.1, f32[256,256]{1,0:T(8,128)} %v.1, f32[512,256]{1,0:T(8,128)} %o.1, ...), custom_call_target="tpu_custom_call" | custom-call | bytes 262144000 | tf_op jit(solution)/shard_map/front/pallas_call | solution.py:1239
  75.3 0.0 all-gather.5.cloned.1.call-start
  75.3 2.5 constant_dynamic-slice_fusion.2.cotangent
  77.8 1.5 collective-permute-start
  79.3 0.0 reduce-scatter.4.cloned.1.call-start
  79.3 0.2 fusion.12
  79.5 10.4 %fusion.raw = f32[2048,512]{1,0:T(8,128)} fusion(bf16[2048,2048]{1,0:T(8,128)(2,1)} %get-tuple-element.51.normed, bf16[2048,768]{1,0:T(8,128)(2,1)S(1)} %copy-done), kind=kOutput, calls=%fused_computation.2 | convolution fusion | flops 4294967296 | bytes 14680064 | tf_op jit(solution)/shard_map/dot_general | solution.py:46
  89.9 0.1 convert_bitcast_fusion
  90.0 3.7 multiply_cosine_fusion
  93.8 1.3 copy.39
  95.1 1.3 pad_maximum_fusion.sine
  96.4 5.8 %collective-permute-done.cot_part = bf16[256,2048]{1,0:T(8,128)(2,1)} collective-permute-done((bf16[256,2048]{1,0:T(8,128)(2,1)}, bf16[256,2048]{1,0:T(8,128)(2,1)}, u32[]{:S(2)}, u32[]{:S(2)}) %collective-permute-start) | collective-permute-done | bytes 1048608 | tf_op jit(solution)/shard_map/ppermute | solution.py:1188
  102.2 1.5 collective-permute-start.1
  103.7 0.6 reshape.245.gain_query
  104.3 0.6 reshape.247.gain_key
  104.9 0.6 fusion.19
  105.5 2.3 constant_dynamic-slice_fusion.1.tokens
  107.8 1.3 pad_maximum_fusion.1.cosine
  109.1 10.8 %attend_forward.1.attended = bf16[2048,256]{1,0:T(8,128)(2,1)} custom-call(f32[2048,512]{1,0:T(8,128)} %fusion.raw, f32[2048,128]{1,0:T(8,128)} %pad_maximum_fusion.1.cosine, f32[2048,128]{1,0:T(8,128)} %pad_maximum_fusion.sine, s32[2048,1]{1,0:T(8,128)} %bitcast.72, f32[1,128]{1,0:T(1,128)} %reshape.245.gain_query, f32[1,128]{1,0:T(1,128)} %reshape.247.gain_key), custom_call_target="tpu_custom_call" | custom-call | flops 1073741824 | bytes 20971520 | tf_op jit(solution)/shard_map/attend_forward/pallas_call | solution.py:1317
  119.9 5.7 %collective-permute-done.1.cot_across = bf16[256,2048]{1,0:T(8,128)(2,1)S(1)} collective-permute-done((bf16[256,2048]{1,0:T(8,128)(2,1)}, bf16[256,2048]{1,0:T(8,128)(2,1)S(1)}, u32[]{:S(2)}, u32[]{:S(2)}) %collective-permute-start.1) | collective-permute-done | bytes 1048608 | tf_op jit(solution)/shard_map/ppermute | solution.py:1191
  125.6 1.0 copy-done.3
  126.6 80.3 %attention_leg.1 = (f32[256,2048]{1,0:T(8,128)}, bf16[2,2,2,256,2048]{4,3,2,1,0:T(8,128)(2,1)}, bf16[2048,2048]{1,0:T(8,128)(2,1)}) custom-call(bf16[2,2,2,256,256]{4,3,2,1,0:T(8,128)(2,1)} %bitcast.71, bf16[2048,768]{1,0:T(8,128)(2,1)} %get-tuple-element.52.packed, bf16[256,2048]{1,0:T(8,128)(2,1)} %constant_dynamic-slice_fusion.1.tokens, ...), custom_call_target="tpu_custom_call" | custom-call | bytes 209715200 | tf_op jit(solution)/shard_map/attention_leg/pallas_call | solution.py:1334
  206.9 0.0 all-gather.3.cloned.1.call-done.weights.right
  206.9 19.4 %mlp_forward.1 = (bf16[2048,768]{1,0:T(8,128)(2,1)}, f32[2048,768]{1,0:T(8,128)}, f32[2048,768]{1,0:T(8,128)}) custom-call(bf16[2048,2048]{1,0:T(8,128)(2,1)} %bitcast.94, bf16[2048,1536]{1,0:T(8,128)(2,1)} %all-gather.3.cloned.1.call-done.weights.right), custom_call_target="tpu_custom_call" | custom-call | flops 12884901888 | bytes 31457280 | tf_op jit(solution)/shard_map/mlp_forward/pallas_call | solution.py:1369
  226.4 11.4 %convolution_convert_fusion.1 = bf16[2048,768]{1,0:T(8,128)(2,1)} fusion(bf16[2048,2048]{1,0:T(8,128)(2,1)} %get-tuple-element.65.cotangent, bf16[2048,768]{1,0:T(8,128)(2,1)} %get-tuple-element.64), kind=kOutput, calls=%fused_computation.1 | convolution fusion | flops 6444023808 | bytes 14680064 | tf_op jit(solution)/shard_map/dot_general | solution.py:46
  237.8 0.0 reduce-scatter.6.cloned.1.call-start
  237.9 14.4 %all-gather.5.cloned.1.call-done.weights.mlp_right = bf16[2048,768]{1,0:T(8,128)(2,1)} async-done(((bf16[512,768]{1,0:T(8,128)(2,1)}), bf16[2048,768]{1,0:T(8,128)(2,1)}) %all-gather.5.cloned.1.call-update) | async-done | bytes 3145744 | tf_op jit(solution)/shard_map/all_gather | solution.py:1205
  252.3 14.7 %mlp_backward.1 = bf16[2048,1536]{1,0:T(8,128)(2,1)} custom-call(bf16[2048,2048]{1,0:T(8,128)(2,1)} %get-tuple-element.65.cotangent, bf16[2048,768]{1,0:T(8,128)(2,1)} %all-gather.5.cloned.1.call-done.weights.mlp_right, f32[2048,768]{1,0:T(8,128)} %get-tuple-element.67.gate_slope, f32[2048,768]{1,0:T(8,128)} %get-tuple-element.68.up_slope), custom_call_target="tpu_custom_call" | custom-call | flops 6442450944 | bytes 31457280 | tf_op jit(solution)/shard_map/mlp_backward/pallas_call | solution.py:1386
  266.9 19.2 %convolution_convert_fusion = bf16[2048,1536]{1,0:T(8,128)(2,1)} fusion(bf16[2048,2048]{1,0:T(8,128)(2,1)} %bitcast.95, bf16[2048,1536]{1,0:T(8,128)(2,1)} %mlp_backward.1), kind=kOutput, calls=%fused_computation | convolution fusion | flops 12888047616 | bytes 20971520 | tf_op jit(solution)/shard_map/dot_general | solution.py:46
  286.1 0.0 reduce-scatter.8.cloned.1.call-start
  286.1 84.2 %hidden_leg.1 = (f32[256,2048]{1,0:T(8,128)}, f32[1,2048]{1,0:T(1,128)}, bf16[2,2,2,256,2048]{4,3,2,1,0:T(8,128)(2,1)}) custom-call(bf16[2,2,2,256,1536]{4,3,2,1,0:T(8,128)(2,1)} %bitcast.69, bf16[2048,1536]{1,0:T(8,128)(2,1)} %all-gather.3.cloned.1.call-done.weights.right, f32[256,2048]{1,0:T(8,128)} %get-tuple-element.70.hidden, ...), custom_call_target="tpu_custom_call" | custom-call | bytes 209715200 | tf_op jit(solution)/shard_map/hidden_leg/pallas_call | solution.py:1399
  370.4 0.0 reduce-scatter.4.cloned.1.call-done.down_grad
  370.4 60.7 %attend_backward.1 = (bf16[2048,512]{1,0:T(8,128)(2,1)}, f32[2,8,128]{2,1,0:T(8,128)}, bf16[8,768,256]{2,1,0:T(8,128)(2,1)}, bf16[256,2048]{1,0:T(8,128)(2,1)}, bf16[256,768]{1,0:T(8,128)(2,1)}) custom-call(f32[2048,512]{1,0:T(8,128)} %fusion.raw, f32[2048,128]{1,0:T(8,128)} %pad_maximum_fusion.1.cosine, f32[2048,128]{1,0:T(8,128)} %pad_maximum_fusion.sine, ...), custom_call_target="tpu_custom_call" | custom-call | flops 17716740096 | bytes 83886080 | tf_op jit(solution)/shard_map/attend_backward/pallas_call | solution.py:1427
  431.2 0.0 reduce-scatter.6.cloned.1.call-done.gate_up_grad
  431.3 0.6 copy-done.10
  431.9 0.1 reshape_squeeze.6
  432.0 0.1 reshape_squeeze.7
  432.0 0.1 pad_maximum_fusion.2
  432.1 0.6 pad.13.gain_parts
  432.8 55.6 %output_leg.1 = (f32[256,2048]{1,0:T(8,128)}, f32[8,128]{1,0:T(8,128)}, bf16[256,1536]{1,0:T(8,128)(2,1)}) custom-call(bf16[2,2,2,256,512]{4,3,2,1,0:T(8,128)(2,1)} %bitcast.74, bf16[2048,768]{1,0:T(8,128)(2,1)} %get-tuple-element.52.packed, bf16[256,2048]{1,0:T(8,128)(2,1)} %constant_dynamic-slice_fusion.1.tokens, f32[1,2048]{1,0:T(1,128)} %bitcast.84, ...), custom_call_target="tpu_custom_call" | custom-call | bytes 209715200 | tf_op jit(solution)/shard_map/output_leg/pallas_call | solution.py:1502
  488.3 0.1 fusion.16
  488.5 1.3 slice_bitcast_fusion.5
  489.7 1.3 slice_bitcast_fusion.3
  491.1 1.8 dynamic-slice_bitcast_fusion.1
  492.8 1.2 fusion.17
  494.0 1.2 collective-permute-start.2
  495.2 0.2 fusion.4
  495.4 1.4 fusion.3
  496.8 1.0 dynamic-slice_bitcast_fusion.2
  497.8 1.6 copy.36
  499.4 0.9 dynamic-slice_bitcast_fusion.4
  500.2 1.4 fusion.2
  501.6 2.9 collective-permute-done.2
  504.5 0.9 slice_bitcast_fusion.1
  505.4 0.1 fusion.8
  505.5 0.8 copy.34
  506.3 0.8 copy.35
  507.1 1.0 fusion.18
  508.1 0.1 fusion.6
  508.2 1.0 copy.33
  509.2 0.9 fusion.7
  510.1 2.3 copy.44
  512.4 1.3 copy.45
  (36 shorter events, 0.2 us)
Async XLA Ops:
  7.2 199.7 %all-gather.3.cloned.1.call-start = ((), (), s32[]{:S(2)}) async-start(), calls=%async_computation.3 | async-start | bytes 7864320 | tf_op jit(solution)/shard_map/all_gather | solution.py:1205
  75.2 4.1 copy-start.6
  75.2 4.1 copy-start.8
  75.2 4.3 copy-start
  75.3 177.0 %all-gather.5.cloned.1.call-start = ((), (), s32[]{:S(2)}) async-start(), calls=%async_computation.4 | async-start | bytes 3932160 | tf_op jit(solution)/shard_map/all_gather | solution.py:1205
  77.8 24.4 %collective-permute-start = (bf16[256,2048]{1,0:T(8,128)(2,1)}, bf16[256,2048]{1,0:T(8,128)(2,1)}, u32[]{:S(2)}, u32[]{:S(2)}) collective-permute-start(bf16[256,2048]{1,0:T(8,128)(2,1)} %constant_dynamic-slice_fusion.2.cotangent), channel_id=1, source_target_pairs={{0,4},{4,0},{8,12},{12,8},{16,20},{20,16},{24,28},{28,24},{1,5},{5... | collective-permute-start | bytes 3145736 | tf_op jit(solution)/shard_map/ppermute | solution.py:1188
  79.3 291.1 %reduce-scatter.4.cloned.1.call-start = ((), (), s32[]{:S(2)}) async-start(), calls=%async_computation.5 | async-start | bytes 3932160 | tf_op jit(solution)/shard_map/reduce_scatter | solution.py:1208
  90.0 13.7 %copy-start.7 = (f32[8,8,128]{2,1,0:T(8,128)S(1)}, f32[8,8,128]{2,1,0:T(8,128)}, u32[]{:S(2)}) copy-start(f32[8,8,128]{2,1,0:T(8,128)} %get-tuple-element.57) | copy-start | bytes 98308
  102.2 23.4 %collective-permute-start.1 = (bf16[256,2048]{1,0:T(8,128)(2,1)}, bf16[256,2048]{1,0:T(8,128)(2,1)S(1)}, u32[]{:S(2)}, u32[]{:S(2)}) collective-permute-start(bf16[256,2048]{1,0:T(8,128)(2,1)} %collective-permute-done.cot_part), channel_id=1, source_target_pairs={{0,2},{1,3},{2,0},{3,1},{4,6},{5,7},{6,4},{7,5},{8,10},{9,11},{10,... | collective-permute-start | bytes 3145736 | tf_op jit(solution)/shard_map/ppermute | solution.py:1191
  125.6 1.0 copy-start.3
  237.8 193.4 %reduce-scatter.6.cloned.1.call-start = ((), (), s32[]{:S(2)}) async-start(), calls=%async_computation.6 | async-start | bytes 7864320 | tf_op jit(solution)/shard_map/reduce_scatter | solution.py:1208
  286.1 205.0 %reduce-scatter.8.cloned.1.call-start = ((), (), s32[]{:S(2)}) async-start(), calls=%async_computation.7 | async-start | bytes 3932160 | tf_op jit(solution)/shard_map/reduce_scatter | solution.py:1208
  431.1 0.7 copy-start.10
  431.1 0.9 copy-start.9
  432.7 55.6 %copy-start.1 = (bf16[512,1536]{1,0:T(8,128)(2,1)S(1)}, bf16[512,1536]{1,0:T(8,128)(2,1)}, u32[]{:S(2)}) copy-start(bf16[512,1536]{1,0:T(8,128)(2,1)} %reduce-scatter.6.cloned.1.call-done.gate_up_grad) | copy-start | bytes 4718596
  432.7 55.6 %copy-start.5 = (bf16[512,768]{1,0:T(8,128)(2,1)S(1)}, bf16[512,768]{1,0:T(8,128)(2,1)}, u32[]{:S(2)}) copy-start(bf16[512,768]{1,0:T(8,128)(2,1)} %reduce-scatter.4.cloned.1.call-done.down_grad) | copy-start | bytes 2359300
  488.3 6.8 %copy-start.4 = (bf16[256,768]{1,0:T(8,128)(2,1)S(1)}, bf16[256,768]{1,0:T(8,128)(2,1)}, u32[]{:S(2)}) copy-start(bf16[256,768]{1,0:T(8,128)(2,1)} %get-tuple-element.88) | copy-start | bytes 1179652
  494.0 10.5 %collective-permute-start.2 = (bf16[768,256]{1,0:T(8,128)(2,1)}, bf16[768,256]{1,0:T(8,128)(2,1)}, u32[]{:S(2)}, u32[]{:S(2)}) collective-permute-start(bf16[768,256]{1,0:T(8,128)(2,1)} %dynamic-slice_bitcast_fusion.1), channel_id=1, source_target_pairs={{0,4},{4,0},{8,12},{12,8},{16,20},{20,16},{24,28},{28,24},{1,5},{5... | collective-permute-start | bytes 1179656 | tf_op jit(solution)/shard_map/ppermute | solution.py:1188
  505.5 7.0 %copy-start.2 = (f32[256,2048]{1,0:T(8,128)S(1)}, f32[256,2048]{1,0:T(8,128)}, u32[]{:S(2)}) copy-start(f32[256,2048]{1,0:T(8,128)} %get-tuple-element.162) | copy-start | bytes 6291460
Sparse Core Ops, SparseCore 0:
  75.4 113.4 all-gather.2
  190.5 61.7 all-gather.4
  254.6 58.8 reduce-scatter.3
  315.7 110.7 reduce-scatter.5
  431.3 58.5 reduce-scatter.7

commit v5 on v4

--- a/solution.py
+++ b/solution.py
@@ -519,9 +519,11 @@
     weight_grads,
     grad_hidden,
     gate_up_grad,
+    down_grad,
     input_grad,
     gain_total,
     gate_up_other,
+    down_other,
     slots,
     swap_send,
     swap_recv,
@@ -535,7 +537,10 @@
     y, y_peer = lax.axis_index("dp") % 2, neighbours()[4]
     half = gate_up_other.shape[0]
     theirs = pl.ds(pl.multiple_of((1 - y) * half, half), half)
-    swap = remote(gate_up_grad.at[theirs], gate_up_other, swap_send, swap_recv, y_peer)
+    swaps = [
+        remote(gate_up_grad.at[theirs], gate_up_other, swap_send.at[0], swap_recv.at[0], y_peer),
+        remote(down_grad.at[theirs], down_other, swap_send.at[1], swap_recv.at[1], y_peer),
+    ]
 
     def step(rows):
         grad = reduce.take(rows)
@@ -545,12 +550,13 @@
     sums.greet()
     slots[...] = gain_parts[...]
     meet(sums.n_dp + sums.n_mp - 2)
-    swap.start()
+    swaps[0].start()
     for k in range(reduce.chunks):
         reduce.produce(k, False)
         reduce.begin(k)
         reduce.produce(k, True)
         reduce.first(k)
+    swaps[1].start()
     owned = weight_grads.shape[2]
     diagonal = lax.broadcasted_iota(jnp.int32, (owned, owned), 0) == lax.broadcasted_iota(
         jnp.int32, (owned, owned), 1
@@ -571,7 +577,8 @@
     sums.finish()
     for k in range(reduce.chunks):
         reduce.release(k)
-    swap.wait()
+    for copy in swaps:
+        copy.wait()
     reduce.finish()
 
 
@@ -649,23 +656,19 @@
     tokens,
     gate,
     up,
-    down,
     full,
     gains,
     docs_other,
     normed_out,
     gate_up_mine,
-    down_mine,
     stage,
     gain,
     normed,
     gate_up_stage,
-    down_stage,
     tokens_mine,
     tokens_other,
     gate_in,
     up_in,
-    down_in,
     local,
     stores,
     swap,
@@ -696,7 +699,7 @@
     loads = [
         pltpu.make_async_copy(source, target, local.at[i])
         for i, (source, target) in enumerate(
-            ((tokens, tokens_mine), (gate, gate_in), (up, up_in), (down, down_in))
+            ((tokens, tokens_mine), (gate, gate_in), (up, up_in))
         )
     ]
     for load in loads:
@@ -723,7 +726,6 @@
     gate_up_swapped = remote(
         gate_up_stage, gate_up_mine.at[mine], swap.at[0, 2], swap.at[1, 2], y_peer
     )
-    down_swapped = remote(down_stage, down_mine.at[mine], swap.at[0, 3], swap.at[1, 3], y_peer)
 
     def ring(step, i):
         slab = lax.rem(z - step + n_slabs, n_slabs)
@@ -752,12 +754,11 @@
         gain_to(j).wait()
         return carry
 
-    def fill_mlp(gate_up_to, down_to, row, which):
+    def fill_mlp(gate_up_to, row, which):
         size = gate.shape[1] // 2
         cols = pl.ds(pl.multiple_of(which * size, 128), size)
         gate_up_to[pl.ds(row, rows), :size] = gate_in[:, cols].astype(BF16)
         gate_up_to[pl.ds(row, rows), size:] = up_in[:, cols].astype(BF16)
-        down_to[pl.ds(row, rows), :] = down_in[cols, :].astype(BF16).T
 
     fill(stage, 0, 1 - y)
     row = 0
@@ -777,9 +778,8 @@
     gains[dp] = gain[...]
     for load in loads[1:]:
         load.wait()
-    fill_mlp(gate_up_stage, down_stage, 0, 1 - y)
+    fill_mlp(gate_up_stage, 0, 1 - y)
     gate_up_swapped.start()
-    down_swapped.start()
     swapped.wait_recv()
     ring(0, 1).start()
     lax.fori_loop(1, n_dp, settle, 0)
@@ -816,7 +816,7 @@
             store(4 + i).start()
 
     loads[0].wait()
-    early = [functools.partial(fill_mlp, gate_up_mine, down_mine, mine.start, y)]
+    early = [functools.partial(fill_mlp, gate_up_mine, mine.start, y)]
     early += [functools.partial(norm_mine, i) for i in range(4)]
     late = [functools.partial(spread.pass_on, c) for c in range(FEW)]
     late += [functools.partial(spread.pass_last, c) for c in range(FEW)]
@@ -858,7 +858,6 @@
     docs_swapped.wait()
     swapped.wait_send()
     gate_up_swapped.wait()
-    down_swapped.wait()
 
     def sent(step, carry):
         for i in range(2):
@@ -952,12 +951,10 @@
     mlp_left,
     mlp_right,
     hidden,
-    down_grad,
     out,
     gains,
     weight_grads,
     output,
-    down_other,
     q,
     k,
     v,
@@ -971,7 +968,6 @@
     mlp_right_held,
     hidden_held,
     loads,
-    swap,
     *scratch
 ):
     factor = HEAD_WIDTH ** (-0.5)
@@ -988,12 +984,6 @@
         )
     ]
 
-    theirs = pl.ds(
-        pl.multiple_of((1 - lax.axis_index("dp") % 2) * down_other.shape[0], down_other.shape[0]),
-        down_other.shape[0],
-    )
-    swapped = remote(down_grad.at[theirs], down_other, swap.at[0], swap.at[1], neighbours()[4])
-
     def mlp_load():
         greet(neighbours()[2:])
         for load in mlp_loads:
@@ -1007,9 +997,6 @@
             if c == 0:
                 meet(3)
             mlp.begin(c)
-        swapped.start()
-
-    def mlp_first():
         for c in range(FEW):
             mlp.produce(c, True)
             mlp.first(c)
@@ -1030,7 +1017,6 @@
         for c in range(FEW):
             mlp.release(c)
         mlp.finish()
-        swapped.wait()
 
     def at_step(step, job):
         pl.when(pl.program_id(0) == step)(job)
@@ -1055,8 +1041,6 @@
         dk[cols] += dot(grad_scores, query, 0, 0) * factor
         dv[cols] += dot(weights.astype(BF16), block_grad, 0, 0)
         if n == 0:
-            at_step(0, mlp_first)
-        if n == 1:
             at_step(1, mlp_second)
     gains[...] = jnp.zeros_like(gains)
 
@@ -1236,32 +1220,29 @@
     pack_cols = attn_cols + query_cols
     pair_rows = 2 * rows
     n_slabs = n_dp // 2
-    attn_full, gains, docs_other, normed_one, mlp_mine, down_mine = call_leg(
+    attn_full, gains, docs_other, normed_one, mlp_mine = call_leg(
         front,
         3,
         "front",
-        [VM] * 9 + [ANY] * 4,
+        [VM] * 9 + [ANY] * 3,
         (
             jax.ShapeDtypeStruct((width, pack_cols), BF16),
             jax.ShapeDtypeStruct((n_dp, 8, 128), F32),
             jax.ShapeDtypeStruct(documents.shape, jnp.int32),
             jax.ShapeDtypeStruct((pair_rows, width), BF16),
             jax.ShapeDtypeStruct((2 * model_rows, 2 * hidden_cols), BF16),
-            jax.ShapeDtypeStruct((2 * model_rows, hidden_cols), BF16),
         ),
-        (VM, VM, VM, ANY, VM, VM),
+        (VM, VM, VM, ANY, VM),
         [
             pltpu.VMEM((model_rows, pack_cols), BF16),
             pltpu.VMEM((8, 128), F32),
             pltpu.VMEM((pair_rows, width), BF16),
             pltpu.VMEM((model_rows, 2 * hidden_cols), BF16),
-            pltpu.VMEM((model_rows, hidden_cols), BF16),
             pltpu.VMEM((rows, width), BF16),
             pltpu.VMEM((rows, width), BF16),
             pltpu.VMEM(gate_weight.shape, F32),
             pltpu.VMEM(up_weight.shape, F32),
-            pltpu.VMEM(down_weight.shape, F32),
-            pltpu.SemaphoreType.DMA((4,)),
+            pltpu.SemaphoreType.DMA((3,)),
             pltpu.SemaphoreType.DMA((8,)),
             pltpu.SemaphoreType.DMA((2, 4)),
             pltpu.SemaphoreType.DMA((n_dp,)),
@@ -1284,14 +1265,15 @@
         tokens,
         gate_weight,
         up_weight,
-        down_weight,
-    )
+    )
+    down_low = down_weight.astype(BF16)
+    down_given, _ = lax.optimization_barrier((half(down_low, 1 - y, 0).T, docs_other))
+    down_got = y_swap(down_given)
 
     cot_part = lax.dynamic_slice_in_dim(cotangent, mp * share, share, 0)
     cot_part, _ = lax.optimization_barrier((cot_part, docs_other))
     cot_part = y_swap(cot_part)
     gate_up_full = slab_gather(mlp_mine)
-    down_full = slab_gather(down_mine)
     gain_one, gain_two, gain_query, gain_key = (g.reshape(1, -1) for g in gain_parts_of(gains))
     docs = jnp.concatenate([documents, docs_other], 0)
     tokens_share = lax.dynamic_slice_in_dim(tokens, mp * share, share, 0)
@@ -1324,7 +1306,8 @@
         2 * pair_flops,
         20 * MIB,
     )(*attention_args)
-    attended, cot_across = lax.optimization_barrier((attended, cot_across))
+    attended, cot_across, down_got = lax.optimization_barrier((attended, cot_across, down_got))
+    down_full = slab_gather(in_order(y, half(down_low, y, 0).T, down_got, 0))
 
     def grouped(cols):
         return (2, 2, 2, share, cols)
@@ -1424,7 +1407,7 @@
     )
     grad_hidden_low = grad_hidden_low.reshape(pair_rows, width)
 
-    raw_grad, head_gain_parts, attn_grad, layer_output, down_other = call_blocks(
+    raw_grad, head_gain_parts, attn_grad, layer_output = call_blocks(
         attend_backward,
         seqs,
         [once(spec) for spec in attention_specs]
@@ -1436,21 +1419,18 @@
             ANY,
             ANY,
             ANY,
-            ANY,
         ],
         (
             jax.ShapeDtypeStruct((pair_rows, attn_cols), BF16),
             jax.ShapeDtypeStruct((seqs, 8, head), F32),
             jax.ShapeDtypeStruct((n_dp, pack_cols, model_rows), BF16),
             jax.ShapeDtypeStruct((share, width), BF16),
-            jax.ShapeDtypeStruct((model_rows, hidden_cols), BF16),
         ),
         (
             once(by_rows(seq_length, attn_cols)),
             pl.BlockSpec((1, 8, head), lambda i: (i, 0, 0)),
             once(whole(n_dp, pack_cols, model_rows)),
             once(whole(share, width)),
-            ANY,
         ),
         [
             pltpu.VMEM((GROUP, seq_length, head), BF16),
@@ -1466,7 +1446,6 @@
             pltpu.VMEM((width, hidden_cols), BF16),
             pltpu.VMEM((share, width), F32),
             pltpu.SemaphoreType.DMA((4,)),
-            pltpu.SemaphoreType.DMA((2,)),
         ]
         + Reduce.scratch(share, width, half_width, FEW),
         5 * pair_flops + 2 * pair_rows * width * (pack_cols + query_cols + hidden_cols),
@@ -1482,7 +1461,6 @@
         active.reshape(grouped(hidden_cols)),
         down_full,
         hidden,
-        down_grad,
     )
     head_gain_parts = head_gain_parts.sum(0)
     attn_grad = attn_grad.reshape(n_dp * pack_cols, model_rows)
@@ -1498,22 +1476,23 @@
         head_gain_parts[1].reshape(n_dp, n_head),
     )
 
-    low = 3 * width // 4
-    input_grad, gain_sums, gate_up_other = call_leg(
+    low = 7 * width // 8
+    input_grad, gain_sums, gate_up_other, down_other = call_leg(
         output_leg,
         2,
         "output_leg",
-        [VM] * 7 + [ANY],
+        [VM] * 7 + [ANY] * 2,
         (
             jax.ShapeDtypeStruct((share, width), F32),
             jax.ShapeDtypeStruct((8, 128), F32),
             jax.ShapeDtypeStruct((model_rows, 2 * hidden_cols), BF16),
+            jax.ShapeDtypeStruct((model_rows, hidden_cols), BF16),
         ),
-        (VM, VM, ANY),
+        (VM, VM, ANY, ANY),
         [
             pltpu.VMEM((n_dp, 8, 128), F32),
-            pltpu.SemaphoreType.DMA,
-            pltpu.SemaphoreType.DMA,
+            pltpu.SemaphoreType.DMA((2,)),
+            pltpu.SemaphoreType.DMA((2,)),
         ]
         + Reduce.scratch(share, width, low)
         + SumGains.scratch(n_dp, 4),
@@ -1527,6 +1506,7 @@
         attn_parts,
         grad_hidden,
         gate_up_grad,
+        down_grad,
     )
     attn_given = lax.dynamic_index_in_dim(attn_grad, 1 - y, 0, False)
     attn_given, gate_up_other, down_other = lax.optimization_barrier(

time: 531 us -> 528 us (level)
    pallas_call x1, Pallas kernels: 60.7 us -> 54.9 us  [on_device(): call_blocks(attend_backward, seqs, [once(spec) for spec in attention_spec...]
    ppermute x2 -> x3, waiting for transfers between devices: 8.64 us -> 11 us  [y_swap(): return lax.ppermute(values, 'dp', [(i, i ^ 1) for i in range(n_dp)])]
    unnamed x31 -> x36, local copies, waits for them, and re-layouts: 10.9 us -> 12.7 us
  transfers between devices with their start and end apart: 8 -> 9, of which waited for: 4 -> 5; matrix products, arithmetic and copies ran while one was open for 13% -> 12% of each run, Pallas kernels for 63% -> 63%
where the time goes in v5:
time: 528 us; the launch traced here: 518 us
  Pallas kernels  391 us (74%)
  matrix products  40.1 us (8%)
  waiting for transfers between devices  29.2 us (6%)
  local copies, waits for them, and re-layouts  26.6 us (5%)
  between operations  14.6 us (3%)
  other arithmetic  11.9 us (2%)
    pallas_call x1, Pallas kernels, on_device(): call_leg(hidden_leg, 1, 'hidden_leg', [ANY] * 2 + [VM] * 3, (jax.ShapeDty...  84.2 us
    pallas_call x1, Pallas kernels, on_device(): call_leg(attention_leg, 0, 'attention_leg', [VM] * 4 + [ANY] * 3, (jax.Sh...  80.5 us
    pallas_call x1, Pallas kernels, on_device(): call_leg(output_leg, 2, 'output_leg', [VM] * 7 + [ANY] * 2, (jax.ShapeDty...  63.3 us
    pallas_call x1, Pallas kernels, on_device(): call_leg(front, 3, 'front', [VM] * 9 + [ANY] * 3, (jax.ShapeDtypeStruct((...  63 us
    pallas_call x1, Pallas kernels, on_device(): call_blocks(attend_backward, seqs, [once(spec) for spec in attention_spec...  54.9 us
    dot_general x3, matrix products, dot(): lax.dot_general(left, right, (((left_dim,), (right_dim,)), ((), ())), pre...  40.1 us
    pallas_call x1, Pallas kernels, on_device(): call_blocks(mlp_forward, blocks, [by_rows(TOKEN_BLOCK, width), whole(widt...  19.4 us
    pallas_call x1, Pallas kernels, on_device(): call_blocks(mlp_backward, blocks, [by_rows(TOKEN_BLOCK, width), whole(wid...  14.6 us
  transfers between devices with their start and end apart: 9, of which 5 were waited for; matrix products, arithmetic and copies ran while one was open for 12% of the time, Pallas kernels for 63%

profile of v5, /device:TPU:0, one launch (start us, length us, event | category | flops | bytes accessed | tf_op | source)
XLA Modules:
  0.0 518.4 jit_solution(1849711897126403372)
XLA Ops:
  7.2 0.0 all-gather.3.cloned.1.call-start
  7.2 63.0 %front.1 = (bf16[2048,768]{1,0:T(8,128)(2,1)}, f32[8,8,128]{2,1,0:T(8,128)}, s32[1,1024]{1,0:T(1,128)}, bf16[2048,2048]{1,0:T(8,128)(2,1)}, bf16[512,1536]{1,0:T(8,128)(2,1)}) custom-call(f32[256,512]{1,0:T(8,128)} %q.1, f32[256,256]{1,0:T(8,128)} %k.1, f32[256,256]{1,0:T(8,128)} %v.1, f32[512,256]{1,0:T(8,128)} %o.1, f32[1,256]{1,0:T(1,128)} %bitcast.94, ...), custom_call_target="tpu_custom_call" | custom-call | bytes 262144000 | tf_op jit(solution)/shard_map/front/pallas_call | solution.py:1223
  70.3 0.0 all-gather.5.cloned.1.call-start
  70.4 2.7 constant_dynamic-slice_fusion.1
  73.1 0.9 collective-permute-start
  74.0 0.2 fusion.12
  74.2 0.1 convert_bitcast_fusion
  74.3 3.7 multiply_cosine_fusion
  78.0 1.3 pad_maximum_fusion.sine
  79.3 1.1 copy-done
  80.5 9.5 %fusion.raw = f32[2048,512]{1,0:T(8,128)} fusion(bf16[2048,2048]{1,0:T(8,128)(2,1)} %get-tuple-element.52.normed, bf16[2048,768]{1,0:T(8,128)(2,1)S(1)} %copy-done), kind=kOutput, calls=%fused_computation.2 | convolution fusion | flops 4294967296 | bytes 14680064 | tf_op jit(solution)/shard_map/dot_general | solution.py:46
  90.0 7.5 %collective-permute-done.cot_part = bf16[256,2048]{1,0:T(8,128)(2,1)S(1)} collective-permute-done((bf16[256,2048]{1,0:T(8,128)(2,1)S(1)}, bf16[256,2048]{1,0:T(8,128)(2,1)S(1)}, u32[]{:S(2)}, u32[]{:S(2)}) %collective-permute-start) | collective-permute-done | bytes 1048608 | tf_op jit(solution)/shard_map/ppermute | solution.py:1172
  97.5 0.5 collective-permute-start.1
  98.0 1.7 copy.33
  99.7 0.8 dynamic-slice_bitcast_fusion.2
  100.5 1.5 collective-permute-start.2
  102.0 1.3 copy.41
  103.3 0.6 reshape.245.gain_query
  103.9 0.6 reshape.247.gain_key
  104.5 1.3 pad_maximum_fusion.1.cosine
  105.8 10.8 %attend_forward.1.attended = bf16[2048,256]{1,0:T(8,128)(2,1)} custom-call(f32[2048,512]{1,0:T(8,128)} %fusion.raw, f32[2048,128]{1,0:T(8,128)} %pad_maximum_fusion.1.cosine, f32[2048,128]{1,0:T(8,128)} %pad_maximum_fusion.sine, s32[2048,1]{1,0:T(8,128)} %bitcast.76, f32[1,128]{1,0:T(1,128)} %reshape.245.gain_query, f32[1,128]{1,0:T(1,128)} %reshape.247.gain_key), custom_call_target="tpu_custom_call" | custom-call | flops 1073741824 | bytes 20971520 | tf_op jit(solution)/shard_map/attend_forward/pallas_call | solution.py:1299
  116.6 4.5 collective-permute-done.1.cot_across
  121.1 1.2 maximum_select_fusion
  122.3 0.5 reduce-scatter.6.cloned.1.call-start
  122.9 0.6 fusion.19
  123.5 80.5 %attention_leg.1 = (f32[256,2048]{1,0:T(8,128)}, bf16[2,2,2,256,2048]{4,3,2,1,0:T(8,128)(2,1)}, bf16[2048,2048]{1,0:T(8,128)(2,1)}) custom-call(bf16[2,2,2,256,256]{4,3,2,1,0:T(8,128)(2,1)} %bitcast.75, bf16[2048,768]{1,0:T(8,128)(2,1)} %get-tuple-element.53.packed, bf16[256,2048]{1,0:T(8,128)(2,1)} %get-tuple-element.149.tokens, f32[1,2048]{1,0:T(1,128)} %bitcast.83, ...), custom_call_target="tpu_custom_call" | custom-call | bytes 209715200 | tf_op jit(solution)/shard_map/attention_leg/pallas_call | solution.py:1317
  204.0 19.4 %mlp_forward.1 = (bf16[2048,768]{1,0:T(8,128)(2,1)}, f32[2048,768]{1,0:T(8,128)}, f32[2048,768]{1,0:T(8,128)}) custom-call(bf16[2048,2048]{1,0:T(8,128)(2,1)} %bitcast.98, bf16[2048,1536]{1,0:T(8,128)(2,1)} %all-gather.3.cloned.1.call-done.weights.right), custom_call_target="tpu_custom_call" | custom-call | flops 12884901888 | bytes 31457280 | tf_op jit(solution)/shard_map/mlp_forward/pallas_call | solution.py:1352
  223.4 11.4 %convolution_convert_fusion.1 = bf16[2048,768]{1,0:T(8,128)(2,1)} fusion(bf16[2048,2048]{1,0:T(8,128)(2,1)} %get-tuple-element.67.cotangent, bf16[2048,768]{1,0:T(8,128)(2,1)} %get-tuple-element.66), kind=kOutput, calls=%fused_computation.1 | convolution fusion | flops 6444023808 | bytes 14680064 | tf_op jit(solution)/shard_map/dot_general | solution.py:46
  234.9 0.2 reduce-scatter.4.cloned.1.call-start
  235.1 12.4 %all-gather.5.cloned.1.call-done.weights.mlp_right = bf16[2048,768]{1,0:T(8,128)(2,1)} async-done(((bf16[512,768]{1,0:T(8,128)(2,1)}), bf16[2048,768]{1,0:T(8,128)(2,1)}) %all-gather.5.cloned.1.call-update) | async-done | bytes 3145744 | tf_op jit(solution)/shard_map/all_gather | solution.py:1189
  247.4 14.6 %mlp_backward.1 = bf16[2048,1536]{1,0:T(8,128)(2,1)} custom-call(bf16[2048,2048]{1,0:T(8,128)(2,1)} %get-tuple-element.67.cotangent, bf16[2048,768]{1,0:T(8,128)(2,1)} %all-gather.5.cloned.1.call-done.weights.mlp_right, f32[2048,768]{1,0:T(8,128)} %get-tuple-element.69.gate_slope, f32[2048,768]{1,0:T(8,128)} %get-tuple-element.70.up_slope), custom_call_target="tpu_custom_call" | custom-call | flops 6442450944 | bytes 31457280 | tf_op jit(solution)/shard_map/mlp_backward/pallas_call | solution.py:1369
  262.0 19.2 %convolution_convert_fusion = bf16[2048,1536]{1,0:T(8,128)(2,1)} fusion(bf16[2048,2048]{1,0:T(8,128)(2,1)} %bitcast.99, bf16[2048,1536]{1,0:T(8,128)(2,1)} %mlp_backward.1), kind=kOutput, calls=%fused_computation | convolution fusion | flops 12888047616 | bytes 20971520 | tf_op jit(solution)/shard_map/dot_general | solution.py:46
  281.2 0.0 reduce-scatter.8.cloned.1.call-start
  281.3 84.2 %hidden_leg.1 = (f32[256,2048]{1,0:T(8,128)}, f32[1,2048]{1,0:T(1,128)}, bf16[2,2,2,256,2048]{4,3,2,1,0:T(8,128)(2,1)}) custom-call(bf16[2,2,2,256,1536]{4,3,2,1,0:T(8,128)(2,1)} %bitcast.73, bf16[2048,1536]{1,0:T(8,128)(2,1)} %all-gather.3.cloned.1.call-done.weights.right, f32[256,2048]{1,0:T(8,128)} %get-tuple-element.72.hidden, ...), custom_call_target="tpu_custom_call" | custom-call | bytes 209715200 | tf_op jit(solution)/shard_map/hidden_leg/pallas_call | solution.py:1382
  365.5 54.9 %attend_backward.1 = (bf16[2048,512]{1,0:T(8,128)(2,1)}, f32[2,8,128]{2,1,0:T(8,128)}, bf16[8,768,256]{2,1,0:T(8,128)(2,1)}, bf16[256,2048]{1,0:T(8,128)(2,1)}) custom-call(f32[2048,512]{1,0:T(8,128)} %fusion.raw, f32[2048,128]{1,0:T(8,128)} %pad_maximum_fusion.1.cosine, f32[2048,128]{1,0:T(8,128)} %pad_maximum_fusion.sine, s32[2048,1]{1,0:T(8,128)} %bitcast.77, ...), custom_call_target="tpu_custom_call" | custom-call | flops 17716740096 | bytes 83886080 | tf_op jit(solution)/shard_map/attend_backward/pallas_call | solution.py:1410
  420.4 1.2 reduce-scatter.4.cloned.1.call-done.gate_up_grad
  421.8 0.1 reshape_squeeze.6
  421.9 0.1 reshape_squeeze.7
  422.0 0.1 pad_maximum_fusion.2
  422.0 0.6 pad.13.gain_parts
  422.7 63.3 %output_leg.1 = (f32[256,2048]{1,0:T(8,128)}, f32[8,128]{1,0:T(8,128)}, bf16[256,1536]{1,0:T(8,128)(2,1)}, bf16[256,768]{1,0:T(8,128)(2,1)}) custom-call(bf16[2,2,2,256,512]{4,3,2,1,0:T(8,128)(2,1)} %bitcast.78, bf16[2048,768]{1,0:T(8,128)(2,1)} %get-tuple-element.53.packed, bf16[256,2048]{1,0:T(8,128)(2,1)} %get-tuple-element.149.tokens, ...), custom_call_target="tpu_custom_call" | custom-call | bytes 209715200 | tf_op jit(solution)/shard_map/output_leg/pallas_call | solution.py:1480
  486.0 0.1 fusion.16
  486.1 0.5 copy-done.12
  486.6 0.5 slice_bitcast_fusion.5
  487.1 0.6 slice_bitcast_fusion.3
  487.7 1.8 dynamic-slice_bitcast_fusion.1
  489.5 1.2 fusion.17
  490.7 1.5 collective-permute-start.3
  492.2 0.2 fusion.4
  492.4 1.4 fusion.3
  493.8 1.0 dynamic-slice_bitcast_fusion.4
  494.8 1.6 copy.38
  496.4 0.9 dynamic-slice_bitcast_fusion.6
  497.3 1.4 fusion.2
  498.7 3.5 collective-permute-done.3
  502.2 0.9 slice_bitcast_fusion.1
  503.1 0.8 copy.37
  504.0 0.8 copy.36
  504.8 1.0 fusion.18
  505.8 0.1 fusion.6
  505.9 1.0 copy.35
  506.9 0.9 fusion.7
  507.8 2.3 copy.46
  510.1 1.3 copy.47
  (46 shorter events, 0.3 us)
Async XLA Ops:
  7.2 196.8 %all-gather.3.cloned.1.call-start = ((), (), s32[]{:S(2)}) async-start(), calls=%async_computation.3 | async-start | bytes 7864320 | tf_op jit(solution)/shard_map/all_gather | solution.py:1189
  70.3 177.2 %all-gather.5.cloned.1.call-start = ((), (), s32[]{:S(2)}) async-start(), calls=%async_computation.4 | async-start | bytes 3932160 | tf_op jit(solution)/shard_map/all_gather | solution.py:1189
  70.3 3.6 copy-start.7
  70.4 3.6 copy-start.9
  73.1 6.3 %copy-start.1 = (bf16[256,2048]{1,0:T(8,128)(2,1)}, bf16[256,2048]{1,0:T(8,128)(2,1)S(1)}, u32[]{:S(2)}) copy-start(bf16[256,2048]{1,0:T(8,128)(2,1)S(1)} %get-tuple-element.55.cotangent) | copy-start | bytes 3145732
  73.1 24.4 %collective-permute-start = (bf16[256,2048]{1,0:T(8,128)(2,1)S(1)}, bf16[256,2048]{1,0:T(8,128)(2,1)S(1)}, u32[]{:S(2)}, u32[]{:S(2)}) collective-permute-start(bf16[256,2048]{1,0:T(8,128)(2,1)S(1)} %get-tuple-element.55.cotangent), channel_id=1, source_target_pairs={{0,4},{4,0},{8,12},{12,8},{16,20},{20,16},{24,28},{28,24},{1,5},{5... | collective-permute-start | bytes 3145736 | tf_op jit(solution)/shard_map/ppermute | solution.py:1172
  78.0 2.5 copy-start
  97.5 5.9 %copy-start.5 = (bf16[256,2048]{1,0:T(8,128)(2,1)}, bf16[256,2048]{1,0:T(8,128)(2,1)S(1)}, u32[]{:S(2)}) copy-start(bf16[256,2048]{1,0:T(8,128)(2,1)S(1)} %collective-permute-done.cot_part) | copy-start | bytes 3145732
  97.5 4.5 copy-start.8
  97.5 23.7 %collective-permute-start.1 = (bf16[256,2048]{1,0:T(8,128)(2,1)S(1)}, bf16[256,2048]{1,0:T(8,128)(2,1)}, u32[]{:S(2)}, u32[]{:S(2)}) collective-permute-start(bf16[256,2048]{1,0:T(8,128)(2,1)S(1)} %collective-permute-done.cot_part), channel_id=1, source_target_pairs={{0,2},{1,3},{2,0},{3,1},{4,6},{5,7},{6,4},{7,5},{8,10},{9,11},{10,... | collective-permute-start | bytes 3145736 | tf_op jit(solution)/shard_map/ppermute | solution.py:1175
  100.5 16.1 %collective-permute-start.2 = (bf16[256,768]{1,0:T(8,128)(2,1)}, bf16[256,768]{1,0:T(8,128)(2,1)S(1)}, u32[]{:S(2)}, u32[]{:S(2)}) collective-permute-start(bf16[256,768]{1,0:T(8,128)(2,1)} %get-tuple-element.60), channel_id=1, source_target_pairs={{0,4},{4,0},{8,12},{12,8},{16,20},{20,16},{24,28},{28,24},{1,5},{5... | collective-permute-start | bytes 1179656 | tf_op jit(solution)/shard_map/ppermute | solution.py:1172
  122.3 298.1 %reduce-scatter.6.cloned.1.call-start = ((), (), s32[]{:S(2)}) async-start(), calls=%async_computation.6 | async-start | bytes 3932160 | tf_op jit(solution)/shard_map/reduce_scatter | solution.py:1192
  234.9 186.8 %reduce-scatter.4.cloned.1.call-start = ((), (), s32[]{:S(2)}) async-start(), calls=%async_computation.5 | async-start | bytes 7864320 | tf_op jit(solution)/shard_map/reduce_scatter | solution.py:1192
  281.2 206.5 %reduce-scatter.8.cloned.1.call-start = ((), (), s32[]{:S(2)}) async-start(), calls=%async_computation.7 | async-start | bytes 3932160 | tf_op jit(solution)/shard_map/reduce_scatter | solution.py:1192
  420.4 1.4 copy-start.11
  420.4 1.6 copy-start.10
  422.7 63.3 %copy-start.4 = (bf16[512,768]{1,0:T(8,128)(2,1)S(1)}, bf16[512,768]{1,0:T(8,128)(2,1)}, u32[]{:S(2)}) copy-start(bf16[512,768]{1,0:T(8,128)(2,1)} %reduce-scatter.6.cloned.1.call-done.down_grad) | copy-start | bytes 2359300
  422.7 63.4 %copy-start.2 = (bf16[512,1536]{1,0:T(8,128)(2,1)S(1)}, bf16[512,1536]{1,0:T(8,128)(2,1)}, u32[]{:S(2)}) copy-start(bf16[512,1536]{1,0:T(8,128)(2,1)} %reduce-scatter.4.cloned.1.call-done.gate_up_grad) | copy-start | bytes 4718596
  486.0 0.7 copy-start.12
  486.0 6.2 %copy-start.6 = (bf16[256,768]{1,0:T(8,128)(2,1)S(1)}, bf16[256,768]{1,0:T(8,128)(2,1)}, u32[]{:S(2)}) copy-start(bf16[256,768]{1,0:T(8,128)(2,1)} %get-tuple-element.90) | copy-start | bytes 1179652
  490.7 11.5 %collective-permute-start.3 = (bf16[768,256]{1,0:T(8,128)(2,1)}, bf16[768,256]{1,0:T(8,128)(2,1)}, u32[]{:S(2)}, u32[]{:S(2)}) collective-permute-start(bf16[768,256]{1,0:T(8,128)(2,1)} %dynamic-slice_bitcast_fusion.1), channel_id=1, source_target_pairs={{0,4},{4,0},{8,12},{12,8},{16,20},{20,16},{24,28},{28,24},{1,5},{5... | collective-permute-start | bytes 1179656 | tf_op jit(solution)/shard_map/ppermute | solution.py:1172
  505.9 4.2 copy-start.3
Sparse Core Ops, SparseCore 0:
  70.4 113.6 all-gather.2
  185.7 61.6 all-gather.4
  249.8 58.8 reduce-scatter.5
  310.9 110.7 reduce-scatter.3
  423.8 61.3 reduce-scatter.7

commit v6 on v5

--- a/solution.py
+++ b/solution.py
@@ -871,6 +871,24 @@
     return [(j, min(128, size - j * 128)) for j in range(-(-size // 128))]
 
 
+def finish_attention(own, other, q, k, v, o):
+    y = lax.axis_index("dp") % 2
+
+    def place(source, which):
+        at = 0
+        for w in (q, k, v):
+            size = w.shape[1] // 2
+            cols = pl.ds(pl.multiple_of(which * size, 128), size)
+            w[:, cols] = source[at : at + size, :].T.astype(F32)
+            at += size
+        size = o.shape[0] // 2
+        rows = pl.ds(pl.multiple_of(which * size, size), size)
+        o[rows, :] = source[at : at + size, :].astype(F32)
+
+    place(own, y)
+    place(other, 1 - y)
+
+
 QUERY_BLOCK = 256
 LONGEST = 512
 
@@ -950,7 +968,6 @@
     packed,
     mlp_left,
     mlp_right,
-    hidden,
     out,
     gains,
     weight_grads,
@@ -966,7 +983,6 @@
     normed_held,
     mlp_left_held,
     mlp_right_held,
-    hidden_held,
     loads,
     *scratch
 ):
@@ -980,7 +996,7 @@
     mlp_loads = [
         pltpu.make_async_copy(source, target, loads.at[i + 1])
         for i, (source, target) in enumerate(
-            ((mlp_left, mlp_left_held), (mlp_right, mlp_right_held), (hidden, hidden_held))
+            ((mlp_left, mlp_left_held), (mlp_right, mlp_right_held))
         )
     ]
 
@@ -990,7 +1006,7 @@
             load.start()
 
     def mlp_begin():
-        for load in mlp_loads[:2]:
+        for load in mlp_loads:
             load.wait()
         for c in range(FEW):
             mlp.produce(c, False)
@@ -1007,9 +1023,8 @@
 
     def mlp_end():
         def step(rows):
-            output[rows] = (hidden_held[rows] + mlp.take(rows)).astype(BF16)
-
-        mlp_loads[2].wait()
+            output[rows] = mlp.take(rows)
+
 
         for c in range(FEW):
             mlp.arrive(c)
@@ -1407,7 +1422,7 @@
     )
     grad_hidden_low = grad_hidden_low.reshape(pair_rows, width)
 
-    raw_grad, head_gain_parts, attn_grad, layer_output = call_blocks(
+    raw_grad, head_gain_parts, attn_grad, mlp_total = call_blocks(
         attend_backward,
         seqs,
         [once(spec) for spec in attention_specs]
@@ -1418,13 +1433,12 @@
             once(whole(width, pack_cols)),
             ANY,
             ANY,
-            ANY,
         ],
         (
             jax.ShapeDtypeStruct((pair_rows, attn_cols), BF16),
             jax.ShapeDtypeStruct((seqs, 8, head), F32),
             jax.ShapeDtypeStruct((n_dp, pack_cols, model_rows), BF16),
-            jax.ShapeDtypeStruct((share, width), BF16),
+            jax.ShapeDtypeStruct((share, width), F32),
         ),
         (
             once(by_rows(seq_length, attn_cols)),
@@ -1444,8 +1458,7 @@
             pltpu.VMEM((seq_length, width), BF16),
             pltpu.VMEM(grouped(hidden_cols), BF16),
             pltpu.VMEM((width, hidden_cols), BF16),
-            pltpu.VMEM((share, width), F32),
-            pltpu.SemaphoreType.DMA((4,)),
+            pltpu.SemaphoreType.DMA((3,)),
         ]
         + Reduce.scratch(share, width, half_width, FEW),
         5 * pair_flops + 2 * pair_rows * width * (pack_cols + query_cols + hidden_cols),
@@ -1460,7 +1473,6 @@
         attn_full,
         active.reshape(grouped(hidden_cols)),
         down_full,
-        hidden,
     )
     head_gain_parts = head_gain_parts.sum(0)
     attn_grad = attn_grad.reshape(n_dp * pack_cols, model_rows)
@@ -1509,9 +1521,10 @@
         down_grad,
     )
     attn_given = lax.dynamic_index_in_dim(attn_grad, 1 - y, 0, False)
-    attn_given, gate_up_other, down_other = lax.optimization_barrier(
-        (attn_given, gate_up_other, down_other)
-    )
+    attn_given, gate_up_other, down_other, mlp_total = lax.optimization_barrier(
+        (attn_given, gate_up_other, down_other, mlp_total)
+    )
+    layer_output = (hidden + mlp_total).astype(BF16)
 
     def columns(own, other, start, axis=1):
         own = half(own, y, 0)[:, start : start + hidden_cols]
@@ -1527,16 +1540,18 @@
     attn_other = y_swap(attn_given)
     attn_own = lax.dynamic_index_in_dim(attn_grad, y, 0, False)
 
-    def attn_columns(start, size, turn=True):
-        own, other = attn_own[start : start + size], attn_other[start : start + size]
-        if turn:
-            own, other = own.T, other.T
-        return in_order(y, own, other, int(turn)).astype(F32)
-
-    query_grad = attn_columns(0, query_cols)
-    key_grad = attn_columns(query_cols, key_cols)
-    value_grad = attn_columns(query_cols + key_cols, key_cols)
-    output_grad = attn_columns(attn_cols, query_cols, False)
+    query_grad, key_grad, value_grad, output_grad = pl.pallas_call(
+        finish_attention,
+        out_shape=tuple(
+            jax.ShapeDtypeStruct(w.shape, F32)
+            for w in (query_weight, key_projection, value_projection, output_weight)
+        ),
+        in_specs=[VM] * 2,
+        out_specs=(VM,) * 4,
+        name="finish_attention",
+        cost_estimate=pl.CostEstimate(flops=0, bytes_accessed=4 * MIB, transcendentals=0),
+        compiler_params=pltpu.CompilerParams(vmem_limit_bytes=32 * MIB),
+    )(attn_own, attn_other)
     attn_gain_grad, mlp_gain_grad, query_gain_grad, key_gain_grad = gain_parts_of(gain_sums)
     return (
         layer_output,

time: 528 us -> 525 us (level)
  local copies, waits for them, and re-layouts: 26.6 us -> 19.2 us
    unnamed x36 -> x38, local copies, waits for them, and re-layouts: 12.7 us -> 7.18 us
  transfers between devices with their start and end apart: 9 -> 9, of which waited for: 5 -> 5; matrix products, arithmetic and copies ran while one was open for 12% -> 13% of each run, Pallas kernels for 63% -> 64%
where the time goes in v6:
time: 525 us; the launch traced here: 515 us
  Pallas kernels  392 us (75%)
  matrix products  40 us (8%)
  waiting for transfers between devices  30.1 us (6%)
  local copies, waits for them, and re-layouts  19.2 us (4%)
  between operations  14.5 us (3%)
  other arithmetic  13.7 us (3%)
    pallas_call x1, Pallas kernels, on_device(): call_leg(hidden_leg, 1, 'hidden_leg', [ANY] * 2 + [VM] * 3, (jax.ShapeDty...  84.2 us
    pallas_call x1, Pallas kernels, on_device(): call_leg(attention_leg, 0, 'attention_leg', [VM] * 4 + [ANY] * 3, (jax.Sh...  80.5 us
    pallas_call x1, Pallas kernels, on_device(): call_leg(output_leg, 2, 'output_leg', [VM] * 7 + [ANY] * 2, (jax.ShapeDty...  63.2 us
    pallas_call x1, Pallas kernels, on_device(): call_leg(front, 3, 'front', [VM] * 9 + [ANY] * 3, (jax.ShapeDtypeStruct((...  63 us
    pallas_call x1, Pallas kernels, on_device(): call_blocks(attend_backward, seqs, [once(spec) for spec in attention_spec...  55.1 us
    dot_general x3, matrix products, dot(): lax.dot_general(left, right, (((left_dim,), (right_dim,)), ((), ())), pre...  40 us
    pallas_call x1, Pallas kernels, on_device(): call_blocks(mlp_forward, blocks, [by_rows(TOKEN_BLOCK, width), whole(widt...  19.5 us
    pallas_call x1, Pallas kernels, on_device(): call_blocks(mlp_backward, blocks, [by_rows(TOKEN_BLOCK, width), whole(wid...  14.6 us
  transfers between devices with their start and end apart: 9, of which 5 were waited for; matrix products, arithmetic and copies ran while one was open for 13% of the time, Pallas kernels for 64%

profile of v6, /device:TPU:0, one launch (start us, length us, event | category | flops | bytes accessed | tf_op | source)
XLA Modules:
  0.0 514.9 jit_solution(10725857764711248034)
XLA Ops:
  7.2 0.0 all-gather.3.cloned.1.call-start
  7.2 63.0 %front.1 = (bf16[2048,768]{1,0:T(8,128)(2,1)}, f32[8,8,128]{2,1,0:T(8,128)}, s32[1,1024]{1,0:T(1,128)}, bf16[2048,2048]{1,0:T(8,128)(2,1)}, bf16[512,1536]{1,0:T(8,128)(2,1)}) custom-call(f32[256,512]{1,0:T(8,128)} %q.1, f32[256,256]{1,0:T(8,128)} %k.1, f32[256,256]{1,0:T(8,128)} %v.1, f32[512,256]{1,0:T(8,128)} %o.1, f32[1,256]{1,0:T(1,128)} %bitcast.74, ...), custom_call_target="tpu_custom_call" | custom-call | bytes 262144000 | tf_op jit(solution)/shard_map/front/pallas_call | solution.py:1238
  70.3 0.0 all-gather.3.cloned.1.call-update
  70.3 0.0 all-gather.5.cloned.1.call-start
  70.4 0.0 copy-start.10
  70.4 2.7 constant_dynamic-slice_fusion.1
  73.1 0.9 collective-permute-start
  74.0 0.2 fusion.8
  74.2 0.1 convert_bitcast_fusion
  74.3 3.7 multiply_cosine_fusion
  78.0 1.3 pad_maximum_fusion.sine
  79.3 1.1 copy-done
  80.5 9.5 %fusion.raw = f32[2048,512]{1,0:T(8,128)} fusion(bf16[2048,2048]{1,0:T(8,128)(2,1)} %get-tuple-element.57.normed, bf16[2048,768]{1,0:T(8,128)(2,1)S(1)} %copy-done), kind=kOutput, calls=%fused_computation.3 | convolution fusion | flops 4294967296 | bytes 14680064 | tf_op jit(solution)/shard_map/dot_general | solution.py:46
  90.0 7.5 %collective-permute-done.cot_part = bf16[256,2048]{1,0:T(8,128)(2,1)S(1)} collective-permute-done((bf16[256,2048]{1,0:T(8,128)(2,1)S(1)}, bf16[256,2048]{1,0:T(8,128)(2,1)S(1)}, u32[]{:S(2)}, u32[]{:S(2)}) %collective-permute-start) | collective-permute-done | bytes 1048608 | tf_op jit(solution)/shard_map/ppermute | solution.py:1187
  97.5 0.5 collective-permute-start.1
  98.0 1.7 copy.30
  99.7 0.8 dynamic-slice_bitcast_fusion.3
  100.5 1.5 collective-permute-start.2
  102.0 1.3 copy.35
  103.4 0.6 reshape.241.gain_query
  103.9 0.6 reshape.243.gain_key
  104.5 1.3 pad_maximum_fusion.1.cosine
  105.8 10.8 %attend_forward.1.attended = bf16[2048,256]{1,0:T(8,128)(2,1)} custom-call(f32[2048,512]{1,0:T(8,128)} %fusion.raw, f32[2048,128]{1,0:T(8,128)} %pad_maximum_fusion.1.cosine, f32[2048,128]{1,0:T(8,128)} %pad_maximum_fusion.sine, s32[2048,1]{1,0:T(8,128)} %bitcast.58, f32[1,128]{1,0:T(1,128)} %reshape.241.gain_query, f32[1,128]{1,0:T(1,128)} %reshape.243.gain_key), custom_call_target="tpu_custom_call" | custom-call | flops 1073741824 | bytes 20971520 | tf_op jit(solution)/shard_map/attend_forward/pallas_call | solution.py:1314
  116.7 4.5 collective-permute-done.1.cot_across
  121.2 1.2 maximum_select_fusion
  122.4 0.0 all-gather.5.cloned.1.call-update
  122.4 0.5 reduce-scatter.6.cloned.1.call-start
  122.9 0.6 fusion.14
  123.5 80.5 %attention_leg.1 = (f32[256,2048]{1,0:T(8,128)}, bf16[2,2,2,256,2048]{4,3,2,1,0:T(8,128)(2,1)}, bf16[2048,2048]{1,0:T(8,128)(2,1)}) custom-call(bf16[2,2,2,256,256]{4,3,2,1,0:T(8,128)(2,1)} %bitcast.57, bf16[2048,768]{1,0:T(8,128)(2,1)} %get-tuple-element.58.packed, bf16[256,2048]{1,0:T(8,128)(2,1)} %get-tuple-element.153.tokens, f32[1,2048]{1,0:T(1,128)} %bitcast.63, ...), custom_call_target="tpu_custom_call" | custom-call | bytes 209715200 | tf_op jit(solution)/shard_map/attention_leg/pallas_call | solution.py:1332
  204.0 0.0 all-gather.3.cloned.1.call-done.weights.right
  204.0 19.5 %mlp_forward.1 = (bf16[2048,768]{1,0:T(8,128)(2,1)}, f32[2048,768]{1,0:T(8,128)}, f32[2048,768]{1,0:T(8,128)}) custom-call(bf16[2048,2048]{1,0:T(8,128)(2,1)} %bitcast.78, bf16[2048,1536]{1,0:T(8,128)(2,1)} %all-gather.3.cloned.1.call-done.weights.right), custom_call_target="tpu_custom_call" | custom-call | flops 12884901888 | bytes 31457280 | tf_op jit(solution)/shard_map/mlp_forward/pallas_call | solution.py:1367
  223.5 11.4 %convolution_convert_fusion.1 = bf16[2048,768]{1,0:T(8,128)(2,1)} fusion(bf16[2048,2048]{1,0:T(8,128)(2,1)} %get-tuple-element.73.cotangent, bf16[2048,768]{1,0:T(8,128)(2,1)} %get-tuple-element.72), kind=kOutput, calls=%fused_computation.1 | convolution fusion | flops 6444023808 | bytes 14680064 | tf_op jit(solution)/shard_map/dot_general | solution.py:46
  234.9 0.0 reduce-scatter.6.cloned.1.call-update
  234.9 0.2 reduce-scatter.4.cloned.1.call-start
  235.2 12.3 %all-gather.5.cloned.1.call-done.weights.mlp_right = bf16[2048,768]{1,0:T(8,128)(2,1)} async-done(((bf16[512,768]{1,0:T(8,128)(2,1)}), bf16[2048,768]{1,0:T(8,128)(2,1)}) %all-gather.5.cloned.1.call-update) | async-done | bytes 3145744 | tf_op jit(solution)/shard_map/all_gather | solution.py:1204
  247.5 14.6 %mlp_backward.1 = bf16[2048,1536]{1,0:T(8,128)(2,1)} custom-call(bf16[2048,2048]{1,0:T(8,128)(2,1)} %get-tuple-element.73.cotangent, bf16[2048,768]{1,0:T(8,128)(2,1)} %all-gather.5.cloned.1.call-done.weights.mlp_right, f32[2048,768]{1,0:T(8,128)} %get-tuple-element.75.gate_slope, f32[2048,768]{1,0:T(8,128)} %get-tuple-element.76.up_slope), custom_call_target="tpu_custom_call" | custom-call | flops 6442450944 | bytes 31457280 | tf_op jit(solution)/shard_map/mlp_backward/pallas_call | solution.py:1384
  262.0 19.1 %convolution_convert_fusion = bf16[2048,1536]{1,0:T(8,128)(2,1)} fusion(bf16[2048,2048]{1,0:T(8,128)(2,1)} %bitcast.79, bf16[2048,1536]{1,0:T(8,128)(2,1)} %mlp_backward.1), kind=kOutput, calls=%fused_computation | convolution fusion | flops 12888047616 | bytes 20971520 | tf_op jit(solution)/shard_map/dot_general | solution.py:46
  281.1 0.0 reduce-scatter.4.cloned.1.call-update
  281.2 0.0 reduce-scatter.8.cloned.1.call-start
  281.2 84.2 %hidden_leg.1 = (f32[256,2048]{1,0:T(8,128)}, f32[1,2048]{1,0:T(1,128)}, bf16[2,2,2,256,2048]{4,3,2,1,0:T(8,128)(2,1)}) custom-call(bf16[2,2,2,256,1536]{4,3,2,1,0:T(8,128)(2,1)} %bitcast.55, bf16[2048,1536]{1,0:T(8,128)(2,1)} %all-gather.3.cloned.1.call-done.weights.right, f32[256,2048]{1,0:T(8,128)} %get-tuple-element.68.hidden, ...), custom_call_target="tpu_custom_call" | custom-call | bytes 209715200 | tf_op jit(solution)/shard_map/hidden_leg/pallas_call | solution.py:1397
  365.4 55.1 %attend_backward.1 = (bf16[2048,512]{1,0:T(8,128)(2,1)}, f32[2,8,128]{2,1,0:T(8,128)}, bf16[8,768,256]{2,1,0:T(8,128)(2,1)}, f32[256,2048]{1,0:T(8,128)}) custom-call(f32[2048,512]{1,0:T(8,128)} %fusion.raw, f32[2048,128]{1,0:T(8,128)} %pad_maximum_fusion.1.cosine, f32[2048,128]{1,0:T(8,128)} %pad_maximum_fusion.sine, s32[2048,1]{1,0:T(8,128)} %bitcast.59, ...), custom_call_target="tpu_custom_call" | custom-call | flops 17716740096 | bytes 83886080 | tf_op jit(solution)/shard_map/attend_backward/pallas_call | solution.py:1425
  420.6 0.0 reduce-scatter.6.cloned.1.call-done.down_grad
  420.6 1.1 reduce-scatter.4.cloned.1.call-done.gate_up_grad
  421.7 0.0 reduce-scatter.8.cloned.1.call-update
  421.8 0.1 reshape_squeeze.7
  421.9 0.1 reshape_squeeze.6
  422.0 0.1 pad_maximum_fusion.2
  422.0 0.6 pad.13.gain_parts
  422.7 63.2 %output_leg.1 = (f32[256,2048]{1,0:T(8,128)}, f32[8,128]{1,0:T(8,128)}, bf16[256,1536]{1,0:T(8,128)(2,1)}, bf16[256,768]{1,0:T(8,128)(2,1)}) custom-call(bf16[2,2,2,256,512]{4,3,2,1,0:T(8,128)(2,1)} %bitcast.60, bf16[2048,768]{1,0:T(8,128)(2,1)} %get-tuple-element.58.packed, bf16[256,2048]{1,0:T(8,128)(2,1)} %get-tuple-element.153.tokens, ...), custom_call_target="tpu_custom_call" | custom-call | bytes 209715200 | tf_op jit(solution)/shard_map/output_leg/pallas_call | solution.py:1492
  486.0 2.1 fusion.12
  488.0 0.5 slice_bitcast_fusion.2
  488.5 0.6 slice_bitcast_fusion
  489.1 1.9 dynamic-slice_bitcast_fusion.1
  491.0 2.9 add_convert_fusion
  493.9 1.4 collective-permute-start.3
  495.4 0.8 fusion.13
  496.2 1.4 fusion.2
  497.6 0.2 fusion.4
  497.8 0.0 copy-start.6
  497.8 1.6 copy.32
  499.4 1.4 fusion.3
  500.8 4.5 collective-permute-done.3.other
  505.3 1.3 finish_attention.1
  506.6 1.3 copy.39
  (42 shorter events, 0.2 us)
Async XLA Ops:
  7.2 196.8 %all-gather.3.cloned.1.call-start = ((), (), s32[]{:S(2)}) async-start(), calls=%async_computation.3 | async-start | bytes 7864320 | tf_op jit(solution)/shard_map/all_gather | solution.py:1204
  70.3 177.2 %all-gather.5.cloned.1.call-start = ((), (), s32[]{:S(2)}) async-start(), calls=%async_computation.4 | async-start | bytes 3932160 | tf_op jit(solution)/shard_map/all_gather | solution.py:1204
  70.4 3.6 copy-start.10
  70.4 3.6 copy-start.12
  73.1 6.3 %copy-start.2 = (bf16[256,2048]{1,0:T(8,128)(2,1)}, bf16[256,2048]{1,0:T(8,128)(2,1)S(1)}, u32[]{:S(2)}) copy-start(bf16[256,2048]{1,0:T(8,128)(2,1)S(1)} %get-tuple-element.60.cotangent) | copy-start | bytes 3145732
  73.1 24.4 %collective-permute-start = (bf16[256,2048]{1,0:T(8,128)(2,1)S(1)}, bf16[256,2048]{1,0:T(8,128)(2,1)S(1)}, u32[]{:S(2)}, u32[]{:S(2)}) collective-permute-start(bf16[256,2048]{1,0:T(8,128)(2,1)S(1)} %get-tuple-element.60.cotangent), channel_id=1, source_target_pairs={{0,4},{4,0},{8,12},{12,8},{16,20},{20,16},{24,28},{28,24},{1,5},{5... | collective-permute-start | bytes 3145736 | tf_op jit(solution)/shard_map/ppermute | solution.py:1187
  78.0 2.5 copy-start
  97.5 5.9 %copy-start.7 = (bf16[256,2048]{1,0:T(8,128)(2,1)}, bf16[256,2048]{1,0:T(8,128)(2,1)S(1)}, u32[]{:S(2)}) copy-start(bf16[256,2048]{1,0:T(8,128)(2,1)S(1)} %collective-permute-done.cot_part) | copy-start | bytes 3145732
  97.5 4.5 copy-start.11
  97.5 23.7 %collective-permute-start.1 = (bf16[256,2048]{1,0:T(8,128)(2,1)S(1)}, bf16[256,2048]{1,0:T(8,128)(2,1)}, u32[]{:S(2)}, u32[]{:S(2)}) collective-permute-start(bf16[256,2048]{1,0:T(8,128)(2,1)S(1)} %collective-permute-done.cot_part), channel_id=1, source_target_pairs={{0,2},{1,3},{2,0},{3,1},{4,6},{5,7},{6,4},{7,5},{8,10},{9,11},{10,... | collective-permute-start | bytes 3145736 | tf_op jit(solution)/shard_map/ppermute | solution.py:1190
  100.5 16.1 %collective-permute-start.2 = (bf16[256,768]{1,0:T(8,128)(2,1)}, bf16[256,768]{1,0:T(8,128)(2,1)S(1)}, u32[]{:S(2)}, u32[]{:S(2)}) collective-permute-start(bf16[256,768]{1,0:T(8,128)(2,1)} %get-tuple-element.65), channel_id=1, source_target_pairs={{0,4},{4,0},{8,12},{12,8},{16,20},{20,16},{24,28},{28,24},{1,5},{5... | collective-permute-start | bytes 1179656 | tf_op jit(solution)/shard_map/ppermute | solution.py:1187
  122.4 298.2 %reduce-scatter.6.cloned.1.call-start = ((), (), s32[]{:S(2)}) async-start(), calls=%async_computation.6 | async-start | bytes 3932160 | tf_op jit(solution)/shard_map/reduce_scatter | solution.py:1207
  234.9 186.7 %reduce-scatter.4.cloned.1.call-start = ((), (), s32[]{:S(2)}) async-start(), calls=%async_computation.5 | async-start | bytes 7864320 | tf_op jit(solution)/shard_map/reduce_scatter | solution.py:1207
  281.2 208.0 %reduce-scatter.8.cloned.1.call-start = ((), (), s32[]{:S(2)}) async-start(), calls=%async_computation.7 | async-start | bytes 3932160 | tf_op jit(solution)/shard_map/reduce_scatter | solution.py:1207
  420.5 1.2 copy-start.14
  420.6 1.4 copy-start.13
  422.7 63.3 %copy-start.4 = (bf16[512,768]{1,0:T(8,128)(2,1)S(1)}, bf16[512,768]{1,0:T(8,128)(2,1)}, u32[]{:S(2)}) copy-start(bf16[512,768]{1,0:T(8,128)(2,1)} %reduce-scatter.6.cloned.1.call-done.down_grad) | copy-start | bytes 2359300
  485.9 2.1 copy-start.15
  485.9 5.1 copy-start.1
  491.0 4.3 copy-start.8
  491.0 5.1 copy-start.5
  493.9 3.6 copy-start.9
  493.9 11.4 %collective-permute-start.3 = (bf16[768,256]{1,0:T(8,128)(2,1)}, bf16[768,256]{1,0:T(8,128)(2,1)S(1)}, u32[]{:S(2)}, u32[]{:S(2)}) collective-permute-start(bf16[768,256]{1,0:T(8,128)(2,1)} %get-tuple-element.94), channel_id=1, source_target_pairs={{0,4},{4,0},{8,12},{12,8},{16,20},{20,16},{24,28},{28,24},{1,5},{5... | collective-permute-start | bytes 1179656 | tf_op jit(solution)/shard_map/ppermute | solution.py:1187
  497.8 1.6 copy-start.6
  499.4 7.2 %copy-start.3 = (f32[256,2048]{1,0:T(8,128)S(1)}, f32[256,2048]{1,0:T(8,128)}, u32[]{:S(2)}) copy-start(f32[256,2048]{1,0:T(8,128)} %get-tuple-element.169) | copy-start | bytes 6291460
Sparse Core Ops, SparseCore 0:
  70.4 113.6 all-gather.2
  185.7 61.6 all-gather.4
  249.8 58.8 reduce-scatter.5
  310.9 110.7 reduce-scatter.3
  423.8 61.2 reduce-scatter.7

commit v7 on v6

--- a/solution.py
+++ b/solution.py
@@ -1521,8 +1521,8 @@
         down_grad,
     )
     attn_given = lax.dynamic_index_in_dim(attn_grad, 1 - y, 0, False)
-    attn_given, gate_up_other, down_other, mlp_total = lax.optimization_barrier(
-        (attn_given, gate_up_other, down_other, mlp_total)
+    attn_given, gate_up_other, down_other = lax.optimization_barrier(
+        (attn_given, gate_up_other, down_other)
     )
     layer_output = (hidden + mlp_total).astype(BF16)
 

time: 525 us -> 523 us (level)
  no operation moved by 1% of the time
where the time goes in v7:
time: 523 us; the launch traced here: 513 us
  Pallas kernels  392 us (75%)
  matrix products  40.1 us (8%)
  waiting for transfers between devices  30.6 us (6%)
  local copies, waits for them, and re-layouts  17.1 us (3%)
  between operations  14.6 us (3%)
  other arithmetic  13.6 us (3%)
    pallas_call x1, Pallas kernels, on_device(): call_leg(hidden_leg, 1, 'hidden_leg', [ANY] * 2 + [VM] * 3, (jax.ShapeDty...  84.2 us
    pallas_call x1, Pallas kernels, on_device(): call_leg(attention_leg, 0, 'attention_leg', [VM] * 4 + [ANY] * 3, (jax.Sh...  80.5 us
    pallas_call x1, Pallas kernels, on_device(): call_leg(output_leg, 2, 'output_leg', [VM] * 7 + [ANY] * 2, (jax.ShapeDty...  63.3 us
    pallas_call x1, Pallas kernels, on_device(): call_leg(front, 3, 'front', [VM] * 9 + [ANY] * 3, (jax.ShapeDtypeStruct((...  63 us
    pallas_call x1, Pallas kernels, on_device(): call_blocks(attend_backward, seqs, [once(spec) for spec in attention_spec...  55.2 us
    dot_general x3, matrix products, dot(): lax.dot_general(left, right, (((left_dim,), (right_dim,)), ((), ())), pre...  40.1 us
    pallas_call x1, Pallas kernels, on_device(): call_blocks(mlp_forward, blocks, [by_rows(TOKEN_BLOCK, width), whole(widt...  19.4 us
    pallas_call x1, Pallas kernels, on_device(): call_blocks(mlp_backward, blocks, [by_rows(TOKEN_BLOCK, width), whole(wid...  14.6 us
  transfers between devices with their start and end apart: 9, of which 5 were waited for; matrix products, arithmetic and copies ran while one was open for 13% of the time, Pallas kernels for 64%

profile of v7, /device:TPU:0, one launch (start us, length us, event | category | flops | bytes accessed | tf_op | source)
XLA Modules:
  0.0 513.4 jit_solution(15425415256397681826)
XLA Ops:
  7.2 0.0 all-gather.3.cloned.1.call-start
  7.2 63.0 %front.1 = (bf16[2048,768]{1,0:T(8,128)(2,1)}, f32[8,8,128]{2,1,0:T(8,128)}, s32[1,1024]{1,0:T(1,128)}, bf16[2048,2048]{1,0:T(8,128)(2,1)}, bf16[512,1536]{1,0:T(8,128)(2,1)}) custom-call(f32[256,512]{1,0:T(8,128)} %q.1, f32[256,256]{1,0:T(8,128)} %k.1, f32[256,256]{1,0:T(8,128)} %v.1, f32[512,256]{1,0:T(8,128)} %o.1, f32[1,256]{1,0:T(1,128)} %bitcast.74, ...), custom_call_target="tpu_custom_call" | custom-call | bytes 262144000 | tf_op jit(solution)/shard_map/front/pallas_call | solution.py:1238
  70.3 0.0 all-gather.3.cloned.1.call-update
  70.3 0.0 all-gather.5.cloned.1.call-start
  70.3 0.0 copy-start.9
  70.4 2.7 constant_dynamic-slice_fusion.1
  73.1 0.9 collective-permute-start
  74.0 0.2 fusion.8
  74.2 0.1 convert_bitcast_fusion
  74.3 3.7 multiply_cosine_fusion
  78.0 1.3 pad_maximum_fusion.sine
  79.3 1.1 copy-done
  80.5 9.5 %fusion.raw = f32[2048,512]{1,0:T(8,128)} fusion(bf16[2048,2048]{1,0:T(8,128)(2,1)} %get-tuple-element.56.normed, bf16[2048,768]{1,0:T(8,128)(2,1)S(1)} %copy-done), kind=kOutput, calls=%fused_computation.3 | convolution fusion | flops 4294967296 | bytes 14680064 | tf_op jit(solution)/shard_map/dot_general | solution.py:46
  90.0 7.5 %collective-permute-done.cot_part = bf16[256,2048]{1,0:T(8,128)(2,1)S(1)} collective-permute-done((bf16[256,2048]{1,0:T(8,128)(2,1)S(1)}, bf16[256,2048]{1,0:T(8,128)(2,1)S(1)}, u32[]{:S(2)}, u32[]{:S(2)}) %collective-permute-start) | collective-permute-done | bytes 1048608 | tf_op jit(solution)/shard_map/ppermute | solution.py:1187
  97.5 0.5 collective-permute-start.1
  98.0 1.7 copy.30
  99.7 0.8 dynamic-slice_bitcast_fusion.3
  100.5 1.5 collective-permute-start.2
  102.0 1.3 copy.35
  103.3 0.6 reshape.241.gain_query
  103.9 0.6 reshape.243.gain_key
  104.5 1.3 pad_maximum_fusion.1.cosine
  105.8 10.8 %attend_forward.1.attended = bf16[2048,256]{1,0:T(8,128)(2,1)} custom-call(f32[2048,512]{1,0:T(8,128)} %fusion.raw, f32[2048,128]{1,0:T(8,128)} %pad_maximum_fusion.1.cosine, f32[2048,128]{1,0:T(8,128)} %pad_maximum_fusion.sine, s32[2048,1]{1,0:T(8,128)} %bitcast.58, f32[1,128]{1,0:T(1,128)} %reshape.241.gain_query, f32[1,128]{1,0:T(1,128)} %reshape.243.gain_key), custom_call_target="tpu_custom_call" | custom-call | flops 1073741824 | bytes 20971520 | tf_op jit(solution)/shard_map/attend_forward/pallas_call | solution.py:1314
  116.6 4.5 collective-permute-done.1.cot_across
  121.1 1.2 maximum_select_fusion
  122.3 0.0 all-gather.5.cloned.1.call-update
  122.3 0.5 reduce-scatter.6.cloned.1.call-start
  122.9 0.6 fusion.14
  123.5 80.5 %attention_leg.1 = (f32[256,2048]{1,0:T(8,128)}, bf16[2,2,2,256,2048]{4,3,2,1,0:T(8,128)(2,1)}, bf16[2048,2048]{1,0:T(8,128)(2,1)}) custom-call(bf16[2,2,2,256,256]{4,3,2,1,0:T(8,128)(2,1)} %bitcast.57, bf16[2048,768]{1,0:T(8,128)(2,1)} %get-tuple-element.57.packed, bf16[256,2048]{1,0:T(8,128)(2,1)} %get-tuple-element.151.tokens, f32[1,2048]{1,0:T(1,128)} %bitcast.63, ...), custom_call_target="tpu_custom_call" | custom-call | bytes 209715200 | tf_op jit(solution)/shard_map/attention_leg/pallas_call | solution.py:1332
  204.0 0.0 all-gather.3.cloned.1.call-done.weights.right
  204.0 19.4 %mlp_forward.1 = (bf16[2048,768]{1,0:T(8,128)(2,1)}, f32[2048,768]{1,0:T(8,128)}, f32[2048,768]{1,0:T(8,128)}) custom-call(bf16[2048,2048]{1,0:T(8,128)(2,1)} %bitcast.78, bf16[2048,1536]{1,0:T(8,128)(2,1)} %all-gather.3.cloned.1.call-done.weights.right), custom_call_target="tpu_custom_call" | custom-call | flops 12884901888 | bytes 31457280 | tf_op jit(solution)/shard_map/mlp_forward/pallas_call | solution.py:1367
  223.4 11.4 %convolution_convert_fusion.1 = bf16[2048,768]{1,0:T(8,128)(2,1)} fusion(bf16[2048,2048]{1,0:T(8,128)(2,1)} %get-tuple-element.72.cotangent, bf16[2048,768]{1,0:T(8,128)(2,1)} %get-tuple-element.71), kind=kOutput, calls=%fused_computation.1 | convolution fusion | flops 6444023808 | bytes 14680064 | tf_op jit(solution)/shard_map/dot_general | solution.py:46
  234.8 0.0 reduce-scatter.6.cloned.1.call-update
  234.9 0.2 reduce-scatter.4.cloned.1.call-start
  235.1 12.4 %all-gather.5.cloned.1.call-done.weights.mlp_right = bf16[2048,768]{1,0:T(8,128)(2,1)} async-done(((bf16[512,768]{1,0:T(8,128)(2,1)}), bf16[2048,768]{1,0:T(8,128)(2,1)}) %all-gather.5.cloned.1.call-update) | async-done | bytes 3145744 | tf_op jit(solution)/shard_map/all_gather | solution.py:1204
  247.4 14.6 %mlp_backward.1 = bf16[2048,1536]{1,0:T(8,128)(2,1)} custom-call(bf16[2048,2048]{1,0:T(8,128)(2,1)} %get-tuple-element.72.cotangent, bf16[2048,768]{1,0:T(8,128)(2,1)} %all-gather.5.cloned.1.call-done.weights.mlp_right, f32[2048,768]{1,0:T(8,128)} %get-tuple-element.74.gate_slope, f32[2048,768]{1,0:T(8,128)} %get-tuple-element.75.up_slope), custom_call_target="tpu_custom_call" | custom-call | flops 6442450944 | bytes 31457280 | tf_op jit(solution)/shard_map/mlp_backward/pallas_call | solution.py:1384
  262.0 19.2 %convolution_convert_fusion = bf16[2048,1536]{1,0:T(8,128)(2,1)} fusion(bf16[2048,2048]{1,0:T(8,128)(2,1)} %bitcast.79, bf16[2048,1536]{1,0:T(8,128)(2,1)} %mlp_backward.1), kind=kOutput, calls=%fused_computation | convolution fusion | flops 12888047616 | bytes 20971520 | tf_op jit(solution)/shard_map/dot_general | solution.py:46
  281.2 0.0 reduce-scatter.4.cloned.1.call-update
  281.2 0.0 reduce-scatter.8.cloned.1.call-start
  281.3 84.2 %hidden_leg.1 = (f32[256,2048]{1,0:T(8,128)}, f32[1,2048]{1,0:T(1,128)}, bf16[2,2,2,256,2048]{4,3,2,1,0:T(8,128)(2,1)}) custom-call(bf16[2,2,2,256,1536]{4,3,2,1,0:T(8,128)(2,1)} %bitcast.55, bf16[2048,1536]{1,0:T(8,128)(2,1)} %all-gather.3.cloned.1.call-done.weights.right, f32[256,2048]{1,0:T(8,128)} %get-tuple-element.67.hidden, ...), custom_call_target="tpu_custom_call" | custom-call | bytes 209715200 | tf_op jit(solution)/shard_map/hidden_leg/pallas_call | solution.py:1397
  365.4 55.2 %attend_backward.1 = (bf16[2048,512]{1,0:T(8,128)(2,1)}, f32[2,8,128]{2,1,0:T(8,128)}, bf16[8,768,256]{2,1,0:T(8,128)(2,1)}, f32[256,2048]{1,0:T(8,128)}) custom-call(f32[2048,512]{1,0:T(8,128)} %fusion.raw, f32[2048,128]{1,0:T(8,128)} %pad_maximum_fusion.1.cosine, f32[2048,128]{1,0:T(8,128)} %pad_maximum_fusion.sine, s32[2048,1]{1,0:T(8,128)} %bitcast.59, ...), custom_call_target="tpu_custom_call" | custom-call | flops 17716740096 | bytes 83886080 | tf_op jit(solution)/shard_map/attend_backward/pallas_call | solution.py:1425
  420.7 0.0 reduce-scatter.6.cloned.1.call-done.down_grad
  420.7 1.0 reduce-scatter.4.cloned.1.call-done.gate_up_grad
  421.7 0.0 reduce-scatter.8.cloned.1.call-update
  421.8 0.1 reshape_squeeze.7
  421.9 0.1 reshape_squeeze.6
  422.0 0.1 pad_maximum_fusion.2
  422.0 0.6 pad.13.gain_parts
  422.7 2.8 add_convert_fusion
  425.5 63.3 %output_leg.1 = (f32[256,2048]{1,0:T(8,128)}, f32[8,128]{1,0:T(8,128)}, bf16[256,1536]{1,0:T(8,128)(2,1)}, bf16[256,768]{1,0:T(8,128)(2,1)}) custom-call(bf16[2,2,2,256,512]{4,3,2,1,0:T(8,128)(2,1)} %bitcast.60, bf16[2048,768]{1,0:T(8,128)(2,1)} %get-tuple-element.57.packed, bf16[256,2048]{1,0:T(8,128)(2,1)} %get-tuple-element.151.tokens, ...), custom_call_target="tpu_custom_call" | custom-call | bytes 209715200 | tf_op jit(solution)/shard_map/output_leg/pallas_call | solution.py:1492
  488.8 0.1 fusion.12
  488.9 0.5 copy-done.14
  489.4 0.5 slice_bitcast_fusion.2
  490.0 0.6 slice_bitcast_fusion
  490.5 2.0 dynamic-slice_bitcast_fusion.1
  492.5 1.5 collective-permute-start.3
  494.0 0.1 fusion.13
  494.0 1.4 fusion.2
  495.4 0.2 fusion.4
  495.6 1.6 copy.32
  497.3 1.4 fusion.3
  498.6 5.2 %collective-permute-done.3.other = bf16[768,256]{1,0:T(8,128)(2,1)S(1)} collective-permute-done((bf16[768,256]{1,0:T(8,128)(2,1)}, bf16[768,256]{1,0:T(8,128)(2,1)S(1)}, u32[]{:S(2)}, u32[]{:S(2)}) %collective-permute-start.3) | collective-permute-done | bytes 393248 | tf_op jit(solution)/shard_map/ppermute | solution.py:1187
  503.8 1.3 finish_attention.1
  505.1 1.3 copy.39
  (40 shorter events, 0.2 us)
Async XLA Ops:
  7.2 196.8 %all-gather.3.cloned.1.call-start = ((), (), s32[]{:S(2)}) async-start(), calls=%async_computation.3 | async-start | bytes 7864320 | tf_op jit(solution)/shard_map/all_gather | solution.py:1204
  70.3 177.2 %all-gather.5.cloned.1.call-start = ((), (), s32[]{:S(2)}) async-start(), calls=%async_computation.4 | async-start | bytes 3932160 | tf_op jit(solution)/shard_map/all_gather | solution.py:1204
  70.3 3.6 copy-start.9
  70.4 3.6 copy-start.11
  73.1 6.3 %copy-start.2 = (bf16[256,2048]{1,0:T(8,128)(2,1)}, bf16[256,2048]{1,0:T(8,128)(2,1)S(1)}, u32[]{:S(2)}) copy-start(bf16[256,2048]{1,0:T(8,128)(2,1)S(1)} %get-tuple-element.59.cotangent) | copy-start | bytes 3145732
  73.1 24.4 %collective-permute-start = (bf16[256,2048]{1,0:T(8,128)(2,1)S(1)}, bf16[256,2048]{1,0:T(8,128)(2,1)S(1)}, u32[]{:S(2)}, u32[]{:S(2)}) collective-permute-start(bf16[256,2048]{1,0:T(8,128)(2,1)S(1)} %get-tuple-element.59.cotangent), channel_id=1, source_target_pairs={{0,4},{4,0},{8,12},{12,8},{16,20},{20,16},{24,28},{28,24},{1,5},{5... | collective-permute-start | bytes 3145736 | tf_op jit(solution)/shard_map/ppermute | solution.py:1187
  78.0 2.5 copy-start
  97.5 5.9 %copy-start.6 = (bf16[256,2048]{1,0:T(8,128)(2,1)}, bf16[256,2048]{1,0:T(8,128)(2,1)S(1)}, u32[]{:S(2)}) copy-start(bf16[256,2048]{1,0:T(8,128)(2,1)S(1)} %collective-permute-done.cot_part) | copy-start | bytes 3145732
  97.5 4.5 copy-start.10
  97.5 23.7 %collective-permute-start.1 = (bf16[256,2048]{1,0:T(8,128)(2,1)S(1)}, bf16[256,2048]{1,0:T(8,128)(2,1)}, u32[]{:S(2)}, u32[]{:S(2)}) collective-permute-start(bf16[256,2048]{1,0:T(8,128)(2,1)S(1)} %collective-permute-done.cot_part), channel_id=1, source_target_pairs={{0,2},{1,3},{2,0},{3,1},{4,6},{5,7},{6,4},{7,5},{8,10},{9,11},{10,... | collective-permute-start | bytes 3145736 | tf_op jit(solution)/shard_map/ppermute | solution.py:1190
  100.5 16.1 %collective-permute-start.2 = (bf16[256,768]{1,0:T(8,128)(2,1)}, bf16[256,768]{1,0:T(8,128)(2,1)S(1)}, u32[]{:S(2)}, u32[]{:S(2)}) collective-permute-start(bf16[256,768]{1,0:T(8,128)(2,1)} %get-tuple-element.64), channel_id=1, source_target_pairs={{0,4},{4,0},{8,12},{12,8},{16,20},{20,16},{24,28},{28,24},{1,5},{5... | collective-permute-start | bytes 1179656 | tf_op jit(solution)/shard_map/ppermute | solution.py:1187
  122.3 298.3 %reduce-scatter.6.cloned.1.call-start = ((), (), s32[]{:S(2)}) async-start(), calls=%async_computation.6 | async-start | bytes 3932160 | tf_op jit(solution)/shard_map/reduce_scatter | solution.py:1207
  234.9 186.8 %reduce-scatter.4.cloned.1.call-start = ((), (), s32[]{:S(2)}) async-start(), calls=%async_computation.5 | async-start | bytes 7864320 | tf_op jit(solution)/shard_map/reduce_scatter | solution.py:1207
  281.2 209.3 %reduce-scatter.8.cloned.1.call-start = ((), (), s32[]{:S(2)}) async-start(), calls=%async_computation.7 | async-start | bytes 3932160 | tf_op jit(solution)/shard_map/reduce_scatter | solution.py:1207
  420.6 1.1 copy-start.13
  420.6 1.3 copy-start.12
  420.7 2.0 copy-start.1
  425.5 63.3 %copy-start.5 = (bf16[512,768]{1,0:T(8,128)(2,1)S(1)}, bf16[512,768]{1,0:T(8,128)(2,1)}, u32[]{:S(2)}) copy-start(bf16[512,768]{1,0:T(8,128)(2,1)} %reduce-scatter.6.cloned.1.call-done.down_grad) | copy-start | bytes 2359300
  425.5 63.4 %copy-start.3 = (bf16[512,1536]{1,0:T(8,128)(2,1)S(1)}, bf16[512,1536]{1,0:T(8,128)(2,1)}, u32[]{:S(2)}) copy-start(bf16[512,1536]{1,0:T(8,128)(2,1)} %reduce-scatter.4.cloned.1.call-done.gate_up_grad) | copy-start | bytes 4718596
  488.8 0.7 copy-start.14
  490.5 3.5 copy-start.7
  492.5 2.9 copy-start.8
  492.5 11.3 %collective-permute-start.3 = (bf16[768,256]{1,0:T(8,128)(2,1)}, bf16[768,256]{1,0:T(8,128)(2,1)S(1)}, u32[]{:S(2)}, u32[]{:S(2)}) collective-permute-start(bf16[768,256]{1,0:T(8,128)(2,1)} %get-tuple-element.92), channel_id=1, source_target_pairs={{0,4},{4,0},{8,12},{12,8},{16,20},{20,16},{24,28},{28,24},{1,5},{5... | collective-permute-start | bytes 1179656 | tf_op jit(solution)/shard_map/ppermute | solution.py:1187
  497.3 7.8 %copy-start.4 = (f32[256,2048]{1,0:T(8,128)S(1)}, f32[256,2048]{1,0:T(8,128)}, u32[]{:S(2)}) copy-start(f32[256,2048]{1,0:T(8,128)} %get-tuple-element.167) | copy-start | bytes 6291460
Sparse Core Ops, SparseCore 0:
  70.4 113.6 all-gather.2
  185.7 61.6 all-gather.4
  249.8 58.8 reduce-scatter.5
  310.9 110.7 reduce-scatter.3
  423.8 61.3 reduce-scatter.7
